TPU v7x, 128 devices: a whole 4x4x4 slice. The times are simulated.
128 devices in a mesh: seq: 4 (over z_lo, core), res: 32 (over y, x, z_hi).
Axes of the slice: x: 4, y: 4, z: 4 (z_hi: 2, z_lo: 2; z = z_hi * 2 + z_lo), core: 2. Of those that a mesh axis runs over, the one named last changes fastest.
Arguments:
- homolog_embedding: bfloat16 [16, 2048, 256], P('seq', 'res'), may hold values from -6 to 6
- pair_input_rows: bfloat16 [2048, 2048, 128], P('res', 'seq'), may hold values from -256 to 256
- incoming_slope: bfloat16 [16, 2048, 256], P('seq', 'res'), may hold values from -6 to 6
- rescale_factor: float32 [256], replicated, may hold values from 0.25 to 1.75
- probe_weights: bfloat16 [256, 256], replicated, may hold values from -0.375 to 0.375
- lookup_weights: bfloat16 [256, 256], replicated, may hold values from -0.375 to 0.375
- content_weights: bfloat16 [256, 256], replicated, may hold values from -0.375 to 0.375
- sigmoid_weights: bfloat16 [256, 256], replicated, may hold values from -0.375 to 0.375
- final_projection: bfloat16 [256, 256], replicated, may hold values from -0.375 to 0.375
- pair_bias_matrix: bfloat16 [128, 8], replicated, may hold values from -1 to 1
Outputs:
- alignment_rows_gradient: bfloat16 [16, 2048, 256], P('seq', 'res')
- pair_input_gradient: bfloat16 [2048, 2048, 128], P('res', 'seq')
- layer_gain_gradient: float32 [256], replicated
- query_matrix_gradient: float32 [256, 256], replicated
- key_matrix_gradient: float32 [256, 256], replicated
- value_matrix_gradient: float32 [256, 256], replicated
- gate_matrix_gradient: float32 [256, 256], replicated
- final_projection_slope: float32 [256, 256], replicated
- pair_bias_matrix_gradient: float32 [128, 8], replicated
All inputs are finite; a program needn't handle non-finite values.
Results may differ from a plain program's by a relative error of at most 0.0034.
The roundings to bfloat16 on the way count: a program that leaves them out, or rounds other values in their place, can miss the bound.
Values may be sent and summed in bfloat16 or wider, within the bound.
A program may use at most 128 MiB of HBM per device.

v0:
```python
import functools
import math

import jax
import jax.numpy as jnp
from jax import lax
from jax.sharding import PartitionSpec as P


def layer_norm_rows(alignment_block):
    content_vectors = alignment_block.astype(jnp.float32)
    centered = content_vectors - jnp.mean(content_vectors, axis=-1, keepdims=True)
    inverse_deviation = lax.rsqrt(jnp.mean(centered * centered, axis=-1, keepdims=True) + 1e-05)
    return (centered * inverse_deviation, inverse_deviation)


def row_backward(bias_full, head_count, dbias_total, row_inputs):
    probe_vectors, keys_row, values_row, gate_row, derivative_modulated = row_inputs
    query_total, channel_width = probe_vectors.shape
    key_count = keys_row.shape[0]
    head_width = channel_width // head_count
    softmax_scale = 1.0 / math.sqrt(head_width)
    query_heads = probe_vectors.reshape(query_total, head_count, head_width)
    key_heads = keys_row.reshape(key_count, head_count, head_width)
    value_heads = values_row.reshape(key_count, head_count, head_width)
    scores = (
        jnp.einsum("ihd,jhd->hij", query_heads, key_heads, preferred_element_type=jnp.float32)
        * softmax_scale
    )
    scores = scores + bias_full.astype(jnp.float32)
    weights_soft = jax.nn.softmax(scores, axis=-1)
    weights_half = weights_soft.astype(jnp.bfloat16)
    attended = jnp.einsum(
        "hij,jhd->ihd", weights_half, value_heads, preferred_element_type=jnp.float32
    ).reshape(query_total, channel_width)
    modulated_result = (gate_row * attended).astype(jnp.bfloat16)
    grad_attended = (derivative_modulated * gate_row).astype(jnp.bfloat16)
    derivative_logits_sigmoid = (
        derivative_modulated * attended * gate_row * (1.0 - gate_row)
    ).astype(jnp.bfloat16)
    grad_heads = grad_attended.reshape(query_total, head_count, head_width)
    grad_weights = jnp.einsum(
        "ihd,jhd->hij", grad_heads, value_heads, preferred_element_type=jnp.float32
    )
    row_inner = jnp.sum(weights_soft * grad_weights, axis=-1, keepdims=True)
    grad_scores = weights_soft * (grad_weights - row_inner)
    scores_half = grad_scores.astype(jnp.bfloat16)
    derivative_probe_weights = (
        jnp.einsum("hij,jhd->ihd", scores_half, key_heads, preferred_element_type=jnp.float32)
        * softmax_scale
    ).astype(jnp.bfloat16)
    derivative_lookup_weights = (
        jnp.einsum("hij,ihd->jhd", scores_half, query_heads, preferred_element_type=jnp.float32)
        * softmax_scale
    )
    derivative_content_weights = jnp.einsum(
        "hij,ihd->jhd", weights_half, grad_heads, preferred_element_type=jnp.float32
    )
    outputs = (
        modulated_result,
        derivative_logits_sigmoid,
        derivative_probe_weights.reshape(query_total, channel_width),
        derivative_lookup_weights.reshape(key_count, channel_width),
        derivative_content_weights.reshape(key_count, channel_width),
    )
    return (dbias_total + grad_scores, outputs)


def body(
    homolog_embedding,
    pair_input_rows,
    incoming_slope,
    rescale_factor,
    probe_weights,
    lookup_weights,
    content_weights,
    sigmoid_weights,
    final_projection,
    pair_bias_matrix,
):
    highest = lax.Precision.HIGHEST
    head_count = pair_bias_matrix.shape[1]
    row_total, query_total, channel_width = homolog_embedding.shape
    standardized_rows, inverse_deviation = layer_norm_rows(homolog_embedding)
    rescaled_embedding = (standardized_rows * rescale_factor).astype(jnp.bfloat16)
    rescaled_plain = rescaled_embedding.reshape(-1, channel_width)
    probe_vectors = (
        jnp.dot(rescaled_plain, probe_weights, preferred_element_type=jnp.float32)
        .astype(jnp.bfloat16)
        .reshape(row_total, query_total, channel_width)
    )
    sigmoid_factors = jax.nn.sigmoid(
        jnp.dot(rescaled_plain, sigmoid_weights, preferred_element_type=jnp.float32)
    ).reshape(row_total, query_total, channel_width)
    incoming_slope_plain = incoming_slope.reshape(-1, channel_width)
    derivative_modulated = jnp.dot(
        incoming_slope_plain, final_projection.T, preferred_element_type=jnp.float32
    ).reshape(row_total, query_total, channel_width)
    bias_local = jnp.einsum(
        "ijc,ch->hij", pair_input_rows, pair_bias_matrix, preferred_element_type=jnp.float32
    ).astype(jnp.bfloat16)
    bias_full = lax.all_gather(bias_local, "seq", axis=2, tiled=True)
    normed_all = lax.all_gather(rescaled_embedding, "res", axis=1, tiled=True)
    key_count = normed_all.shape[1]
    all_flat = normed_all.reshape(-1, channel_width)
    lookup_vectors = (
        jnp.dot(all_flat, lookup_weights, preferred_element_type=jnp.float32)
        .astype(jnp.bfloat16)
        .reshape(row_total, key_count, channel_width)
    )
    content_vectors = (
        jnp.dot(all_flat, content_weights, preferred_element_type=jnp.float32)
        .astype(jnp.bfloat16)
        .reshape(row_total, key_count, channel_width)
    )
    dbias_init = jnp.zeros(bias_full.shape, jnp.float32)
    dbias_local, row_results = lax.scan(
        functools.partial(row_backward, bias_full, head_count),
        dbias_init,
        (probe_vectors, lookup_vectors, content_vectors, sigmoid_factors, derivative_modulated),
    )
    (
        modulated_result,
        derivative_logits_sigmoid,
        derivative_probe_weights,
        derivative_lookup_weights,
        derivative_content_weights,
    ) = row_results
    key_weight_wide = lookup_weights.astype(jnp.float32)
    value_weight_wide = content_weights.astype(jnp.float32)
    lookup_plain = derivative_lookup_weights.reshape(-1, channel_width)
    content_plain = derivative_content_weights.reshape(-1, channel_width)
    key_term = (
        jnp.dot(lookup_plain, key_weight_wide.T, precision=highest)
        + jnp.dot(content_plain, value_weight_wide.T, precision=highest)
    ).reshape(row_total, -1, channel_width)
    grad_from_keys = lax.psum_scatter(key_term, "res", scatter_dimension=1, tiled=True).reshape(
        -1, channel_width
    )
    all_wide = all_flat.astype(jnp.float32)
    part_key = jnp.dot(all_wide.T, lookup_plain, precision=highest)
    part_value = jnp.dot(all_wide.T, content_plain, precision=highest)
    probe_plain = derivative_probe_weights.reshape(-1, channel_width)
    sigmoid_factor_plain = derivative_logits_sigmoid.reshape(-1, channel_width)
    part_query = jnp.dot(rescaled_plain.T, probe_plain, preferred_element_type=jnp.float32)
    part_gate = jnp.dot(rescaled_plain.T, sigmoid_factor_plain, preferred_element_type=jnp.float32)
    part_out = jnp.dot(
        modulated_result.reshape(-1, channel_width).T,
        incoming_slope_plain,
        preferred_element_type=jnp.float32,
    )
    derivative_rescaled = (
        jnp.dot(probe_plain, probe_weights.T, preferred_element_type=jnp.float32)
        + jnp.dot(sigmoid_factor_plain, sigmoid_weights.T, preferred_element_type=jnp.float32)
        + grad_from_keys
    )
    derivative_rescaled = derivative_rescaled.reshape(row_total, query_total, channel_width)
    part_gain = jnp.sum(derivative_rescaled * standardized_rows, axis=(0, 1))
    centered_scaled_gradient = derivative_rescaled * rescale_factor
    alignment_rows_gradient = (
        inverse_deviation
        * (
            centered_scaled_gradient
            - jnp.mean(centered_scaled_gradient, axis=-1, keepdims=True)
            - standardized_rows
            * jnp.mean(centered_scaled_gradient * standardized_rows, axis=-1, keepdims=True)
        )
    ).astype(jnp.bfloat16)
    dbias_own = lax.psum_scatter(dbias_local, "seq", scatter_dimension=2, tiled=True).astype(
        jnp.bfloat16
    )
    pair_input_gradient = jnp.einsum(
        "hij,ch->ijc", dbias_own, pair_bias_matrix, preferred_element_type=jnp.float32
    ).astype(jnp.bfloat16)
    part_bias = jnp.einsum(
        "ijc,hij->ch", pair_input_rows, dbias_own, preferred_element_type=jnp.float32
    )
    totals = lax.psum(
        (part_gain, part_query, part_key, part_value, part_gate, part_out, part_bias),
        ("seq", "res"),
    )
    return (
        alignment_rows_gradient,
        pair_input_gradient,
        totals[0],
        totals[1],
        totals[2],
        totals[3],
        totals[4],
        totals[5],
        totals[6],
    )


def solution(mesh):
    in_specs = (
        P("seq", "res", None),
        P("res", "seq", None),
        P("seq", "res", None),
        P(),
        P(),
        P(),
        P(),
        P(),
        P(),
        P(),
    )
    out_specs = (P("seq", "res", None), P("res", "seq", None), P(), P(), P(), P(), P(), P(), P())
    return jax.shard_map(body, mesh=mesh, in_specs=in_specs, out_specs=out_specs, check_vma=False)
```

profile of v0, /device:TPU:0, one launch (start us, length us, event | category | flops | bytes accessed | tf_op | source)
XLA Modules:
  0.0 667.7 jit_solution(14989727427753423162)
XLA Ops:
  7.3 6.7 %convolution_convert_fusion.3 = bf16[8,64,512]{2,0,1:T(8,128)(2,1)} fusion(bf16[64,512,128]{2,1,0:T(8,128)(2,1)} %param.13, bf16[128,8]{0,1:T(8,128)(2,1)} %param.21), kind=kOutput, calls=%fused_computation.37 | convolution fusion | flops 67371008 | bytes 8914944 | tf_op jit(solution)/shard_map/ijc,ch->hij/dot_general | solution.py:99
  18.7 26.8 %all-gather.5.cloned.1.call-done = bf16[8,64,2048]{2,0,1:T(8,128)(2,1)} async-done(((bf16[8,64,512]{2,0,1:T(8,128)(2,1)}), bf16[8,64,2048]{2,0,1:T(8,128)(2,1)}) %all-gather.5.cloned.1.call-update) | async-done | bytes 2097168 | tf_op jit(solution)/shard_map/all_gather | solution.py:102
  45.5 4.1 copy.34
  49.5 83.2 %all-gather.3.cloned.1.call-done = bf16[4,2048,256]{2,1,0:T(8,128)(2,1)} async-done(((bf16[4,64,256]{2,1,0:T(8,128)(2,1)}), bf16[4,2048,256]{2,1,0:T(8,128)(2,1)}) %all-gather.3.cloned.1.call-update) | async-done | bytes 4194320 | tf_op jit(solution)/shard_map/all_gather | solution.py:103
  132.8 5.6 convolution_convert_fusion
  141.6 105.2 %while.21 = (s32[]{:T(128)}, f32[8,64,2048]{2,1,0:T(8,128)}, bf16[4,64,256]{1,2,0:T(8,128)(2,1)}, bf16[4,64,256]{1,2,0:T(8,128)(2,1)}, bf16[4,64,256]{1,2,0:T(8,...) while((s32[]{:T(128)}, f32[8,64,2048]{2,1,0:T(8,128)}, ...), condition=%wide.region_6.7_spmd.clone, body=%wide.region_2.6_spmd.clone.sunk | while | flops 422233600 | bytes 126007688 | solution.py:117
  146.3 4.9 fusion.108
  159.7 3.5 fusion.111
  172.6 4.9 fusion.108
  186.0 3.5 fusion.111
  198.9 4.9 fusion.108
  212.3 3.5 fusion.111
  225.2 4.9 fusion.108
  247.0 9.0 %copy.40 = f32[4,2048,256]{2,1,0:T(8,128)} copy(f32[4,2048,256]{1,2,0:T(8,128)} %get-tuple-element.83) | data formatting | bytes 16777216 | tf_op jit(solution)/shard_map/while | solution.py:117
  256.0 8.7 %copy.41 = f32[4,2048,256]{2,1,0:T(8,128)} copy(f32[4,2048,256]{1,2,0:T(8,128)} %get-tuple-element.84) | data formatting | bytes 16777216 | tf_op jit(solution)/shard_map/while | solution.py:117
  264.7 6.6 fusion.38
  271.4 6.4 convolution_add_fusion
  282.2 11.1 %convolution_bitcast_fusion.2 = f32[256,256]{1,0:T(8,128)} fusion(bf16[4,2048,256]{2,1,0:T(8,128)(2,1)} %all-gather.3.cloned.1.call-done, f32[4,2048,256]{1,2,0:T(8,128)} %get-tuple-element.84), kind=kOutput, calls=%fused_computation.40 | convolution fusion | flops 6442450944 | bytes 12845056 | tf_op jit(solution)/shard_map/dot_general | solution.py:142
  293.2 8.4 %convolution_bitcast_fusion.3 = f32[256,256]{1,0:T(8,128)} fusion(bf16[4,2048,256]{2,1,0:T(8,128)(2,1)S(1)} %copy-done.5, f32[4,2048,256]{1,2,0:T(8,128)} %get-tuple-element.83), kind=kOutput, calls=%fused_computation.41 | convolution fusion | flops 6442450944 | bytes 12845056 | tf_op jit(solution)/shard_map/dot_general | solution.py:141
  303.0 4.8 convolution_bitcast_fusion.5
  307.9 5.5 convolution_convert_fusion.2
  313.4 185.4 %reduce-scatter.3.cloned.1.call-done = f32[4,64,256]{2,1,0:T(8,128)} async-done(((f32[4,2048,256]{2,1,0:T(8,128)}), f32[4,64,256]{2,1,0:T(8,128)}) %reduce-scatter.3.cloned.1.call-update) | async-done | bytes 262160 | tf_op jit(solution)/shard_map/reduce_scatter | solution.py:137
  500.4 62.7 %all-reduce = (f32[256]{0:T(256)}, f32[128,8]{0,1:T(8,128)}) all-reduce(f32[256]{0:T(256)S(1)} %get-tuple-element.155, f32[128,8]{0,1:T(8,128)S(1)} %convolution_bitcast_fusion.5), channel_id=1, replica_groups=mesh['seq'=4,'res'=32] {'seq','res'}, use_global_device_ids=true, to_apply=%region_12.13 | all-reduce | flops 1280 | bytes 10240 | tf_op jit(solution)/shard_map/psum | solution.py:178
  564.0 88.8 %all-reduce.4.cloned.1.call-done = (f32[256,256]{1,0:T(8,128)}, f32[256,256]{1,0:T(8,128)}, f32[256,256]{1,0:T(8,128)}, f32[256,256]{1,0:T(8,128)}, f32[256,256]{1,0:T(8,128)}) async-done(((f32[256,256]{1,0:T(8,128)}, f32[256,256]{1,0:T(8,128)}, f32[256,256]{1,0:T(8,128)}, f32[256,256]{1,0:T(8,128)}, f32[256,256]{1,0:T(8,128)}), (f32[256,256]{1,0:T(8,128)}, f32[256,256]{1,0:T(8,128)}, f32[256,256]{1,0:T(8,128)}, ...) | async-done | bytes 1310736 | tf_op jit(solution)/shard_map/psum | solution.py:178
  (221 shorter events, 98.8 us)
Async XLA Ops:
  7.2 131.2 %copy-start = (bf16[256,256]{1,0:T(8,128)(2,1)S(1)}, bf16[256,256]{1,0:T(8,128)(2,1)}, u32[]{:S(2)}) copy-start(bf16[256,256]{1,0:T(8,128)(2,1)} %param.17) | copy-start | bytes 393220
  7.2 6.9 %copy-start.8 = (bf16[4,64,256]{2,1,0:T(8,128)(2,1)S(1)}, bf16[4,64,256]{2,1,0:T(8,128)(2,1)}, u32[]{:S(2)}) copy-start(bf16[4,64,256]{2,1,0:T(8,128)(2,1)} %param.12) | copy-start | bytes 393220
  7.2 7.2 %copy-start.30 = (f32[256]{0:T(256)S(1)}, f32[256]{0:T(256)}, u32[]{:S(2)}) copy-start(f32[256]{0:T(256)} %param.15) | copy-start | bytes 3076
  7.2 8.2 %copy-start.18 = (bf16[256,256]{1,0:T(8,128)(2,1)S(1)}, bf16[256,256]{1,0:T(8,128)(2,1)}, u32[]{:S(2)}) copy-start(bf16[256,256]{1,0:T(8,128)(2,1)} %param.16) | copy-start | bytes 393220
  7.2 9.3 %copy-start.24 = (bf16[256,256]{1,0:T(8,128)(2,1)S(1)}, bf16[256,256]{1,0:T(8,128)(2,1)}, u32[]{:S(2)}) copy-start(bf16[256,256]{1,0:T(8,128)(2,1)} %param.19) | copy-start | bytes 393220
  7.2 10.4 %copy-start.16 = (bf16[4,64,256]{2,1,0:T(8,128)(2,1)S(1)}, bf16[4,64,256]{2,1,0:T(8,128)(2,1)}, u32[]{:S(2)}) copy-start(bf16[4,64,256]{2,1,0:T(8,128)(2,1)} %param.14) | copy-start | bytes 393220
  7.3 10.4 %copy-start.23 = (bf16[256,256]{1,0:T(8,128)(2,1)S(1)}, bf16[256,256]{1,0:T(8,128)(2,1)}, u32[]{:S(2)}) copy-start(bf16[256,256]{1,0:T(8,128)(2,1)} %param.20) | copy-start | bytes 393220
  7.3 38.2 %all-gather.5.cloned.1.call-start = ((), (), s32[]{:S(2)}) async-start(), calls=%async_computation.3 | async-start | bytes 2621440 | tf_op jit(solution)/shard_map/all_gather | solution.py:102
  14.0 118.8 %copy-start.14 = (bf16[256,256]{1,0:T(8,128)(2,1)S(1)}, bf16[256,256]{1,0:T(8,128)(2,1)}, u32[]{:S(2)}) copy-start(bf16[256,256]{1,0:T(8,128)(2,1)} %param.18) | copy-start | bytes 393220
  14.0 118.7 %all-gather.3.cloned.1.call-start = ((), (), s32[]{:S(2)}) async-start(), calls=%async_computation.2 | async-start | bytes 4325376 | tf_op jit(solution)/shard_map/all_gather | solution.py:103
  15.3 286.4 %reduce-scatter.5.cloned.1.call-start = ((), (), s32[]{:S(2)}) async-start(), calls=%async_computation.5 | async-start | bytes 5242880 | tf_op jit(solution)/shard_map/reduce_scatter | solution.py:169
  132.8 5.6 copy-start.4
  151.3 4.7 copy-start.1
  246.8 252.1 %reduce-scatter.3.cloned.1.call-start = ((), (), s32[]{:S(2)}) async-start(), calls=%async_computation.4 | async-start | bytes 8650752 | tf_op jit(solution)/shard_map/reduce_scatter | solution.py:137
  264.7 6.7 copy-start.6
  264.7 6.7 copy-start.15
  277.8 375.0 %all-reduce.4.cloned.1.call-start = ((), (), s32[]{:S(2)}) async-start(), calls=%async_computation.6 | async-start | bytes 2621440 | tf_op jit(solution)/shard_map/psum | solution.py:178
  282.2 11.1 %copy-start.5 = (bf16[4,2048,256]{2,1,0:T(8,128)(2,1)S(1)}, bf16[4,2048,256]{2,1,0:T(8,128)(2,1)}, u32[]{:S(2)}) copy-start(bf16[4,2048,256]{2,1,0:T(8,128)(2,1)} %all-gather.3.cloned.1.call-done) | copy-start | bytes 12582916
  303.0 4.8 copy-start.32
  307.8 191.0 %copy-start.25 = (bf16[256,256]{1,0:T(8,128)(2,1)S(1)}, bf16[256,256]{1,0:T(8,128)(2,1)}, u32[]{:S(2)}) copy-start(bf16[256,256]{1,0:T(8,128)(2,1)} %param.19) | copy-start | bytes 393220
  307.8 191.0 %copy-start.31 = (f32[256]{0:T(256)S(1)}, f32[256]{0:T(256)}, u32[]{:S(2)}) copy-start(f32[256]{0:T(256)} %param.15) | copy-start | bytes 3076
  307.8 192.3 %copy-start.9 = (bf16[4,64,256]{2,1,0:T(8,128)(2,1)S(1)}, bf16[4,64,256]{2,1,0:T(8,128)(2,1)}, u32[]{:S(2)}) copy-start(bf16[4,64,256]{2,1,0:T(8,128)(2,1)} %param.12) | copy-start | bytes 393220
  307.9 192.3 %copy-start.27 = (f32[4,64]{1,0:T(4,128)S(1)}, f32[4,64]{1,0:T(4,128)}, u32[]{:S(2)}) copy-start(f32[4,64]{1,0:T(4,128)} %copy-done.26) | copy-start | bytes 3076
  307.9 192.3 %copy-start.29 = (f32[4,64]{1,0:T(4,128)S(1)}, f32[4,64]{1,0:T(4,128)}, u32[]{:S(2)}) copy-start(f32[4,64]{1,0:T(4,128)} %copy-done.28) | copy-start | bytes 3076
  (35 other events, 85.4 us)
Sparse Core Ops, SparseCore 0:
  14.1 31.2 all-gather.4
  49.2 83.5 all-gather.2
  246.9 42.0 reduce-scatter.4
  291.3 207.5 reduce-scatter.2
  505.0 147.8 all-reduce.3
where the time goes:
time: 670 us; the launch traced here: 668 us
  waiting for transfers between devices  384 us (57%)
  matrix products  116 us (17%)
  local copies, waits for them, and re-layouts  68.4 us (10%)
  blocking collectives  62.7 us (9%)
  other arithmetic  21.5 us (3%)
  between operations  14.2 us (2%)
    reduce_scatter x1, waiting for transfers between devices, body(): lax.psum_scatter(key_term, 'res', scatter_dimension=1, tiled=True)  185 us
    psum x1, waiting for transfers between devices, body(): lax.psum((part_gain, part_query, part_key, part_value, part_gate, part_ou...  88.8 us
    all_gather x1, waiting for transfers between devices, body(): normed_all = lax.all_gather(rescaled_embedding, 'res', axis=1, tiled=True)  83.2 us
    psum x1, blocking collectives, body(): lax.psum((part_gain, part_query, part_key, part_value, part_gate, part_ou...  62.7 us
    all_gather x1, waiting for transfers between devices, body(): bias_full = lax.all_gather(bias_local, 'seq', axis=2, tiled=True)  26.8 us
    sub x4, matrix products, row_backward(): weights_soft = jax.nn.softmax(scores, axis=-1)  19.8 us
    while x4, local copies, waits for them, and re-layouts, body(): lax.scan(functools.partial(row_backward, bias_full, head_count), dbias_in...  17.9 us
    dynamic_slice x32, local copies, waits for them, and re-layouts, body(): lax.scan(functools.partial(row_backward, bias_full, head_count), dbias_in...  16.4 us
  transfers between devices with their start and end apart: 5, of which 4 were waited for; matrix products, arithmetic and copies ran while one was open for 11% of the time, Pallas kernels for 0%

commit v1 on v0

v1 whole, which is shorter than its diff:
```python
import functools
import math

import jax
import jax.numpy as jnp
from jax import lax
from jax.experimental import pallas as pl
from jax.experimental.pallas import tpu as pltpu
from jax.sharding import PartitionSpec as P

MESH = pl.DeviceIdType.MESH
F32 = jnp.float32
BF16 = jnp.bfloat16
VM = pl.BlockSpec(memory_space=pltpu.VMEM)


class Place:
    def __init__(self):
        seq = lax.axis_index("seq")
        res = lax.axis_index("res")
        self.seq, self.res = seq, res
        self.z_lo, self.core = seq // 2, seq % 2
        self.g, self.z_hi = res // 4, res % 2
        self.x_hi = self.g % 2
        x_lo = (res // 2) % 2
        self.h = ((x_lo + self.x_hi) % 2) * 4 + self.z_hi * 2 + self.z_lo

    def spot(self, h):
        return h % 2, ((h // 4 + self.x_hi) % 2) * 2 + (h // 2) % 2

    def member(self, h):
        z_lo, r4 = self.spot(h)
        return (z_lo * 2 + self.core, self.g * 4 + r4)

    def block(self, g):
        return (self.seq, g * 4 + ((self.h // 4 + g % 2) % 2) * 2 + self.z_hi)

    def partner(self):
        return (self.z_lo * 2 + 1 - self.core, self.res)


def enter(devices):
    barrier = pltpu.get_barrier_semaphore()
    for device in devices:
        pl.semaphore_signal(barrier, inc=1, device_id=device, device_id_type=MESH)
    pl.semaphore_wait(barrier, len(devices))


def remote(src, dst, send, recv, device):
    return pltpu.make_async_remote_copy(
        src_ref=src, dst_ref=dst, send_sem=send, recv_sem=recv, device_id=device, device_id_type=MESH
    )


def params(collective_id):
    return pltpu.CompilerParams(
        collective_id=collective_id, has_side_effects=True, vmem_limit_bytes=48 * 1024 * 1024
    )


def aligned(x, n):
    return pl.multiple_of(x * n, n)


def scatter_kernel(t_ref, b_ref, x_ref, bias_ref, ts, tr, bs, br, ps, pr, local):
    p = Place()
    enter([p.member((p.h + k) % 8) for k in range(1, 8)] + [p.partner()])
    z_lo, r4 = p.spot(p.h)
    rows = pl.ds(z_lo * 4, 4)
    toks = pl.ds(aligned(r4, 64), 64)
    cols = pl.ds(aligned(p.seq, 512), 512)
    copies = []
    for k in (4, 3, 5, 2, 6, 1, 7):
        h = (p.h + k) % 8
        dev = p.member(h)
        a = remote(t_ref.at[h], x_ref.at[rows, toks], ts.at[k - 1], tr.at[k - 1], dev)
        b = remote(b_ref.at[h], bias_ref.at[toks, cols], bs.at[k - 1], br.at[k - 1], dev)
        a.start()
        b.start()
        copies += [a, b]
    own = pltpu.make_async_copy(t_ref.at[p.h], x_ref.at[rows, toks], local.at[0])
    own.start()
    own2 = pltpu.make_async_copy(b_ref.at[p.h], bias_ref.at[toks, cols], local.at[1])
    own2.start()
    own.wait()
    own2.wait()
    for c in copies:
        c.wait()
    pair = []
    for b in range(2):
        cols = pl.ds(aligned(b * 2 + p.core, 512), 512)
        c = remote(bias_ref.at[:, cols], bias_ref.at[:, cols], ps.at[b], pr.at[b], p.partner())
        c.start()
        pair.append(c)
    for c in pair:
        c.wait()


def scatter(tokens, bias):
    dma = pltpu.SemaphoreType.DMA
    return pl.pallas_call(
        scatter_kernel,
        out_shape=(
            jax.ShapeDtypeStruct((8, 256, 128), BF16),
            jax.ShapeDtypeStruct((256, 2048), BF16),
        ),
        in_specs=[VM, VM],
        out_specs=(VM, VM),
        scratch_shapes=[dma((7,)), dma((7,)), dma((7,)), dma((7,)), dma((2,)), dma((2,)), dma((2,))],
        compiler_params=params(0),
        name="scatter",
    )(tokens, bias)


def gather_kernel(k_ref, o_ref, ss, rs, local):
    p = Place()
    enter([p.block((p.g + k) % 8) for k in range(1, 8)])
    here = pl.ds(aligned(p.g, 256), 256)
    copies = []
    for k in (4, 3, 5, 2, 6, 1, 7):
        c = remote(k_ref, o_ref.at[:, :, here], ss.at[k - 1], rs.at[k - 1], p.block((p.g + k) % 8))
        c.start()
        copies.append(c)
    own = pltpu.make_async_copy(k_ref, o_ref.at[:, :, here], local)
    own.start()
    own.wait()
    for c in copies:
        c.wait()


def gather(kv):
    dma = pltpu.SemaphoreType.DMA
    return pl.pallas_call(
        gather_kernel,
        out_shape=jax.ShapeDtypeStruct((8, 64, 2048), BF16),
        in_specs=[VM],
        out_specs=VM,
        scratch_shapes=[dma((7,)), dma((7,)), dma],
        compiler_params=params(1),
        name="gather",
    )(kv)


QB = 128


def attention_kernel(x_ref, kv_ref, b_ref, o_ref, dkv_ref, db_ref):
    scale = 1.0 / math.sqrt(32)
    first = pl.program_id(0) == 0
    kt = kv_ref[0, 0:32, :]
    vt = kv_ref[0, 32:64, :]
    tn = (((0,), (0,)), ((), ()))
    nt = (((1,), (1,)), ((), ()))

    dk = jnp.zeros((32, 2048), F32)
    dv = jnp.zeros((32, 2048), F32)
    for n in range(256 // QB):
        q = pl.ds(n * QB, QB)
        qt = x_ref[0, 0:32, q]
        dot = x_ref[0, 96:128, q]
        s = lax.dot_general(qt, kt, tn, preferred_element_type=F32) * scale
        s = s + b_ref[q, :].astype(F32)
        e = jnp.exp(s - jnp.max(s, axis=1, keepdims=True))
        soft = e * (1.0 / jnp.sum(e, axis=1, keepdims=True))
        half = soft.astype(BF16)
        gs = lax.dot_general(dot, vt, tn, preferred_element_type=F32)
        gs = soft * (gs - jnp.sum(soft * gs, axis=1, keepdims=True))
        gh = gs.astype(BF16)

        @pl.when(first)
        def _():
            db_ref[q, :] = gs

        @pl.when(jnp.logical_not(first))
        def _():
            db_ref[q, :] += gs

        o_ref[0, 0:32, q] = lax.dot_general(vt, half, nt, preferred_element_type=F32)
        dq = lax.dot_general(kt, gh, nt, preferred_element_type=F32) * scale
        o_ref[0, 32:64, q] = dq.astype(BF16).astype(F32)
        dk = dk + jnp.dot(qt, gh, preferred_element_type=F32)
        dv = dv + jnp.dot(dot, half, preferred_element_type=F32)
    dkv_ref[0, 0:32, :] = (dk * scale).astype(dkv_ref.dtype)
    dkv_ref[0, 32:64, :] = dv.astype(dkv_ref.dtype)


def attention(x, kv, bias):
    return pl.pallas_call(
        attention_kernel,
        grid=(8,),
        out_shape=(
            jax.ShapeDtypeStruct((8, 64, 256), F32),
            jax.ShapeDtypeStruct((8, 64, 2048), BF16),
            jax.ShapeDtypeStruct((256, 2048), F32),
        ),
        in_specs=[
            pl.BlockSpec((1, 128, 256), lambda s: (s, 0, 0)),
            pl.BlockSpec((1, 64, 2048), lambda s: (s, 0, 0)),
            pl.BlockSpec((256, 2048), lambda s: (0, 0)),
        ],
        out_specs=(
            pl.BlockSpec((1, 64, 256), lambda s: (s, 0, 0)),
            pl.BlockSpec((1, 64, 2048), lambda s: (s, 0, 0)),
            pl.BlockSpec((256, 2048), lambda s: (0, 0)),
        ),
        compiler_params=pltpu.CompilerParams(vmem_limit_bytes=48 * 1024 * 1024),
        name="attention",
    )(x, kv, bias)


def partials_kernel(d_ref, o_ref, buf, ss, rs):
    p = Place()
    enter([p.block((p.g + k) % 8) for k in range(1, 8)])
    copies = []
    for k in (4, 3, 5, 2, 6, 1, 7):
        g = (p.g + k) % 8
        c = remote(
            d_ref.at[:, :, pl.ds(aligned(g, 256), 256)], buf.at[k - 1], ss.at[k - 1], rs.at[k - 1], p.block(g)
        )
        c.start()
        copies.append(c)
    for c in copies:
        c.wait()
    here = pl.ds(aligned(p.g, 256), 256)
    for s in range(8):
        total = d_ref[s, :, here].astype(F32)
        for k in range(7):
            total = total + buf[k, s].astype(F32)
        o_ref[s] = total


def partials(dkv):
    dma = pltpu.SemaphoreType.DMA
    return pl.pallas_call(
        partials_kernel,
        out_shape=jax.ShapeDtypeStruct((8, 64, 256), F32),
        in_specs=[VM],
        out_specs=VM,
        scratch_shapes=[pltpu.VMEM((7, 8, 64, 256), dkv.dtype), dma((7,)), dma((7,))],
        compiler_params=params(2),
        name="partials",
    )(dkv)


def collect_kernel(y_ref, d_ref, t_ref, b_ref, mine, other, ts, tr, bs, br, ps, pr, local):
    p = Place()
    enter([p.member((p.h + k) % 8) for k in range(1, 8)] + [p.partner()])
    copies = []
    for b in range(2):
        cols = pl.ds(aligned(b * 2 + 1 - p.core, 512), 512)
        c = remote(d_ref.at[:, cols], other.at[b], ps.at[b], pr.at[b], p.partner())
        c.start()
        copies.append(c)
    later = []
    for k in (4, 3, 5, 2, 6, 1, 7):
        h = (p.h + k) % 8
        z_lo, r4 = p.spot(h)
        a = remote(
            y_ref.at[pl.ds(z_lo * 4, 4), pl.ds(aligned(r4, 64), 64)],
            t_ref.at[p.h],
            ts.at[k - 1],
            tr.at[k - 1],
            p.member(h),
        )
        a.start()
        later.append(a)
    z_lo, r4 = p.spot(p.h)
    own = pltpu.make_async_copy(
        y_ref.at[pl.ds(z_lo * 4, 4), pl.ds(aligned(r4, 64), 64)], t_ref.at[p.h], local.at[0]
    )
    own.start()
    for b in range(2):
        copies[b].wait()
        cols = pl.ds(aligned(b * 2 + p.core, 512), 512)
        mine[b] = (d_ref[:, cols] + other[b]).astype(BF16)
    for k in (4, 3, 5, 2, 6, 1, 7):
        h = (p.h + k) % 8
        z_lo, r4 = p.spot(h)
        a = remote(
            mine.at[z_lo, pl.ds(aligned(r4, 64), 64)], b_ref.at[p.h], bs.at[k - 1], br.at[k - 1], p.member(h)
        )
        a.start()
        later.append(a)
    z_lo, r4 = p.spot(p.h)
    own2 = pltpu.make_async_copy(mine.at[z_lo, pl.ds(aligned(r4, 64), 64)], b_ref.at[p.h], local.at[1])
    own2.start()
    own.wait()
    own2.wait()
    for a in later:
        a.wait()


def collect(y, d):
    dma = pltpu.SemaphoreType.DMA
    return pl.pallas_call(
        collect_kernel,
        out_shape=(
            jax.ShapeDtypeStruct((8, 4, 64, 128), F32),
            jax.ShapeDtypeStruct((8, 64, 512), BF16),
        ),
        in_specs=[VM, VM],
        out_specs=(VM, VM),
        scratch_shapes=[
            pltpu.VMEM((2, 256, 512), BF16),
            pltpu.VMEM((2, 256, 512), F32),
            dma((7,)), dma((7,)), dma((7,)), dma((7,)), dma((2,)), dma((2,)), dma((2,)),
        ],
        compiler_params=params(3),
        name="collect",
    )(y, d)


def reduce_kernel(w_ref, o_ref, b0, a0, b1, a1, b2, s0, r0, s1, r1, s2, r2, s3, r3, s4, r4, s5, r5):
    p = Place()
    enter(
        [p.member((p.h + k) % 8) for k in range(1, 8)]
        + [p.block((p.g + k) % 8) for k in range(1, 8)]
        + [p.partner()]
    )
    order = (4, 3, 5, 2, 6, 1, 7)
    pair = remote(w_ref.at[1 - p.core], b0, s0, r0, p.partner())
    pair.start()
    pair.wait()
    for m in range(8):
        a0[m] = w_ref[p.core, m] + b0[m]
    copies = []
    for k in order:
        h = (p.h + k) % 8
        c = remote(a0.at[h], b1.at[k - 1], s1.at[k - 1], r1.at[k - 1], p.member(h))
        c.start()
        copies.append(c)
    for c in copies:
        c.wait()
    for m in range(8):
        total = a0[p.h, m]
        for k in range(7):
            total = total + b1[k, m]
        a1[m] = total
    copies = []
    for k in order:
        g = (p.g + k) % 8
        c = remote(a1.at[g], b2.at[k - 1], s2.at[k - 1], r2.at[k - 1], p.block(g))
        c.start()
        copies.append(c)
    for c in copies:
        c.wait()
    total = a1[p.g]
    for k in range(7):
        total = total + b2[k]
    o_ref[p.core, p.h, p.g] = total
    copies = []
    piece = o_ref.at[p.core, p.h, p.g]
    for k in order:
        c = remote(piece, piece, s3.at[k - 1], r3.at[k - 1], p.block((p.g + k) % 8))
        c.start()
        copies.append(c)
    for c in copies:
        c.wait()
    copies = []
    piece = o_ref.at[p.core, p.h]
    for k in order:
        c = remote(piece, piece, s4.at[k - 1], r4.at[k - 1], p.member((p.h + k) % 8))
        c.start()
        copies.append(c)
    for c in copies:
        c.wait()
    piece = o_ref.at[p.core]
    pair = remote(piece, piece, s5, r5, p.partner())
    pair.start()
    pair.wait()


def reduce_all(w):
    dma = pltpu.SemaphoreType.DMA
    n = w.shape[3]
    return pl.pallas_call(
        reduce_kernel,
        out_shape=jax.ShapeDtypeStruct(w.shape, F32),
        in_specs=[VM],
        out_specs=VM,
        scratch_shapes=[
            pltpu.VMEM((8, 8, n, 128), F32),
            pltpu.VMEM((8, 8, n, 128), F32),
            pltpu.VMEM((7, 8, n, 128), F32),
            pltpu.VMEM((8, n, 128), F32),
            pltpu.VMEM((7, n, 128), F32),
            dma, dma, dma((7,)), dma((7,)), dma((7,)), dma((7,)),
            dma((7,)), dma((7,)), dma((7,)), dma((7,)), dma, dma,
        ],
        compiler_params=params(4),
        name="reduce_all",
    )(w)


def body(
    homolog_embedding,
    pair_input_rows,
    incoming_slope,
    rescale_factor,
    probe_weights,
    lookup_weights,
    content_weights,
    sigmoid_weights,
    final_projection,
    pair_bias_matrix,
):
    highest = lax.Precision.HIGHEST
    rows, toks, width = homolog_embedding.shape
    wide = homolog_embedding.astype(F32)
    centered = wide - jnp.mean(wide, axis=-1, keepdims=True)
    inv = lax.rsqrt(jnp.mean(centered * centered, axis=-1, keepdims=True) + 1e-05)
    hat = centered * inv
    plain = (hat * rescale_factor).astype(BF16).reshape(-1, width)
    slope = incoming_slope.reshape(-1, width)

    def dot(a, b):
        return jnp.dot(a, b, preferred_element_type=F32)

    q = dot(plain, probe_weights).astype(BF16)
    k = dot(plain, lookup_weights).astype(BF16)
    v = dot(plain, content_weights).astype(BF16)
    gate = jax.nn.sigmoid(dot(plain, sigmoid_weights))
    grad_gated = dot(slope, final_projection.T)
    grad_att = (grad_gated * gate).astype(BF16)
    tokens = jnp.stack([a.reshape(-1, 8, 32) for a in (q, k, v, grad_att)], axis=2)
    tokens = jnp.transpose(tokens.reshape(-1, 8, 128), (1, 0, 2)).reshape(8, rows, toks, 128)
    bias = jnp.einsum(
        "ijc,ch->hij", pair_input_rows, pair_bias_matrix, preferred_element_type=F32
    ).astype(BF16)

    x, bias_full = scatter(tokens, bias)
    xt = jnp.transpose(x, (0, 2, 1))
    kv = gather(xt[:, 32:96, :])
    out, dkv_part, db = attention(xt, kv, bias_full)
    dkv = partials(dkv_part)
    y = jnp.transpose(jnp.concatenate([out, dkv], axis=1), (0, 2, 1))
    back, db_own = collect(y, db)

    back = jnp.transpose(back.reshape(8, rows * toks, 4, 32), (2, 1, 0, 3)).reshape(4, rows * toks, width)
    attended, dq, dk, dv = back[0], back[1].astype(BF16), back[2], back[3]
    gated = (gate * attended).astype(BF16)
    grad_gate = (grad_gated * attended * gate * (1.0 - gate)).astype(BF16)

    plain_wide = plain.astype(F32)
    part_key = jnp.dot(plain_wide.T, dk, precision=highest)
    part_value = jnp.dot(plain_wide.T, dv, precision=highest)
    part_query = dot(plain.T, dq)
    part_gate = dot(plain.T, grad_gate)
    part_out = dot(gated.T, slope)
    grad_normed = (
        dot(dq, probe_weights.T)
        + dot(grad_gate, sigmoid_weights.T)
        + jnp.dot(dk, lookup_weights.astype(F32).T, precision=highest)
        + jnp.dot(dv, content_weights.astype(F32).T, precision=highest)
    ).reshape(rows, toks, width)
    part_gain = jnp.sum(grad_normed * hat, axis=(0, 1))
    scaled = grad_normed * rescale_factor
    alignment = (
        inv
        * (
            scaled
            - jnp.mean(scaled, axis=-1, keepdims=True)
            - hat * jnp.mean(scaled * hat, axis=-1, keepdims=True)
        )
    ).astype(BF16)
    pair_grad = jnp.einsum(
        "hij,ch->ijc", db_own, pair_bias_matrix, preferred_element_type=F32
    ).astype(BF16)
    part_bias = jnp.einsum("ijc,hij->ch", pair_input_rows, db_own, preferred_element_type=F32)

    packed = jnp.concatenate(
        [
            part_query,
            part_key,
            part_value,
            part_gate,
            part_out,
            part_gain.reshape(1, width),
            part_bias.reshape(4, width),
            jnp.zeros((251, width), F32),
        ],
        axis=0,
    )
    packed = jnp.stack([packed[:, :128], packed[:, 128:]]).reshape(2, 8, 8, 24, 128)
    total = reduce_all(packed).reshape(2, 1536, 128)
    total = jnp.concatenate([total[0], total[1]], axis=1)
    return (
        alignment,
        pair_grad,
        total[1280],
        total[0:256],
        total[256:512],
        total[512:768],
        total[768:1024],
        total[1024:1280],
        total[1281:1285].reshape(128, 8),
    )


def solution(mesh):
    in_specs = (
        P("seq", "res", None),
        P("res", "seq", None),
        P("seq", "res", None),
        P(),
        P(),
        P(),
        P(),
        P(),
        P(),
        P(),
    )
    out_specs = (P("seq", "res", None), P("res", "seq", None), P(), P(), P(), P(), P(), P(), P())
    return jax.shard_map(body, mesh=mesh, in_specs=in_specs, out_specs=out_specs, check_vma=False)
```

time: 670 us -> 219 us (0.33)
  waiting for transfers between devices: 384 us -> 0 us
  Pallas kernels: 0 us -> 167 us
  matrix products: 116 us -> 25.2 us
  blocking collectives: 62.7 us -> 0 us
  local copies, waits for them, and re-layouts: 68.4 us -> 18 us
  other arithmetic: 21.5 us -> 6.46 us
  between operations: 14.2 us -> 1.08 us
    reduce_scatter x2 -> x0, waiting for transfers between devices: 185 us -> none  [the longest x1 185 us: body(): lax.psum_scatter(key_term, 'res', scatter_dimension=1, tiled=True)]
    pallas_call x0 -> x6, Pallas kernels: none -> 167 us  [the longest x1 39 us: reduce_all(): pl.pallas_call(reduce_kernel, out_shape=jax.ShapeDtypeStruct(w.shape, F32...]
    all_gather x2 -> x0, waiting for transfers between devices: 110 us -> none  [the longest x1 83.2 us: body(): normed_all = lax.all_gather(rescaled_embedding, 'res', axis=1, tiled=True)]
    psum x1 -> x0, waiting for transfers between devices: 88.8 us -> none  [body(): lax.psum((part_gain, part_query, part_key, part_value, part_gate, part_ou...]
    dot_general x36 -> x16, matrix products: 89.3 us -> 19.6 us  [the longest x10 7.09 us: dot(): return jnp.dot(a, b, preferred_element_type=F32)]
    psum x1 -> x0, blocking collectives: 62.7 us -> none  [body(): lax.psum((part_gain, part_query, part_key, part_value, part_gate, part_ou...]
    while x60 -> x0, local copies, waits for them, and re-layouts: 22.3 us -> none  [the longest x4 17.9 us: body(): lax.scan(functools.partial(row_backward, bias_full, head_count), dbias_in...]
    sub x4 -> x0, matrix products: 19.8 us -> none  [row_backward(): weights_soft = jax.nn.softmax(scores, axis=-1)]
  transfers between devices with their start and end apart: 5 -> 0, of which waited for: 4 -> 0; matrix products, arithmetic and copies ran while one was open for 11% -> 0% of each run, Pallas kernels for 0% -> 0%
where the time goes in v1:
time: 219 us; the launch traced here: 217 us
  Pallas kernels  167 us (76%)
  matrix products  25.2 us (12%)
  local copies, waits for them, and re-layouts  18 us (8%)
  other arithmetic  6.46 us (3%)
    pallas_call x1, Pallas kernels, reduce_all(): pl.pallas_call(reduce_kernel, out_shape=jax.ShapeDtypeStruct(w.shape, F32...  39 us
    pallas_call x1, Pallas kernels, gather(): pl.pallas_call(gather_kernel, out_shape=jax.ShapeDtypeStruct((8, 64, 2048...  29.9 us
    pallas_call x1, Pallas kernels, partials(): pl.pallas_call(partials_kernel, out_shape=jax.ShapeDtypeStruct((8, 64, 25...  28.6 us
    pallas_call x1, Pallas kernels, attention(): pl.pallas_call(attention_kernel, grid=(8,), out_shape=(jax.ShapeDtypeStru...  24.6 us
    pallas_call x1, Pallas kernels, collect(): pl.pallas_call(collect_kernel, out_shape=(jax.ShapeDtypeStruct((8, 4, 64,...  22.4 us
    pallas_call x1, Pallas kernels, scatter(): pl.pallas_call(scatter_kernel, out_shape=(jax.ShapeDtypeStruct((8, 256, 1...  22 us
    dot_general x10, matrix products, dot(): return jnp.dot(a, b, preferred_element_type=F32)  7.09 us
    unnamed x39, local copies, waits for them, and re-layouts  6.96 us

profile of v1, /device:TPU:0, one launch (start us, length us, event | category | flops | bytes accessed | tf_op | source)
XLA Modules:
  0.0 217.3 jit_solution(13335961367927609853)
XLA Ops:
  1.6 1.0 convert_reduce_fusion
  2.6 1.1 fusion.17
  3.7 1.0 fusion.11
  4.7 1.1 convolution_convert_fusion.1
  5.9 1.1 convolution_convert_fusion.2
  7.0 1.1 convolution_convert_fusion.3
  9.8 5.6 %fusion.28 = bf16[8,64,512]{2,0,1:T(8,128)(2,1)S(1)} fusion(bf16[64,512,128]{2,1,0:T(8,128)(2,1)} %param.11, bf16[128,8]{0,1:T(8,128)(2,1)S(1)} %copy-done.17), kind=kOutput, calls=%fused_computation.59 | convolution fusion | flops 67108864 | bytes 8914944 | tf_op jit(solution)/shard_map/ijc,ch->hij/dot_general | solution.py:427
  15.6 22.0 %scatter.1 = (bf16[8,256,128]{2,1,0:T(8,128)(2,1)S(1)}, bf16[256,2048]{1,0:T(8,128)(2,1)S(1)}) custom-call(bf16[8,4,64,128]{3,2,1,0:T(8,128)(2,1)S(1)} %bitcast.90, bf16[8,64,512]{2,1,0:T(8,128)(2,1)S(1)} %copy.47.b_ref), custom_call_target="tpu_custom_call" | custom-call | tf_op jit(solution)/shard_map/scatter/pallas_call | solution.py:101
  37.6 1.0 copy-done.3
  38.8 29.9 %gather.1.kv_ref = bf16[8,64,2048]{2,1,0:T(8,128)(2,1)S(1)} custom-call(bf16[8,64,256]{2,1,0:T(8,128)(2,1)S(1)} %slice.70.k_ref), custom_call_target="tpu_custom_call" | custom-call | tf_op jit(solution)/shard_map/gather/pallas_call | solution.py:133
  68.7 1.3 copy-done.1
  70.1 24.6 %attention.1 = (f32[8,64,256]{2,1,0:T(8,128)S(1)}, bf16[8,64,2048]{2,1,0:T(8,128)(2,1)S(1)}, f32[256,2048]{1,0:T(8,128)}) custom-call(bf16[8,128,256]{2,1,0:T(8,128)(2,1)S(1)} %bitcast.89, bf16[8,64,2048]{2,1,0:T(8,128)(2,1)} %copy-done.1, bf16[256,2048]{1,0:T(8,128)(2,1)S(1)} %copy-done.4), custom_call_target="tpu_custom_call" | custom-call | tf_op jit(solution)/shard_map/attention/pallas_call | solution.py:188
  94.7 1.3 copy.35
  96.0 28.6 %partials.1 = f32[8,64,256]{2,1,0:T(8,128)S(1)} custom-call(bf16[8,64,2048]{2,1,0:T(8,128)(2,1)S(1)} %get-tuple-element.19.d_ref), custom_call_target="tpu_custom_call" | custom-call | tf_op jit(solution)/shard_map/partials/pallas_call | solution.py:234
  126.2 1.2 copy-done.2
  127.5 22.4 %collect.1 = (f32[8,4,64,128]{3,2,1,0:T(8,128)S(1)}, bf16[8,64,512]{2,1,0:T(8,128)(2,1)S(1)}) custom-call(f32[8,256,128]{2,1,0:T(8,128)S(1)} %maximum_bitcast_fusion.y_ref, f32[256,2048]{1,0:T(8,128)S(1)} %copy-done.2), custom_call_target="tpu_custom_call" | custom-call | tf_op jit(solution)/shard_map/collect/pallas_call | solution.py:295
  149.8 4.8 %convolution_bitcast_fusion = f32[128,8]{0,1:T(8,128)S(1)} fusion(bf16[64,512,128]{2,1,0:T(8,128)(2,1)} %param.11, bf16[8,64,512]{2,1,0:T(8,128)(2,1)S(1)} %get-tuple-element.22), kind=kOutput, calls=%fused_computation.22 | convolution fusion | flops 67108864 | bytes 8916992 | tf_op jit(solution)/shard_map/ijc,hij->ch/dot_general | solution.py:469
  154.8 1.8 copy.37
  156.6 2.5 %reshape.97 = f32[8,256,4,32]{1,3,2,0:T(8,128)S(1)} reshape(f32[8,4,64,128]{2,1,3,0:T(4,128)} %copy.37) | data formatting | bytes 2097152 | tf_op jit(solution)/shard_map/reshape | solution.py:439
  160.7 1.0 fusion.36
  166.0 3.1 %concatenate.11 = f32[1536,256]{1,0:T(8,128)S(1)} concatenate(f32[256,256]{1,0:T(8,128)} %fusion.34, f32[256,256]{1,0:T(8,128)S(1)} %fusion.35, f32[256,256]{1,0:T(8,128)S(1)} %copy-done.7, f32[256,256]{1,0:T(8,128)} %fusion.37, f32[256,256]{1,0:T(8,128)S(1)} %fusion.38, f32[1,256]{1,0:T(1,128)S(1)} %bitcast.121, f32[4,256]{1,0:T(4,128)S(1)} %reshape.100, f32[251,256]{1,0:T(8,128)} %broadcast_in_dim.2), dimensions={0} | concatenate | bytes 3145728 | tf_op jit(solution)/shard_map/concatenate | solution.py:471
  169.4 39.0 %reduce_all.1 = f32[2,8,8,24,128]{4,3,2,1,0:T(8,128)S(1)} custom-call(f32[2,8,8,24,128]{4,3,2,1,0:T(8,128)S(1)} %pad_maximum_fusion.w_ref), custom_call_target="tpu_custom_call" | custom-call | tf_op jit(solution)/shard_map/reduce_all/pallas_call | solution.py:376
  210.0 1.1 fusion.18
  211.8 5.5 %convolution_convert_fusion = bf16[64,512,128]{2,1,0:T(8,128)(2,1)} fusion(bf16[8,64,512]{2,1,0:T(8,128)(2,1)S(1)} %get-tuple-element.22, bf16[128,8]{0,1:T(8,128)(2,1)S(1)} %copy-done.18), kind=kOutput, calls=%fused_computation | convolution fusion | flops 71303168 | bytes 8914944 | tf_op jit(solution)/shard_map/hij,ch->ijc/dot_general | solution.py:466
  (72 shorter events, 13.0 us)
Async XLA Ops:
  0.6 0.9 copy-start
  0.7 7.5 %copy-start.15 = (bf16[256,256]{1,0:T(8,128)(2,1)S(1)}, bf16[256,256]{1,0:T(8,128)(2,1)}, u32[]{:S(2)}) copy-start(bf16[256,256]{1,0:T(8,128)(2,1)} %param.17) | copy-start | bytes 393220
  0.7 7.8 %copy-start.14 = (bf16[256,256]{1,0:T(8,128)(2,1)S(1)}, bf16[256,256]{1,0:T(8,128)(2,1)}, u32[]{:S(2)}) copy-start(bf16[256,256]{1,0:T(8,128)(2,1)} %param.18) | copy-start | bytes 393220
  8.4 1.0 copy-start.8
  8.5 1.3 copy-start.17
  37.6 1.0 copy-start.3
  38.8 31.3 %copy-start.4 = (bf16[256,2048]{1,0:T(8,128)(2,1)S(1)}, bf16[256,2048]{1,0:T(8,128)(2,1)}, u32[]{:S(2)}) copy-start(bf16[256,2048]{1,0:T(8,128)(2,1)} %copy-done.3) | copy-start | bytes 3145732
  68.7 1.3 copy-start.1
  124.6 1.2 copy-start.5
  125.9 1.6 copy-start.2
  159.1 1.0 copy-start.9
  159.1 1.0 copy-start.10
  160.2 3.5 %copy-start.13 = (bf16[256,256]{1,0:T(8,128)(2,1)S(1)}, bf16[256,256]{1,0:T(8,128)(2,1)}, u32[]{:S(2)}) copy-start(bf16[256,256]{1,0:T(8,128)(2,1)} %param.14) | copy-start | bytes 393220
  160.7 3.4 %copy-start.11 = (bf16[256,256]{1,0:T(8,128)(2,1)S(1)}, bf16[256,256]{1,0:T(8,128)(2,1)}, u32[]{:S(2)}) copy-start(bf16[256,256]{1,0:T(8,128)(2,1)} %param.15) | copy-start | bytes 393220
  161.7 2.8 %copy-start.12 = (bf16[256,256]{1,0:T(8,128)(2,1)S(1)}, bf16[256,256]{1,0:T(8,128)(2,1)}, u32[]{:S(2)}) copy-start(bf16[256,256]{1,0:T(8,128)(2,1)} %param.16) | copy-start | bytes 393220
  161.7 2.8 %copy-start.16 = (f32[256]{0:T(256)S(1)}, f32[256]{0:T(256)}, u32[]{:S(2)}) copy-start(f32[256]{0:T(256)} %param.13) | copy-start | bytes 3076
  163.6 1.5 copy-start.6
  164.1 1.9 copy-start.7
  210.0 1.8 copy-start.18

commit v2 on v1

v2 whole, which is shorter than its diff:
```python
import functools
import math

import jax
import jax.numpy as jnp
from jax import lax
from jax.experimental import pallas as pl
from jax.experimental.pallas import tpu as pltpu
from jax.sharding import PartitionSpec as P

MESH = pl.DeviceIdType.MESH
F32 = jnp.float32
BF16 = jnp.bfloat16
VM = pl.BlockSpec(memory_space=pltpu.VMEM)


class Place:
    def __init__(self):
        seq = lax.axis_index("seq")
        res = lax.axis_index("res")
        self.seq, self.res = seq, res
        self.z_lo, self.core = seq // 2, seq % 2
        self.g, self.z_hi = res // 4, res % 2
        self.x_hi = self.g % 2
        x_lo = (res // 2) % 2
        self.h = ((x_lo + self.x_hi) % 2) * 4 + self.z_hi * 2 + self.z_lo

    def spot(self, h):
        return h % 2, ((h // 4 + self.x_hi) % 2) * 2 + (h // 2) % 2

    def member(self, h):
        z_lo, r4 = self.spot(h)
        return (z_lo * 2 + self.core, self.g * 4 + r4)

    def block(self, g):
        return (self.seq, g * 4 + ((self.h // 4 + g % 2) % 2) * 2 + self.z_hi)

    def partner(self):
        return (self.z_lo * 2 + 1 - self.core, self.res)


def enter(devices):
    barrier = pltpu.get_barrier_semaphore()
    for device in devices:
        pl.semaphore_signal(barrier, inc=1, device_id=device, device_id_type=MESH)
    pl.semaphore_wait(barrier, len(devices))


def remote(src, dst, send, recv, device):
    return pltpu.make_async_remote_copy(
        src_ref=src, dst_ref=dst, send_sem=send, recv_sem=recv, device_id=device, device_id_type=MESH
    )


def params(collective_id):
    return pltpu.CompilerParams(
        collective_id=collective_id, has_side_effects=True, vmem_limit_bytes=48 * 1024 * 1024
    )


def aligned(x, n):
    return pl.multiple_of(x * n, n)


ORDER = (4, 3, 5, 2, 6, 1, 7)
CHUNKS = 4
QB = 128


def scatter_kernel(t_ref, x_ref, ts, tr, local):
    p = Place()
    enter([p.member((p.h + k) % 8) for k in range(1, 8)])
    z_lo, r4 = p.spot(p.h)
    here = x_ref.at[pl.ds(z_lo * 4, 4), pl.ds(aligned(r4, 64), 64)]
    copies = []
    for k in ORDER:
        h = (p.h + k) % 8
        a = remote(t_ref.at[h], here, ts.at[k - 1], tr.at[k - 1], p.member(h))
        a.start()
        copies.append(a)
    own = pltpu.make_async_copy(t_ref.at[p.h], here, local)
    own.start()
    own.wait()
    for c in copies:
        c.wait()


def scatter(tokens):
    dma = pltpu.SemaphoreType.DMA
    return pl.pallas_call(
        scatter_kernel,
        out_shape=jax.ShapeDtypeStruct((8, 256, 128), BF16),
        in_specs=[VM],
        out_specs=VM,
        scratch_shapes=[dma((7,)), dma((7,)), dma],
        compiler_params=params(0),
        name="scatter",
    )(tokens)


def row_backward(xt, kv, bias, db, dkv, row):
    scale = 1.0 / math.sqrt(32)
    kt = kv[row, 0:32, :]
    vt = kv[row, 32:64, :]
    tn = (((0,), (0,)), ((), ()))
    nt = (((1,), (1,)), ((), ()))
    dk = jnp.zeros((32, 2048), F32)
    dv = jnp.zeros((32, 2048), F32)
    outs = []
    for n in range(256 // QB):
        q = pl.ds(n * QB, QB)
        qt = xt[row, 0:32, q]
        dot = xt[row, 96:128, q]
        s = lax.dot_general(qt, kt, tn, preferred_element_type=F32) * scale
        s = s + bias[q, :].astype(F32)
        e = jnp.exp(s - jnp.max(s, axis=1, keepdims=True))
        soft = e * (1.0 / jnp.sum(e, axis=1, keepdims=True))
        half = soft.astype(BF16)
        gs = lax.dot_general(dot, vt, tn, preferred_element_type=F32)
        gs = soft * (gs - jnp.sum(soft * gs, axis=1, keepdims=True))
        gh = gs.astype(BF16)
        db[q, :] += gs
        att = lax.dot_general(vt, half, nt, preferred_element_type=F32)
        dq = lax.dot_general(kt, gh, nt, preferred_element_type=F32) * scale
        outs.append(jnp.concatenate([att, dq.astype(BF16).astype(F32)], axis=0))
        dk = dk + jnp.dot(qt, gh, preferred_element_type=F32)
        dv = dv + jnp.dot(dot, half, preferred_element_type=F32)
    dkv[row, 0:32, :] = (dk * scale).astype(dkv.dtype)
    dkv[row, 32:64, :] = dv.astype(dkv.dtype)
    return jnp.concatenate(outs, axis=1)


def main_kernel(
    xt, b_ref, ta, td, bo,
    kv, bias, db, dkv, parts, ya, yd, mine, other,
    ks, kr, bs, br, ps, pr, es, er, as_, ar, ds, dr, fs, fr, hs, hr, local,
):
    p = Place()
    enter(
        [p.member((p.h + k) % 8) for k in range(1, 8)]
        + [p.block((p.g + k) % 8) for k in range(1, 8)]
        + [p.partner()]
    )
    z_lo, r4 = p.spot(p.h)
    toks = pl.ds(aligned(r4, 64), 64)
    here = pl.ds(aligned(p.g, 256), 256)
    per = 8 // CHUNKS

    def keys(c, k):
        rows = pl.ds(c * per, per)
        return remote(
            xt.at[rows, 32:96], kv.at[rows, :, here], ks.at[c, k - 1], kr.at[c, k - 1], p.block((p.g + k) % 8)
        )

    def partial(c, k):
        rows = pl.ds(c * per, per)
        g = (p.g + k) % 8
        return remote(
            dkv.at[rows, :, pl.ds(aligned(g, 256), 256)],
            parts.at[k - 1, rows],
            es.at[c, k - 1],
            er.at[c, k - 1],
            p.block(g),
        )

    first = []
    cols = pl.ds(aligned(p.seq, 512), 512)
    for k in ORDER:
        h = (p.h + k) % 8
        b = remote(b_ref.at[h], bias.at[toks, cols], bs.at[k - 1], br.at[k - 1], p.member(h))
        b.start()
        first.append(b)
        keys(0, k).start()
    own_b = pltpu.make_async_copy(b_ref.at[p.h], bias.at[toks, cols], local.at[0])
    own_b.start()
    own_k = pltpu.make_async_copy(xt.at[:, 32:96], kv.at[:, :, here], local.at[1])
    own_k.start()
    for c in range(1, CHUNKS):
        for k in ORDER:
            keys(c, k).start()
    db[...] = jnp.zeros_like(db)
    own_b.wait()
    own_k.wait()
    for b in first:
        b.wait()
    first = []
    for b in range(2):
        cols = pl.ds(aligned(b * 2 + p.core, 512), 512)
        c = remote(bias.at[:, cols], bias.at[:, cols], ps.at[b], pr.at[b], p.partner())
        c.start()
        first.append(c)
    for c in first:
        c.wait()

    def step(c, carry):
        for k in ORDER:
            keys(c, k).wait_recv()
        outs = []
        for i in range(per):
            outs.append(row_backward(xt, kv, bias, db, dkv, c * per + i))
        for k in ORDER:
            partial(c, k).start()
        ya[c] = jnp.transpose(jnp.concatenate(outs, axis=0))
        return carry

    lax.fori_loop(0, CHUNKS, step, 0)

    pair = []
    for b in range(2):
        cols = pl.ds(aligned(b * 2 + 1 - p.core, 512), 512)
        c = remote(db.at[:, cols], other.at[b], fs.at[b], fr.at[b], p.partner())
        c.start()
        pair.append(c)

    def give(src, dst, send, recv, k):
        h = (p.h + k) % 8
        z, r = p.spot(h)
        return remote(
            src.at[pl.ds(z * 2, 2), pl.ds(aligned(r, 64), 64)], dst.at[p.h], send.at[k - 1], recv.at[k - 1], p.member(h)
        )

    last = []
    for k in ORDER:
        a = give(ya, ta, as_, ar, k)
        a.start()
        last.append(a)
    own_a = pltpu.make_async_copy(ya.at[pl.ds(z_lo * 2, 2), toks], ta.at[p.h], local.at[0])
    own_a.start()
    for b in range(2):
        pair[b].wait()
        cols = pl.ds(aligned(b * 2 + p.core, 512), 512)
        mine[b] = (db[:, cols] + other[b]).astype(BF16)
    for k in ORDER:
        h = (p.h + k) % 8
        z, r = p.spot(h)
        a = remote(
            mine.at[z, pl.ds(aligned(r, 64), 64)], bo.at[p.h], hs.at[k - 1], hr.at[k - 1], p.member(h)
        )
        a.start()
        last.append(a)
    own_m = pltpu.make_async_copy(mine.at[z_lo, toks], bo.at[p.h], local.at[1])
    own_m.start()

    def total(c, carry):
        for k in ORDER:
            partial(c, k).wait_recv()
        outs = []
        for i in range(per):
            row = c * per + i
            t = dkv[row, :, here].astype(F32)
            for k in range(7):
                t = t + parts[k, row].astype(F32)
            outs.append(t)
        yd[c] = jnp.transpose(jnp.concatenate(outs, axis=0))
        return carry

    lax.fori_loop(0, CHUNKS, total, 0)
    for k in ORDER:
        a = give(yd, td, ds, dr, k)
        a.start()
        last.append(a)
    own_d = pltpu.make_async_copy(yd.at[pl.ds(z_lo * 2, 2), toks], td.at[p.h], local.at[2])
    own_d.start()
    own_a.wait()
    own_m.wait()
    own_d.wait()
    for a in last:
        a.wait()

    def drain(c, carry):
        for k in ORDER:
            keys(c, k).wait_send()
            partial(c, k).wait_send()
        return carry

    lax.fori_loop(0, CHUNKS, drain, 0)


def main(xt, bias):
    dma = pltpu.SemaphoreType.DMA
    vmem = pltpu.VMEM
    return pl.pallas_call(
        main_kernel,
        out_shape=(
            jax.ShapeDtypeStruct((8, 2, 64, 128), F32),
            jax.ShapeDtypeStruct((8, 2, 64, 128), F32),
            jax.ShapeDtypeStruct((8, 64, 512), BF16),
        ),
        in_specs=[VM, VM],
        out_specs=(VM, VM, VM),
        scratch_shapes=[
            vmem((8, 64, 2048), BF16),
            vmem((256, 2048), BF16),
            vmem((256, 2048), F32),
            vmem((8, 64, 2048), BF16),
            vmem((7, 8, 64, 256), BF16),
            vmem((4, 256, 128), F32),
            vmem((4, 256, 128), F32),
            vmem((2, 256, 512), BF16),
            vmem((2, 256, 512), F32),
            dma((CHUNKS, 7)), dma((CHUNKS, 7)),
            dma((7,)), dma((7,)),
            dma((2,)), dma((2,)),
            dma((CHUNKS, 7)), dma((CHUNKS, 7)),
            dma((7,)), dma((7,)),
            dma((7,)), dma((7,)),
            dma((2,)), dma((2,)),
            dma((7,)), dma((7,)),
            dma((3,)),
        ],
        compiler_params=params(1),
        name="main",
    )(xt, bias)


def reduce_kernel(w_ref, o_ref, b0, a0, b1, a1, b2, s0, r0, s1, r1, s2, r2, s3, r3, s4, r4, s5, r5):
    p = Place()
    enter(
        [p.member((p.h + k) % 8) for k in range(1, 8)]
        + [p.block((p.g + k) % 8) for k in range(1, 8)]
        + [p.partner()]
    )
    pair = remote(w_ref.at[1 - p.core], b0, s0, r0, p.partner())
    pair.start()
    pair.wait()
    for m in range(8):
        a0[m] = w_ref[p.core, m] + b0[m]
    copies = []
    for k in ORDER:
        h = (p.h + k) % 8
        c = remote(a0.at[h], b1.at[k - 1], s1.at[k - 1], r1.at[k - 1], p.member(h))
        c.start()
        copies.append(c)
    for c in copies:
        c.wait()
    for m in range(8):
        total = a0[p.h, m]
        for k in range(7):
            total = total + b1[k, m]
        a1[m] = total
    copies = []
    for k in ORDER:
        g = (p.g + k) % 8
        c = remote(a1.at[g], b2.at[k - 1], s2.at[k - 1], r2.at[k - 1], p.block(g))
        c.start()
        copies.append(c)
    for c in copies:
        c.wait()
    total = a1[p.g]
    for k in range(7):
        total = total + b2[k]
    o_ref[p.core, p.h, p.g] = total
    copies = []
    piece = o_ref.at[p.core, p.h, p.g]
    for k in ORDER:
        c = remote(piece, piece, s3.at[k - 1], r3.at[k - 1], p.block((p.g + k) % 8))
        c.start()
        copies.append(c)
    for c in copies:
        c.wait()
    copies = []
    piece = o_ref.at[p.core, p.h]
    for k in ORDER:
        c = remote(piece, piece, s4.at[k - 1], r4.at[k - 1], p.member((p.h + k) % 8))
        c.start()
        copies.append(c)
    for c in copies:
        c.wait()
    piece = o_ref.at[p.core]
    pair = remote(piece, piece, s5, r5, p.partner())
    pair.start()
    pair.wait()


def reduce_all(w):
    dma = pltpu.SemaphoreType.DMA
    n = w.shape[3]
    return pl.pallas_call(
        reduce_kernel,
        out_shape=jax.ShapeDtypeStruct(w.shape, F32),
        in_specs=[VM],
        out_specs=VM,
        scratch_shapes=[
            pltpu.VMEM((8, 8, n, 128), F32),
            pltpu.VMEM((8, 8, n, 128), F32),
            pltpu.VMEM((7, 8, n, 128), F32),
            pltpu.VMEM((8, n, 128), F32),
            pltpu.VMEM((7, n, 128), F32),
            dma, dma, dma((7,)), dma((7,)), dma((7,)), dma((7,)),
            dma((7,)), dma((7,)), dma((7,)), dma((7,)), dma, dma,
        ],
        compiler_params=params(2),
        name="reduce_all",
    )(w)


def body(
    homolog_embedding,
    pair_input_rows,
    incoming_slope,
    rescale_factor,
    probe_weights,
    lookup_weights,
    content_weights,
    sigmoid_weights,
    final_projection,
    pair_bias_matrix,
):
    highest = lax.Precision.HIGHEST
    rows, toks, width = homolog_embedding.shape
    wide = homolog_embedding.astype(F32)
    centered = wide - jnp.mean(wide, axis=-1, keepdims=True)
    inv = lax.rsqrt(jnp.mean(centered * centered, axis=-1, keepdims=True) + 1e-05)
    hat = centered * inv
    plain = (hat * rescale_factor).astype(BF16).reshape(-1, width)
    slope = incoming_slope.reshape(-1, width)

    def dot(a, b):
        return jnp.dot(a, b, preferred_element_type=F32)

    q = dot(plain, probe_weights).astype(BF16)
    k = dot(plain, lookup_weights).astype(BF16)
    v = dot(plain, content_weights).astype(BF16)
    gate = jax.nn.sigmoid(dot(plain, sigmoid_weights))
    grad_gated = dot(slope, final_projection.T)
    grad_att = (grad_gated * gate).astype(BF16)
    tokens = jnp.stack([a.reshape(-1, 8, 32) for a in (q, k, v, grad_att)], axis=2)
    tokens = jnp.transpose(tokens.reshape(-1, 8, 128), (1, 0, 2)).reshape(8, rows, toks, 128)
    bias = jnp.einsum(
        "ijc,ch->hij", pair_input_rows, pair_bias_matrix, preferred_element_type=F32
    ).astype(BF16)

    xt = jnp.transpose(scatter(tokens), (0, 2, 1))
    back, back_kv, db_own = main(xt, bias)

    def tokenwise(a):
        a = jnp.transpose(a.reshape(8, 2, toks, 2, 2, 32), (4, 1, 3, 2, 0, 5))
        return a.reshape(2, rows * toks, width)

    attended, dq = tokenwise(back)
    dq = dq.astype(BF16)
    dk, dv = tokenwise(back_kv)
    gated = (gate * attended).astype(BF16)
    grad_gate = (grad_gated * attended * gate * (1.0 - gate)).astype(BF16)

    plain_wide = plain.astype(F32)
    part_key = jnp.dot(plain_wide.T, dk, precision=highest)
    part_value = jnp.dot(plain_wide.T, dv, precision=highest)
    part_query = dot(plain.T, dq)
    part_gate = dot(plain.T, grad_gate)
    part_out = dot(gated.T, slope)
    grad_normed = (
        dot(dq, probe_weights.T)
        + dot(grad_gate, sigmoid_weights.T)
        + jnp.dot(dk, lookup_weights.astype(F32).T, precision=highest)
        + jnp.dot(dv, content_weights.astype(F32).T, precision=highest)
    ).reshape(rows, toks, width)
    part_gain = jnp.sum(grad_normed * hat, axis=(0, 1))
    scaled = grad_normed * rescale_factor
    alignment = (
        inv
        * (
            scaled
            - jnp.mean(scaled, axis=-1, keepdims=True)
            - hat * jnp.mean(scaled * hat, axis=-1, keepdims=True)
        )
    ).astype(BF16)
    pair_grad = jnp.einsum(
        "hij,ch->ijc", db_own, pair_bias_matrix, preferred_element_type=F32
    ).astype(BF16)
    part_bias = jnp.einsum("ijc,hij->ch", pair_input_rows, db_own, preferred_element_type=F32)

    packed = jnp.concatenate(
        [
            part_query,
            part_key,
            part_value,
            part_gate,
            part_out,
            part_gain.reshape(1, width),
            part_bias.reshape(4, width),
            jnp.zeros((251, width), F32),
        ],
        axis=0,
    )
    packed = jnp.stack([packed[:, :128], packed[:, 128:]]).reshape(2, 8, 8, 24, 128)
    total = reduce_all(packed).reshape(2, 1536, 128)
    total = jnp.concatenate([total[0], total[1]], axis=1)
    return (
        alignment,
        pair_grad,
        total[1280],
        total[0:256],
        total[256:512],
        total[512:768],
        total[768:1024],
        total[1024:1280],
        total[1281:1285].reshape(128, 8),
    )


def solution(mesh):
    in_specs = (
        P("seq", "res", None),
        P("res", "seq", None),
        P("seq", "res", None),
        P(),
        P(),
        P(),
        P(),
        P(),
        P(),
        P(),
    )
    out_specs = (P("seq", "res", None), P("res", "seq", None), P(), P(), P(), P(), P(), P(), P())
    return jax.shard_map(body, mesh=mesh, in_specs=in_specs, out_specs=out_specs, check_vma=False)
```

time: 219 us -> 158 us (0.72)
  Pallas kernels: 167 us -> 113 us
  local copies, waits for them, and re-layouts: 18 us -> 10.6 us
    pallas_call x5 -> x2, Pallas kernels: 128 us -> 73.1 us  [the longest x1 60.1 us: main(): pl.pallas_call(main_kernel, out_shape=(jax.ShapeDtypeStruct((8, 2, 64, 12...]
    unnamed x39 -> x31, local copies, waits for them, and re-layouts: 6.96 us -> 1.71 us
    another operation x0 -> x9, local copies, waits for them, and re-layouts: none -> 2.73 us  [the longest x5 1.79 us: body(): dk, dv = tokenwise(back_kv)]
    pallas_call x4 -> x3, local copies, waits for them, and re-layouts: 3.61 us -> 0.89 us  [the longest x2 0.68 us: main(): pl.pallas_call(main_kernel, out_shape=(jax.ShapeDtypeStruct((8, 2, 64, 12...]
    reshape x1 -> x0, local copies, waits for them, and re-layouts: 2.48 us -> none  [body(): back.reshape(8, rows * toks, 4, 32)]
where the time goes in v2:
time: 158 us; the launch traced here: 156 us
  Pallas kernels  113 us (72%)
  matrix products  25.2 us (16%)
  local copies, waits for them, and re-layouts  10.6 us (7%)
  other arithmetic  6.11 us (4%)
    pallas_call x1, Pallas kernels, main(): pl.pallas_call(main_kernel, out_shape=(jax.ShapeDtypeStruct((8, 2, 64, 12...  60.1 us
    pallas_call x1, Pallas kernels, reduce_all(): pl.pallas_call(reduce_kernel, out_shape=jax.ShapeDtypeStruct(w.shape, F32...  40.1 us
    pallas_call x1, Pallas kernels, scatter(): pl.pallas_call(scatter_kernel, out_shape=jax.ShapeDtypeStruct((8, 256, 12...  13 us
    dot_general x10, matrix products, dot(): return jnp.dot(a, b, preferred_element_type=F32)  6.36 us
    dot_general x1, matrix products, body(): jnp.einsum('ijc,ch->hij', pair_input_rows, pair_bias_matrix, preferred_el...  5.64 us
    dot_general x1, matrix products, body(): jnp.einsum('hij,ch->ijc', db_own, pair_bias_matrix, preferred_element_typ...  5.5 us
    dot_general x1, matrix products, body(): jnp.einsum('ijc,hij->ch', pair_input_rows, db_own, preferred_element_type...  4.78 us

profile of v2, /device:TPU:0, one launch (start us, length us, event | category | flops | bytes accessed | tf_op | source)
XLA Modules:
  0.0 156.2 jit_solution(7021532669008554395)
XLA Ops:
  0.7 0.9 copy-done
  1.6 1.0 convert_reduce_fusion
  2.6 1.1 fusion.17
  3.7 1.0 fusion.11
  4.7 1.1 convolution_convert_fusion.1
  5.9 1.1 convolution_convert_fusion.2
  7.0 1.1 convolution_convert_fusion.3
  8.5 0.9 multiply_convert_fusion.2
  9.8 13.0 %scatter.1 = bf16[8,256,128]{2,1,0:T(8,128)(2,1)S(1)} custom-call(bf16[8,4,64,128]{3,2,1,0:T(8,128)(2,1)S(1)} %bitcast.83), custom_call_target="tpu_custom_call" | custom-call | tf_op jit(solution)/shard_map/scatter/pallas_call | solution.py:90
  23.0 5.6 %fusion.25 = bf16[8,64,512]{2,0,1:T(8,128)(2,1)S(1)} fusion(bf16[64,512,128]{2,1,0:T(8,128)(2,1)} %param.11, bf16[128,8]{0,1:T(8,128)(2,1)S(1)} %copy-done.13), kind=kOutput, calls=%fused_computation.55 | convolution fusion | flops 67108864 | bytes 8914944 | tf_op jit(solution)/shard_map/ijc,ch->hij/dot_general | solution.py:429
  28.8 60.1 %main.1 = (f32[8,2,64,128]{3,2,1,0:T(8,128)S(1)}, f32[8,2,64,128]{3,2,1,0:T(8,128)S(1)}, bf16[8,64,512]{2,1,0:T(8,128)(2,1)S(1)}) custom-call(bf16[8,128,256]{2,1,0:T(8,128)(2,1)S(1)} %bitcast.82, bf16[8,64,512]{2,1,0:T(8,128)(2,1)S(1)} %copy.48.b_ref), custom_call_target="tpu_custom_call" | custom-call | tf_op jit(solution)/shard_map/main/pallas_call | solution.py:282
  88.9 4.8 %convolution_bitcast_fusion = f32[128,8]{0,1:T(8,128)S(1)} fusion(bf16[64,512,128]{2,1,0:T(8,128)(2,1)} %param.11, bf16[8,64,512]{2,1,0:T(8,128)(2,1)S(1)} %get-tuple-element.14), kind=kOutput, calls=%fused_computation.22 | convolution fusion | flops 67108864 | bytes 8916992 | tf_op jit(solution)/shard_map/ijc,hij->ch/dot_general | solution.py:471
  96.1 0.9 fusion.31
  99.0 1.0 fusion.33
  101.3 0.5 multiply_reduce_fusion
  101.8 1.0 fusion.32
  103.2 0.7 broadcast_in_dim.2
  103.9 3.1 %concatenate.7 = f32[1536,256]{1,0:T(8,128)S(1)} concatenate(f32[256,256]{1,0:T(8,128)S(1)} %copy-done.5, f32[256,256]{1,0:T(8,128)} %fusion.32, f32[256,256]{1,0:T(8,128)} %fusion.33, f32[256,256]{1,0:T(8,128)S(1)} %fusion.34, f32[256,256]{1,0:T(8,128)S(1)} %fusion.23, f32[1,256]{1,0:T(1,128)S(1)} %bitcast.109, f32[4,256]{1,0:T(4,128)S(1)} %reshape.105, f32[251,256]{1,0:T(8,128)} %broadcast_in_dim.2), dimensions={0} | concatenate | bytes 3145728 | tf_op jit(solution)/shard_map/concatenate | solution.py:473
  107.2 40.1 %reduce_all.1 = f32[2,8,8,24,128]{4,3,2,1,0:T(8,128)S(1)} custom-call(f32[2,8,8,24,128]{4,3,2,1,0:T(8,128)S(1)} %pad_maximum_fusion.w_ref), custom_call_target="tpu_custom_call" | custom-call | tf_op jit(solution)/shard_map/reduce_all/pallas_call | solution.py:378
  147.4 0.6 pad_maximum_fusion.3
  148.0 0.9 fusion.15
  148.9 1.1 fusion.18
  150.0 0.7 copy.42
  150.7 5.5 %convolution_convert_fusion = bf16[64,512,128]{2,1,0:T(8,128)(2,1)} fusion(bf16[8,64,512]{2,1,0:T(8,128)(2,1)S(1)} %get-tuple-element.14, bf16[128,8]{0,1:T(8,128)(2,1)S(1)} %copy-done.14), kind=kOutput, calls=%fused_computation | convolution fusion | flops 71303168 | bytes 8914944 | tf_op jit(solution)/shard_map/hij,ch->ijc/dot_general | solution.py:468
  (66 shorter events, 7.2 us)
Async XLA Ops:
  0.6 0.9 copy-start
  0.7 7.5 %copy-start.10 = (bf16[256,256]{1,0:T(8,128)(2,1)S(1)}, bf16[256,256]{1,0:T(8,128)(2,1)}, u32[]{:S(2)}) copy-start(bf16[256,256]{1,0:T(8,128)(2,1)} %param.17) | copy-start | bytes 393220
  0.7 7.8 %copy-start.9 = (bf16[256,256]{1,0:T(8,128)(2,1)S(1)}, bf16[256,256]{1,0:T(8,128)(2,1)}, u32[]{:S(2)}) copy-start(bf16[256,256]{1,0:T(8,128)(2,1)} %param.18) | copy-start | bytes 393220
  8.4 1.0 copy-start.2
  9.5 13.5 %copy-start.13 = (bf16[128,8]{0,1:T(8,128)(2,1)S(1)}, bf16[128,8]{0,1:T(8,128)(2,1)}, u32[]{:S(2)}) copy-start(bf16[128,8]{0,1:T(8,128)(2,1)} %param.19) | copy-start | bytes 6148
  94.3 1.0 copy-start.3
  94.3 1.0 copy-start.4
  95.4 1.6 %copy-start.8 = (bf16[256,256]{1,0:T(8,128)(2,1)S(1)}, bf16[256,256]{1,0:T(8,128)(2,1)}, u32[]{:S(2)}) copy-start(bf16[256,256]{1,0:T(8,128)(2,1)} %param.14) | copy-start | bytes 393220
  95.4 1.8 %copy-start.11 = (bf16[256,256]{1,0:T(8,128)(2,1)S(1)}, bf16[256,256]{1,0:T(8,128)(2,1)}, u32[]{:S(2)}) copy-start(bf16[256,256]{1,0:T(8,128)(2,1)} %param.17) | copy-start | bytes 393220
  98.5 2.4 %copy-start.6 = (bf16[256,256]{1,0:T(8,128)(2,1)S(1)}, bf16[256,256]{1,0:T(8,128)(2,1)}, u32[]{:S(2)}) copy-start(bf16[256,256]{1,0:T(8,128)(2,1)} %param.15) | copy-start | bytes 393220
  99.0 2.3 %copy-start.7 = (bf16[256,256]{1,0:T(8,128)(2,1)S(1)}, bf16[256,256]{1,0:T(8,128)(2,1)}, u32[]{:S(2)}) copy-start(bf16[256,256]{1,0:T(8,128)(2,1)} %param.16) | copy-start | bytes 393220
  99.0 2.3 %copy-start.12 = (f32[256]{0:T(256)S(1)}, f32[256]{0:T(256)}, u32[]{:S(2)}) copy-start(f32[256]{0:T(256)} %param.13) | copy-start | bytes 3076
  100.4 2.5 %copy-start.1 = (bf16[4,64,256]{2,1,0:T(8,128)(2,1)S(1)}, bf16[4,64,256]{2,1,0:T(8,128)(2,1)}, u32[]{:S(2)}) copy-start(bf16[4,64,256]{2,1,0:T(8,128)(2,1)} %param.10) | copy-start | bytes 393220
  101.3 2.6 %copy-start.5 = (f32[256,256]{1,0:T(8,128)S(1)}, f32[256,256]{1,0:T(8,128)}, u32[]{:S(2)}) copy-start(f32[256,256]{1,0:T(8,128)} %fusion.31) | copy-start | bytes 786436
  148.9 1.8 %copy-start.14 = (bf16[128,8]{0,1:T(8,128)(2,1)S(1)}, bf16[128,8]{0,1:T(8,128)(2,1)}, u32[]{:S(2)}) copy-start(bf16[128,8]{0,1:T(8,128)(2,1)} %param.19) | copy-start | bytes 6148

commit v3 on v2

v3 whole, which is shorter than its diff:
```python
import functools
import math

import jax
import jax.numpy as jnp
from jax import lax
from jax.experimental import pallas as pl
from jax.experimental.pallas import tpu as pltpu
from jax.sharding import PartitionSpec as P

MESH = pl.DeviceIdType.MESH
F32 = jnp.float32
BF16 = jnp.bfloat16
VM = pl.BlockSpec(memory_space=pltpu.VMEM)


class Place:
    def __init__(self):
        seq = lax.axis_index("seq")
        res = lax.axis_index("res")
        self.seq, self.res = seq, res
        self.z_lo, self.core = seq // 2, seq % 2
        self.g, self.z_hi = res // 4, res % 2
        self.x_hi = self.g % 2
        x_lo = (res // 2) % 2
        self.h = ((x_lo + self.x_hi) % 2) * 4 + self.z_hi * 2 + self.z_lo

    def spot(self, h):
        return h % 2, ((h // 4 + self.x_hi) % 2) * 2 + (h // 2) % 2

    def member(self, h):
        z_lo, r4 = self.spot(h)
        return (z_lo * 2 + self.core, self.g * 4 + r4)

    def block(self, g):
        return (self.seq, g * 4 + ((self.h // 4 + g % 2) % 2) * 2 + self.z_hi)

    def partner(self):
        return (self.z_lo * 2 + 1 - self.core, self.res)


def enter(devices):
    barrier = pltpu.get_barrier_semaphore()
    for device in devices:
        pl.semaphore_signal(barrier, inc=1, device_id=device, device_id_type=MESH)
    pl.semaphore_wait(barrier, len(devices))


def remote(src, dst, send, recv, device):
    return pltpu.make_async_remote_copy(
        src_ref=src, dst_ref=dst, send_sem=send, recv_sem=recv, device_id=device, device_id_type=MESH
    )


def params(collective_id):
    return pltpu.CompilerParams(
        collective_id=collective_id, has_side_effects=True, vmem_limit_bytes=48 * 1024 * 1024
    )


def aligned(x, n):
    return pl.multiple_of(x * n, n)


ORDER = (4, 3, 5, 2, 6, 1, 7)
CHUNKS = 4
QB = 128


ORDER = (4, 3, 5, 2, 6, 1, 7)
CHUNKS = 4
QB = 128


def row_backward(xt, kv, bias, db, dkv, row):
    scale = 1.0 / math.sqrt(32)
    kt = kv[row, 0:32, :]
    vt = kv[row, 32:64, :]
    tn = (((0,), (0,)), ((), ()))
    nt = (((1,), (1,)), ((), ()))
    dk = jnp.zeros((32, 2048), F32)
    dv = jnp.zeros((32, 2048), F32)
    outs = []
    for n in range(256 // QB):
        q = pl.ds(n * QB, QB)
        qt = xt[row, 0:32, q]
        dot = xt[row, 96:128, q]
        s = lax.dot_general(qt, kt, tn, preferred_element_type=F32) * scale
        s = s + bias[q, :].astype(F32)
        e = jnp.exp(s - jnp.max(s, axis=1, keepdims=True))
        soft = e * (1.0 / jnp.sum(e, axis=1, keepdims=True))
        half = soft.astype(BF16)
        gs = lax.dot_general(dot, vt, tn, preferred_element_type=F32)
        gs = soft * (gs - jnp.sum(soft * gs, axis=1, keepdims=True))
        gh = gs.astype(BF16)
        db[q, :] += gs
        att = lax.dot_general(vt, half, nt, preferred_element_type=F32)
        dq = lax.dot_general(kt, gh, nt, preferred_element_type=F32) * scale
        outs.append(jnp.concatenate([att, dq.astype(BF16).astype(F32)], axis=0))
        dk = dk + jnp.dot(qt, gh, preferred_element_type=F32)
        dv = dv + jnp.dot(dot, half, preferred_element_type=F32)
    dkv[row, 0:32, :] = (dk * scale).astype(dkv.dtype)
    dkv[row, 32:64, :] = dv.astype(dkv.dtype)
    return jnp.concatenate(outs, axis=1)


TN = (((0,), (0,)), ((), ()))
NT = (((1,), (1,)), ((), ()))


def mm(a, b, dims=(((1,), (0,)), ((), ()))):
    return lax.dot_general(a, b, dims, preferred_element_type=F32)


def halves(a):
    hi = a.astype(BF16)
    return hi, (a - hi.astype(F32)).astype(BF16)


class Fan:
    def __init__(self, p, send, recv):
        self.p, self.send, self.recv = p, send, recv

    def members(self, stage, src, dst):
        return self.all(stage, src, dst, self.p.h, self.p.member)

    def blocks(self, stage, src, dst):
        return self.all(stage, src, dst, self.p.g, self.p.block)

    def all(self, stage, src, dst, me, device):
        copies = []
        for k in ORDER:
            n = (me + k) % 8
            c = remote(src(n), dst(k), self.send.at[stage, k - 1], self.recv.at[stage, k - 1], device(n))
            c.start()
            copies.append(c)
        return copies

    def partner(self, stage, src, dst):
        c = remote(src, dst, self.send.at[stage, 0], self.recv.at[stage, 0], self.p.partner())
        c.start()
        return [c]


def finish(copies):
    for c in copies:
        c.wait()


class Reduce:
    def __init__(self, p, w, o, bufs, sems):
        self.p, self.w, self.o = p, w, o
        self.b0, self.a0, self.b1, self.a1, self.b2 = bufs
        self.fan = Fan(p, *sems)
        rows = w.shape[1]
        self.n1, self.n2 = rows // 8, rows // 64
        self.lanes = pl.ds(aligned(p.core, 128), 128)
        self.copies = []

    def pair(self):
        self.copies = self.fan.partner(0, self.w.at[1 - self.p.core], self.b0)

    def member(self):
        finish(self.copies)
        self.a0[...] = self.w[self.p.core] + self.b0[...]
        n = self.n1
        self.copies = self.fan.members(
            1, lambda h: self.a0.at[pl.ds(aligned(h, n), n)], lambda k: self.b1.at[k - 1]
        )

    def block(self):
        finish(self.copies)
        total = self.a0[pl.ds(aligned(self.p.h, self.n1), self.n1)]
        for k in range(7):
            total = total + self.b1[k]
        self.a1[...] = total
        n = self.n2
        self.copies = self.fan.blocks(
            2, lambda g: self.a1.at[pl.ds(aligned(g, n), n)], lambda k: self.b2.at[k - 1]
        )

    def back_block(self):
        finish(self.copies)
        n = self.n2
        total = self.a1[pl.ds(aligned(self.p.g, n), n)]
        for k in range(7):
            total = total + self.b2[k]
        rows = pl.ds(pl.multiple_of(self.p.h * self.n1 + self.p.g * n, n), n)
        self.o[rows, self.lanes] = total
        piece = self.o.at[rows, self.lanes]
        self.copies = self.fan.blocks(3, lambda g: piece, lambda k: piece)

    def back_member(self):
        finish(self.copies)
        piece = self.o.at[pl.ds(aligned(self.p.h, self.n1), self.n1), self.lanes]
        self.copies = self.fan.members(4, lambda h: piece, lambda k: piece)

    def back_pair(self):
        finish(self.copies)
        piece = self.o.at[:, self.lanes]
        self.copies = self.fan.partner(5, piece, piece)

    def done(self):
        finish(self.copies)
        self.copies = []


def main_kernel(
    hom, slope, gain, wq, wk, wv, wg, wo, pbt, pair_hbm,
    align, bo, oa, ob, ex_out,
    sc, sm,
):
    p = Place()
    z_lo, r4 = p.spot(p.h)
    toks = pl.ds(aligned(r4, 64), 64)
    here = pl.ds(aligned(p.g, 256), 256)
    cols = pl.ds(aligned(p.seq, 512), 512)
    per = 8 // CHUNKS
    xr, xt, kv, bias, db, dkv, parts = (sc[n] for n in ("xr", "xt", "kv", "bias", "db", "dkv", "parts"))
    rows_buf, local = sc["rows"], sm["local"]

    def stream(n):
        return pltpu.make_async_copy(pair_hbm.at[pl.ds(n * 16, 16)], rows_buf.at[n % 2], sm["hbm"].at[n % 2])

    stream(0).start()
    stream(1).start()

    x = jnp.transpose(hom[...].astype(F32))
    centered = x - jnp.mean(x, axis=0, keepdims=True)
    inv = lax.rsqrt(jnp.mean(centered * centered, axis=0, keepdims=True) + 1e-05)
    hat = centered * inv
    scale_t = jnp.transpose(jnp.broadcast_to(gain[...], (256, 256)))
    normed = (hat * scale_t).astype(BF16)
    sc["hat"][...] = hat
    sc["scale"][...] = scale_t
    sc["inv"][...] = jnp.broadcast_to(inv, (8, 256))
    sc["normed"][...] = normed
    t_ref = sc["t"]
    for n, w in enumerate((wq, wk, wv)):
        t_ref[:, n * 32 : n * 32 + 32, :] = mm(w[...], normed, TN).astype(BF16).reshape(8, 32, 256)
    gate = jax.nn.sigmoid(mm(wg[...], normed, TN))
    grad_gated = mm(wo[...], slope[...], NT)
    sc["gate"][...] = gate
    sc["gg"][...] = grad_gated
    t_ref[:, 96:128, :] = (grad_gated * gate).astype(BF16).reshape(8, 32, 256)

    enter(
        [p.member((p.h + k) % 8) for k in range(1, 8)]
        + [p.block((p.g + k) % 8) for k in range(1, 8)]
        + [p.partner()]
    )
    fan = Fan(p, sm["send"], sm["recv"])

    moved = fan.members(0, lambda h: t_ref.at[h], lambda k: xr.at[z_lo, r4])
    own_t = pltpu.make_async_copy(t_ref.at[p.h], xr.at[z_lo, r4], local.at[0])
    own_t.start()

    b_ref = sc["b"]
    for n in range(4):
        stream(n).wait()
        flat = rows_buf[n % 2].reshape(16 * 512, 128)
        out = mm(pbt[...], flat, NT)
        out = jnp.stack([out[:, i * 512 : (i + 1) * 512] for i in range(16)], axis=1)
        b_ref[:, n * 16 : (n + 1) * 16, :] = out.astype(BF16)
        if n + 2 < 4:
            stream(n + 2).start()
    biases = fan.members(1, lambda h: b_ref.at[h], lambda k: bias.at[toks, cols])
    own_b = pltpu.make_async_copy(b_ref.at[p.h], bias.at[toks, cols], local.at[1])
    own_b.start()

    own_t.wait()
    finish(moved)
    for z in range(2):
        for pp in range(2):
            for i in range(2):
                lane = pp * 128 + i * 64
                xt[z * 4 + pp * 2 + i] = jnp.concatenate(
                    [xr[z, r, :, lane : lane + 64] for r in range(4)], axis=1
                )

    def keys(c, k):
        rows = pl.ds(c * per, per)
        return remote(
            xt.at[rows, 32:96], kv.at[rows, :, here], sm["ks"].at[c, k - 1], sm["kr"].at[c, k - 1],
            p.block((p.g + k) % 8),
        )

    def partial(c, k):
        rows = pl.ds(c * per, per)
        g = (p.g + k) % 8
        return remote(
            dkv.at[rows, :, pl.ds(aligned(g, 256), 256)],
            parts.at[k - 1, rows],
            sm["es"].at[c, k - 1],
            sm["er"].at[c, k - 1],
            p.block(g),
        )

    for c in range(CHUNKS):
        for k in ORDER:
            keys(c, k).start()
    own_k = pltpu.make_async_copy(xt.at[:, 32:96], kv.at[:, :, here], local.at[2])
    own_k.start()
    db[...] = jnp.zeros_like(db)
    own_b.wait()
    own_k.wait()
    finish(biases)
    moved = []
    for b in range(2):
        part = bias.at[:, pl.ds(aligned(b * 2 + p.core, 512), 512)]
        moved += fan.partner(2 + b, part, part)
    finish(moved)

    ya, yd = sc["ya"], sc["yd"]

    def by_member(outs, dst, c):
        for r in range(4):
            lane = slice(r * 64, r * 64 + 64)
            dst[c, r] = jnp.concatenate([outs[0][:, lane], outs[1][:, lane]], axis=1)

    def step(c, carry):
        for k in ORDER:
            keys(c, k).wait_recv()
        outs = []
        for i in range(per):
            outs.append(row_backward(xt, kv, bias, db, dkv, c * per + i))
        for k in ORDER:
            partial(c, k).start()
        by_member(outs, ya, c)
        return carry

    lax.fori_loop(0, CHUNKS, step, 0)

    stream(0).start()
    stream(1).start()
    other, mine, ta, td = sc["other"], sc["mine"], sc["ta"], sc["td"]
    pair = []
    for b in range(2):
        pair += fan.partner(4 + b, db.at[:, pl.ds(aligned(b * 2 + 1 - p.core, 512), 512)], other.at[b])

    def give(stage, src, dst):
        def of(h):
            z, r = p.spot(h)
            return src.at[pl.ds(z * 2, 2), r]

        return fan.members(stage, of, lambda k: dst.at[p.h])

    back = give(6, ya, ta)
    own_a = pltpu.make_async_copy(ya.at[pl.ds(z_lo * 2, 2), r4], ta.at[p.h], local.at[0])
    own_a.start()
    for b in range(2):
        pair[b].wait()
        mine[b] = (db[:, pl.ds(aligned(b * 2 + p.core, 512), 512)] + other[b]).astype(BF16)

    def bias_of(h):
        z, r = p.spot(h)
        return mine.at[z, pl.ds(aligned(r, 64), 64)]

    bias_back = fan.members(7, bias_of, lambda k: bo.at[p.h])
    own_m = pltpu.make_async_copy(bias_of(p.h), bo.at[p.h], local.at[1])
    own_m.start()

    def assemble(src, part):
        rows = slice(part * 32, part * 32 + 32)
        return jnp.concatenate([src[:, pp, rows, :].reshape(256, 128) for pp in range(2)], axis=1)

    own_a.wait()
    finish(back)
    attended = assemble(ta, 0)
    dq = assemble(ta, 1).astype(BF16)
    gate = sc["gate"][...]
    gated = (gate * attended).astype(BF16)
    grad_gate = (sc["gg"][...] * attended * gate * (1.0 - gate)).astype(BF16)
    sc["dq"][...] = dq
    sc["dg"][...] = grad_gate
    normed = sc["normed"][...]
    wa, wb = sc["wa"], sc["wb"]

    def put(dst, n, value):
        for i in range(2):
            dst[i, n * 256 : n * 256 + 256, :] = value[:, i * 128 : i * 128 + 128]

    put(wa, 0, mm(normed, dq, NT))
    put(wa, 1, mm(normed, grad_gate, NT))
    put(wa, 2, mm(gated, slope[...]))
    wa[:, 768:1024, :] = jnp.zeros((2, 256, 128), F32)
    first = Reduce(p, wa, oa, [sc[n] for n in ("a_b0", "a_a0", "a_b1", "a_a1", "a_b2")], (sm["as"], sm["ar"]))
    last = Reduce(p, wb, ob, [sc[n] for n in ("b_b0", "b_a0", "b_b1", "b_a1", "b_b2")], (sm["bs"], sm["br"]))
    first.pair()

    own_m.wait()
    finish(bias_back)
    grad_bias = jnp.zeros((8, 128), F32)
    for n in range(4):
        stream(n).wait()
        part = bo[:, n * 16 : (n + 1) * 16, :].astype(F32)
        for i in range(16):
            grad_bias = grad_bias + mm(part[:, i, :].astype(BF16), rows_buf[n % 2, i])
        if n + 2 < 4:
            stream(n + 2).start()
        if n == 0:
            first.member()
    first.block()

    def total(c, carry):
        for k in ORDER:
            partial(c, k).wait_recv()
        outs = []
        for i in range(per):
            row = c * per + i
            t = dkv[row, :, here].astype(F32)
            for k in range(7):
                t = t + parts[k, row].astype(F32)
            outs.append(t)
        by_member(outs, yd, c)
        return carry

    lax.fori_loop(0, CHUNKS, total, 0)
    back = give(8, yd, td)
    own_d = pltpu.make_async_copy(yd.at[pl.ds(z_lo * 2, 2), r4], td.at[p.h], local.at[0])
    own_d.start()
    first.back_block()
    grad_normed = mm(wq[...], sc["dq"][...]) + mm(wg[...], sc["dg"][...])
    own_d.wait()
    finish(back)
    first.back_member()

    dk_hi, dk_lo = halves(assemble(td, 0))
    dv_hi, dv_lo = halves(assemble(td, 1))
    normed = sc["normed"][...]
    put(wb, 0, mm(normed, dk_hi, NT) + mm(normed, dk_lo, NT))
    put(wb, 1, mm(normed, dv_hi, NT) + mm(normed, dv_lo, NT))
    last.pair()
    grad_normed = grad_normed + mm(wk[...], dk_hi) + mm(wk[...], dk_lo) + mm(wv[...], dv_hi) + mm(wv[...], dv_lo)
    hat = sc["hat"][...]
    by_gain = jnp.sum(jnp.transpose(grad_normed * hat), axis=0, keepdims=True)
    ex, ex_own, exm, exb = sc["ex"], sc["ex_own"], sc["exm"], sc["exb"]
    ex[0:8, :] = grad_bias
    ex[8:16, :] = jnp.concatenate([by_gain[:, :128], by_gain[:, 128:], jnp.zeros((6, 128), F32)], axis=0)
    extra = fan.partner(9, ex, ex_own)
    last.member()
    finish(extra)
    exm[p.h] = ex[...] + ex_own[...]
    extra = fan.members(10, lambda h: exm.at[p.h], lambda k: exm.at[p.h])

    scaled = grad_normed * sc["scale"][...]
    m1 = jnp.mean(scaled, axis=0, keepdims=True)
    m2 = jnp.mean(scaled * hat, axis=0, keepdims=True)
    align[...] = jnp.transpose(sc["inv"][0:1, :] * (scaled - m1 - hat * m2)).astype(BF16)

    last.block()
    finish(extra)
    exb[p.g] = sum_of(exm)
    extra = fan.blocks(11, lambda g: exb.at[p.g], lambda k: exb.at[p.g])
    first.back_pair()
    last.back_block()
    finish(extra)
    ex_out[...] = sum_of(exb)
    last.back_member()
    last.back_pair()
    first.done()
    last.done()

    def drain(c, carry):
        for k in ORDER:
            keys(c, k).wait_send()
            partial(c, k).wait_send()
        return carry

    lax.fori_loop(0, CHUNKS, drain, 0)


def sum_of(ref):
    total = ref[0]
    for n in range(1, 8):
        total = total + ref[n]
    return total


def main(hom, slope, gain, wq, wk, wv, wg, wo, pbt, pair_rows):
    dma = pltpu.SemaphoreType.DMA
    vmem = pltpu.VMEM

    def reduce_bufs(name, rows):
        return {
            name + "_b0": vmem((rows, 128), F32),
            name + "_a0": vmem((rows, 128), F32),
            name + "_b1": vmem((7, rows // 8, 128), F32),
            name + "_a1": vmem((rows // 8, 128), F32),
            name + "_b2": vmem((7, rows // 64, 128), F32),
        }

    square = vmem((256, 256), F32)
    square_half = vmem((256, 256), BF16)
    scratch = {
        "rows": vmem((2, 16, 512, 128), BF16),
        "hat": square, "scale": square, "inv": vmem((8, 256), F32), "gate": square, "gg": square,
        "normed": square_half, "dq": square_half, "dg": square_half,
        "t": vmem((8, 128, 256), BF16),
        "b": vmem((8, 64, 512), BF16),
        "xr": vmem((2, 4, 128, 256), BF16),
        "xt": vmem((8, 128, 256), BF16),
        "kv": vmem((8, 64, 2048), BF16),
        "bias": vmem((256, 2048), BF16),
        "db": vmem((256, 2048), F32),
        "dkv": vmem((8, 64, 2048), BF16),
        "parts": vmem((7, 8, 64, 256), BF16),
        "ya": vmem((4, 4, 64, 128), F32),
        "yd": vmem((4, 4, 64, 128), F32),
        "ta": vmem((8, 2, 64, 128), F32),
        "td": vmem((8, 2, 64, 128), F32),
        "mine": vmem((2, 256, 512), BF16),
        "other": vmem((2, 256, 512), F32),
        "wa": vmem((2, 1024, 128), F32),
        "wb": vmem((2, 512, 128), F32),
        "ex": vmem((16, 128), F32), "ex_own": vmem((16, 128), F32),
        "exm": vmem((8, 16, 128), F32), "exb": vmem((8, 16, 128), F32),
        **reduce_bufs("a", 1024),
        **reduce_bufs("b", 512),
    }
    sems = {
        "hbm": dma((2,)), "local": dma((3,)),
        "send": dma((12, 7)), "recv": dma((12, 7)),
        "ks": dma((CHUNKS, 7)), "kr": dma((CHUNKS, 7)),
        "es": dma((CHUNKS, 7)), "er": dma((CHUNKS, 7)),
        "as": dma((6, 7)), "ar": dma((6, 7)),
        "bs": dma((6, 7)), "br": dma((6, 7)),
    }
    return pl.pallas_call(
        main_kernel,
        out_shape=(
            jax.ShapeDtypeStruct((256, 256), BF16),
            jax.ShapeDtypeStruct((8, 64, 512), BF16),
            jax.ShapeDtypeStruct((1024, 256), F32),
            jax.ShapeDtypeStruct((512, 256), F32),
            jax.ShapeDtypeStruct((16, 128), F32),
        ),
        in_specs=[VM] * 9 + [pl.BlockSpec(memory_space=pl.ANY)],
        out_specs=(VM,) * 5,
        scratch_shapes=[scratch, sems],
        compiler_params=params(0),
        name="main",
    )(hom, slope, gain, wq, wk, wv, wg, wo, pbt, pair_rows)


def body(
    homolog_embedding,
    pair_input_rows,
    incoming_slope,
    rescale_factor,
    probe_weights,
    lookup_weights,
    content_weights,
    sigmoid_weights,
    final_projection,
    pair_bias_matrix,
):
    rows, toks, width = homolog_embedding.shape
    align, db_own, oa, ob, extra = main(
        homolog_embedding.reshape(-1, width),
        incoming_slope.reshape(-1, width),
        rescale_factor.reshape(1, width),
        probe_weights,
        lookup_weights,
        content_weights,
        sigmoid_weights,
        final_projection,
        pair_bias_matrix.T,
        pair_input_rows,
    )
    pair_grad = jnp.einsum(
        "hij,ch->ijc", db_own, pair_bias_matrix, preferred_element_type=F32
    ).astype(BF16)
    return (
        align.reshape(rows, toks, width),
        pair_grad,
        extra[8:10].reshape(width),
        oa[0:256],
        ob[0:256],
        ob[256:512],
        oa[256:512],
        oa[512:768],
        extra[0:8].T,
    )


def solution(mesh):
    in_specs = (
        P("seq", "res", None),
        P("res", "seq", None),
        P("seq", "res", None),
        P(),
        P(),
        P(),
        P(),
        P(),
        P(),
        P(),
    )
    out_specs = (P("seq", "res", None), P("res", "seq", None), P(), P(), P(), P(), P(), P(), P())
    return jax.shard_map(body, mesh=mesh, in_specs=in_specs, out_specs=out_specs, check_vma=False)
```

time: 158 us -> 127 us (0.80)
  matrix products: 25.2 us -> 5.51 us
  other arithmetic: 6.11 us -> 0 us
  Pallas kernels: 113 us -> 109 us
    dot_general x16 -> x0, matrix products: 19.7 us -> none  [the longest x10 6.36 us: dot(): return jnp.dot(a, b, preferred_element_type=F32)]
    unnamed x31 -> x19, local copies, waits for them, and re-layouts: 1.71 us -> 8.33 us
    pallas_call x3 -> x1, Pallas kernels: 113 us -> 109 us  [main(): pl.pallas_call(main_kernel, out_shape=(jax.ShapeDtypeStruct((256, 256), B...]
    concatenate x1 -> x0, local copies, waits for them, and re-layouts: 3.12 us -> none  [body(): jnp.concatenate([part_query, part_key, part_value, part_gate, part_out, p...]
    another operation x9 -> x0, local copies, waits for them, and re-layouts: 2.73 us -> none  [the longest x5 1.79 us: body(): dk, dv = tokenwise(back_kv)]
    reduce_sum x3 -> x0, other arithmetic: 2.32 us -> none  [the longest x1 1.09 us: body(): jnp.mean(centered * centered, axis=-1, keepdims=True) + 1e-05]
    convert_element_type x3 -> x0, other arithmetic: 1.96 us -> none  [the longest x1 1.04 us: body(): plain = (hat * rescale_factor).astype(BF16).reshape(-1, width)]
where the time goes in v3:
time: 127 us; the launch traced here: 126 us
  Pallas kernels  109 us (86%)
  local copies, waits for them, and re-layouts  10.6 us (8%)
  matrix products  5.51 us (4%)
    pallas_call x1, Pallas kernels, main(): pl.pallas_call(main_kernel, out_shape=(jax.ShapeDtypeStruct((256, 256), B...  109 us
    unnamed x19, local copies, waits for them, and re-layouts  8.33 us
    dot_general x1, matrix products, body(): jnp.einsum('hij,ch->ijc', db_own, pair_bias_matrix, preferred_element_typ...  5.51 us

profile of v3, /device:TPU:0, one launch (start us, length us, event | category | flops | bytes accessed | tf_op | source)
XLA Modules:
  0.0 125.6 jit_solution(12077729210093555807)
XLA Ops:
  0.6 0.0 copy-start
  0.7 0.9 copy-done
  1.6 0.0 copy-start.1
  1.6 0.9 copy-done.1
  2.5 0.0 copy-start.2
  2.5 0.9 copy-done.2
  3.4 0.0 copy-start.3
  3.4 0.9 copy-done.3
  4.3 0.0 copy-start.4
  4.3 0.9 copy-done.4
  5.2 0.0 copy-start.5
  5.2 0.9 copy-done.5
  6.1 0.0 copy-start.6
  6.1 0.9 copy-done.6
  7.0 0.0 copy-start.7
  7.0 0.7 copy-done.7
  7.7 0.0 copy-start.8
  7.7 0.7 copy-done.8
  8.3 108.9 %main.1 = (bf16[256,256]{1,0:T(8,128)(2,1)S(1)}, bf16[8,64,512]{2,1,0:T(8,128)(2,1)S(1)}, f32[1024,256]{1,0:T(8,128)S(1)}, f32[512,256]{1,0:T(8,128)S(1)}, f32[16,128]{1,0:T(8,128)S(1)}) custom-call(bf16[256,256]{1,0:T(8,128)(2,1)S(1)} %bitcast.12, bf16[256,256]{1,0:T(8,128)(2,1)S(1)} %bitcast.13, f32[1,256]{1,0:T(1,128)S(1)} %bitcast.16, ...), custom_call_target="tpu_custom_call" | custom-call | tf_op jit(solution)/shard_map/main/pallas_call | solution.py:529
  117.3 0.6 slice_bitcast_fusion.1
  117.8 0.6 slice_bitcast_fusion
  118.4 1.1 fusion.2
  119.5 5.5 %convolution_convert_fusion = bf16[64,512,128]{2,1,0:T(8,128)(2,1)} fusion(bf16[8,64,512]{2,1,0:T(8,128)(2,1)S(1)} %get-tuple-element.15, bf16[128,8]{0,1:T(8,128)(2,1)S(1)} %copy-done.7), kind=kOutput, calls=%fused_computation | convolution fusion | flops 71303168 | bytes 8914944 | tf_op jit(solution)/shard_map/hij,ch->ijc/dot_general | solution.py:571
  125.0 0.7 copy.23
Async XLA Ops:
  0.6 0.9 copy-start
  1.6 0.9 copy-start.1
  2.5 0.9 copy-start.2
  3.4 0.9 copy-start.3
  4.3 0.9 copy-start.4
  5.2 0.9 copy-start.5
  6.1 0.9 copy-start.6
  7.0 0.7 copy-start.7
  7.7 0.7 copy-start.8

commit v4 on v3

v4 whole, which is shorter than its diff:
```python
import functools
import math

import jax
import jax.numpy as jnp
from jax import lax
from jax.experimental import pallas as pl
from jax.experimental.pallas import tpu as pltpu
from jax.sharding import PartitionSpec as P

MESH = pl.DeviceIdType.MESH
F32 = jnp.float32
BF16 = jnp.bfloat16
VM = pl.BlockSpec(memory_space=pltpu.VMEM)
HB = pl.BlockSpec(memory_space=pltpu.HBM)


class Place:
    def __init__(self):
        seq = lax.axis_index("seq")
        res = lax.axis_index("res")
        self.seq, self.res = seq, res
        self.z_lo, self.core = seq // 2, seq % 2
        self.g, self.z_hi = res // 4, res % 2
        self.x_hi = self.g % 2
        x_lo = (res // 2) % 2
        self.h = ((x_lo + self.x_hi) % 2) * 4 + self.z_hi * 2 + self.z_lo

    def spot(self, h):
        return h % 2, ((h // 4 + self.x_hi) % 2) * 2 + (h // 2) % 2

    def member(self, h):
        z_lo, r4 = self.spot(h)
        return (z_lo * 2 + self.core, self.g * 4 + r4)

    def block(self, g):
        return (self.seq, g * 4 + ((self.h // 4 + g % 2) % 2) * 2 + self.z_hi)

    def partner(self):
        return (self.z_lo * 2 + 1 - self.core, self.res)


def greet(devices):
    barrier = pltpu.get_barrier_semaphore()
    for device in devices:
        pl.semaphore_signal(barrier, inc=1, device_id=device, device_id_type=MESH)


def remote(src, dst, send, recv, device):
    return pltpu.make_async_remote_copy(
        src_ref=src, dst_ref=dst, send_sem=send, recv_sem=recv, device_id=device, device_id_type=MESH
    )


def params(collective_id):
    return pltpu.CompilerParams(
        collective_id=collective_id, has_side_effects=True, vmem_limit_bytes=48 * 1024 * 1024
    )


def aligned(x, n):
    return pl.multiple_of(x * n, n)


ORDER = (4, 3, 5, 2, 6, 1, 7)
CHUNKS = 4
QB = 128


ORDER = (4, 3, 5, 2, 6, 1, 7)
CHUNKS = 4
QB = 128


def row_backward(xt, kv, bias, db, dkv, row):
    scale = 1.0 / math.sqrt(32)
    kt = kv[row, 0:32, :]
    vt = kv[row, 32:64, :]
    dk = jnp.zeros((32, 2048), F32)
    dv = jnp.zeros((32, 2048), F32)
    outs = []
    for n in range(256 // QB):
        q = pl.ds(n * QB, QB)
        qt = xt[row, 64:96, q]
        dot = xt[row, 96:128, q]
        s = mm(qt, kt, TN) * scale
        s = s + bias[q, :].astype(F32)
        e = jnp.exp(s - jnp.max(s, axis=1, keepdims=True))
        soft = e * (1.0 / jnp.sum(e, axis=1, keepdims=True))
        half = soft.astype(BF16)
        gs = mm(dot, vt, TN)
        gs = soft * (gs - jnp.sum(soft * gs, axis=1, keepdims=True))
        gh = gs.astype(BF16)
        db[q, :] += gs
        att = mm(vt, half, NT)
        dq = mm(kt, gh, NT) * scale
        outs.append(jnp.concatenate([att, dq.astype(BF16).astype(F32)], axis=0))
        dk = dk + mm(qt, gh)
        dv = dv + mm(dot, half)
    dkv[row, 0:32, :] = (dk * scale).astype(dkv.dtype)
    dkv[row, 32:64, :] = dv.astype(dkv.dtype)
    return jnp.concatenate(outs, axis=1)


TN = (((0,), (0,)), ((), ()))
NT = (((1,), (1,)), ((), ()))


def mm(a, b, dims=(((1,), (0,)), ((), ()))):
    return lax.dot_general(a, b, dims, preferred_element_type=F32)


def halves(a):
    hi = a.astype(BF16)
    return hi, (a - hi.astype(F32)).astype(BF16)


class Fan:
    def __init__(self, p, send, recv):
        self.p, self.send, self.recv = p, send, recv

    def members(self, stage, src, dst):
        return self.all(stage, src, dst, self.p.h, self.p.member)

    def blocks(self, stage, src, dst):
        return self.all(stage, src, dst, self.p.g, self.p.block)

    def all(self, stage, src, dst, me, device):
        copies = []
        for k in ORDER:
            n = (me + k) % 8
            c = remote(src(n), dst(k), self.send.at[stage, k - 1], self.recv.at[stage, k - 1], device(n))
            c.start()
            copies.append(c)
        return copies

    def partner(self, stage, src, dst):
        c = remote(src, dst, self.send.at[stage, 0], self.recv.at[stage, 0], self.p.partner())
        c.start()
        return [c]


def finish(copies):
    for c in copies:
        c.wait()


class Reduce:
    def __init__(self, p, w, o, bufs, sems):
        self.p, self.w, self.o = p, w, o
        self.b0, self.a0, self.b1, self.a1 = bufs
        self.fan = Fan(p, *sems)
        self.n = w.shape[1] // 8
        self.lanes = pl.ds(aligned(p.core, 128), 128)
        self.copies = []

    def rows(self, g):
        return pl.ds(aligned(g, self.n), self.n)

    def pair(self):
        self.copies = self.fan.partner(0, self.w.at[1 - self.p.core], self.b0)

    def block(self):
        finish(self.copies)
        self.a0[...] = self.w[self.p.core] + self.b0[...]
        self.copies = self.fan.blocks(1, lambda g: self.a0.at[self.rows(g)], lambda k: self.b1.at[k - 1])

    def member(self):
        finish(self.copies)
        total = self.a0[self.rows(self.p.g)]
        for k in range(7):
            total = total + self.b1[k]
        self.a1[self.p.h] = total
        piece = self.a1.at[self.p.h]
        self.copies = self.fan.members(2, lambda h: piece, lambda k: piece)

    def back_block(self):
        finish(self.copies)
        self.o[self.rows(self.p.g), self.lanes] = sum_of(self.a1)
        piece = self.o.at[self.rows(self.p.g), self.lanes]
        self.copies = self.fan.blocks(3, lambda g: piece, lambda k: piece)

    def back_pair(self):
        finish(self.copies)
        piece = self.o.at[:, self.lanes]
        self.copies = self.fan.partner(4, piece, piece)

    def done(self):
        finish(self.copies)
        self.copies = []


def only(value, n, i):
    row = lax.broadcasted_iota(jnp.int32, value.shape, 0) % n
    return jnp.where(row == i, value, jnp.zeros_like(value))


def spread(pbt):
    return jnp.broadcast_to(pbt.astype(F32)[:, None, :], (8, 16, 128)).reshape(128, 128)


def main_kernel(
    hom_in, slope_in, gain_in, wq_in, wk_in, wv_in, wg_in, wo_in, pbt_in, pair_hbm,
    align, bo, oa, ob, ex_out,
    sc, sm,
):
    p = Place()
    z_lo, r4 = p.spot(p.h)
    toks = pl.ds(aligned(r4, 64), 64)
    here = pl.ds(aligned(p.g, 256), 256)
    cols = pl.ds(aligned(p.seq, 512), 512)
    per = 8 // CHUNKS
    xr, xt, kv, bias, db, dkv, parts = (sc[n] for n in ("xr", "xt", "kv", "bias", "db", "dkv", "parts"))
    rows_buf, local = sc["rows"], sm["local"]

    greet(
        [p.member((p.h + k) % 8) for k in range(1, 8)]
        + [p.block((p.g + k) % 8) for k in range(1, 8)]
        + [p.partner()]
    )
    loads = {}
    names = ("hom", "gain", "wk", "wv", "slope", "wo", "wg", "wq", "pbt")
    for n, (name, src) in enumerate(
        zip(names, (hom_in, gain_in, wk_in, wv_in, slope_in, wo_in, wg_in, wq_in, pbt_in))
    ):
        loads[name] = pltpu.make_async_copy(src, sc[name], sm["in"].at[n])
        loads[name].start()

    def stream(n):
        return pltpu.make_async_copy(pair_hbm.at[pl.ds(n * 16, 16)], rows_buf.at[n % 2], sm["hbm"].at[n % 2])

    stream(0).start()
    stream(1).start()
    hom, gain, wk, wv, slope, wo, wg, wq, pbt = (sc[n] for n in names)

    loads["hom"].wait()
    loads["gain"].wait()
    x = jnp.transpose(hom[...].astype(F32))
    centered = x - jnp.mean(x, axis=0, keepdims=True)
    inv = lax.rsqrt(jnp.mean(centered * centered, axis=0, keepdims=True) + 1e-05)
    hat = centered * inv
    scale_t = jnp.transpose(jnp.broadcast_to(gain[...], (256, 256)))
    normed = (hat * scale_t).astype(BF16)
    t_ref = sc["t"]
    loads["wk"].wait()
    loads["wv"].wait()
    for n, w in enumerate((wk, wv)):
        t_ref[:, n * 32 : n * 32 + 32, :] = mm(w[...], normed, TN).astype(BF16).reshape(8, 32, 256)
    pl.semaphore_wait(pltpu.get_barrier_semaphore(), 15)
    fan = Fan(p, sm["send"], sm["recv"])

    moved = fan.members(0, lambda h: t_ref.at[h, 0:64], lambda k: xr.at[z_lo, r4, 0:64])
    own_t = pltpu.make_async_copy(t_ref.at[p.h, 0:64], xr.at[z_lo, r4, 0:64], local.at[0])
    own_t.start()
    sc["hat"][...] = hat
    sc["scale"][...] = scale_t
    sc["inv"][...] = jnp.broadcast_to(inv, (8, 256))
    sc["normed"][...] = normed
    for name in ("slope", "wo", "wg", "wq", "pbt"):
        loads[name].wait()
    t_ref[:, 64:96, :] = mm(wq[...], normed, TN).astype(BF16).reshape(8, 32, 256)
    gate = jax.nn.sigmoid(mm(wg[...], normed, TN))
    grad_gated = mm(wo[...], slope[...], NT)
    sc["gate"][...] = gate
    sc["gg"][...] = grad_gated
    t_ref[:, 96:128, :] = (grad_gated * gate).astype(BF16).reshape(8, 32, 256)
    moved_q = fan.members(12, lambda h: t_ref.at[h, 64:128], lambda k: xr.at[z_lo, r4, 64:128])
    own_q = pltpu.make_async_copy(t_ref.at[p.h, 64:128], xr.at[z_lo, r4, 64:128], local.at[3])
    own_q.start()

    b_ref, mask = sc["b"], sc["mask"]
    base = spread(pbt[...])
    for i in range(16):
        mask[i] = only(base, 16, i).astype(BF16)
    for n in range(4):
        stream(n).wait()
        out = mm(mask[0], rows_buf[n % 2, 0], NT)
        for i in range(1, 16):
            out = out + mm(mask[i], rows_buf[n % 2, i], NT)
        b_ref[:, n * 16 : (n + 1) * 16, :] = out.astype(BF16).reshape(8, 16, 512)
        if n + 2 < 4:
            stream(n + 2).start()
    biases = fan.members(1, lambda h: b_ref.at[h], lambda k: bias.at[toks, cols])
    own_b = pltpu.make_async_copy(b_ref.at[p.h], bias.at[toks, cols], local.at[1])
    own_b.start()

    def by_row(lo):
        for z in range(2):
            for pp in range(2):
                for i in range(2):
                    lane = pp * 128 + i * 64
                    xt[z * 4 + pp * 2 + i, lo : lo + 64] = jnp.concatenate(
                        [xr[z, r, lo : lo + 64, lane : lane + 64] for r in range(4)], axis=1
                    )

    own_t.wait()
    finish(moved)
    by_row(0)

    def keys(c, k):
        rows = pl.ds(c * per, per)
        return remote(
            xt.at[rows, 0:64], kv.at[rows, :, here], sm["ks"].at[c, k - 1], sm["kr"].at[c, k - 1],
            p.block((p.g + k) % 8),
        )

    def partial(c, k):
        rows = pl.ds(c * per, per)
        g = (p.g + k) % 8
        return remote(
            dkv.at[rows, :, pl.ds(aligned(g, 256), 256)],
            parts.at[k - 1, rows],
            sm["es"].at[c, k - 1],
            sm["er"].at[c, k - 1],
            p.block(g),
        )

    for c in range(CHUNKS):
        for k in ORDER:
            keys(c, k).start()
    own_k = pltpu.make_async_copy(xt.at[:, 0:64], kv.at[:, :, here], local.at[2])
    own_k.start()
    db[...] = jnp.zeros_like(db)
    own_q.wait()
    finish(moved_q)
    by_row(64)
    own_k.wait()
    own_b.wait()
    finish(biases)
    moved = []
    for b in range(2):
        part = bias.at[:, pl.ds(aligned(b * 2 + p.core, 512), 512)]
        moved += fan.partner(2 + b, part, part)
    finish(moved)

    ya, yd = sc["ya"], sc["yd"]

    def by_member(outs, dst, c):
        for r in range(4):
            lane = slice(r * 64, r * 64 + 64)
            dst[c, r] = jnp.concatenate([outs[0][:, lane], outs[1][:, lane]], axis=1)

    ta, td, other, mine = sc["ta"], sc["td"], sc["other"], sc["mine"]

    def give(stage, src, dst, k, z):
        h = (p.h + k) % 8
        return remote(
            src.at[pl.ds(z * 2, 2), p.spot(h)[1]], dst.at[p.h],
            sm["send"].at[stage, k - 1], sm["recv"].at[stage, k - 1], p.member(h),
        )

    def keep(n, src, dst):
        return pltpu.make_async_copy(src.at[pl.ds(z_lo * 2, 2), r4], dst.at[p.h], local.at[n])

    def give_half(stage, n, src, dst, z):
        @pl.when(z_lo == z)
        def _():
            for k in (4, 2, 6):
                give(stage, src, dst, k, z).start()
            keep(n, src, dst).start()

        @pl.when(z_lo != z)
        def _():
            for k in (3, 5, 1, 7):
                give(stage, src, dst, k, z).start()

    def taken(stage, n, src, dst):
        keep(n, src, dst).wait()
        for k in ORDER:
            give(stage, src, dst, k, 0).wait()

    def step(c, carry):
        for k in ORDER:
            keys(c, k).wait_recv()
        outs = []
        for i in range(per):
            outs.append(row_backward(xt, kv, bias, db, dkv, c * per + i))
        for k in ORDER:
            partial(c, k).start()
        by_member(outs, ya, c)
        for z in range(2):

            @pl.when(c == 2 * z + 1)
            def _():
                give_half(6, 0, ya, ta, z)

        return carry

    lax.fori_loop(0, CHUNKS, step, 0)

    stream(0).start()
    stream(1).start()
    pair = []
    for b in range(2):
        pair += fan.partner(4 + b, db.at[:, pl.ds(aligned(b * 2 + 1 - p.core, 512), 512)], other.at[b])

    def total(c, carry):
        for k in ORDER:
            partial(c, k).wait_recv()
        outs = []
        for i in range(per):
            row = c * per + i
            t = dkv[row, :, here].astype(F32)
            for k in range(7):
                t = t + parts[k, row].astype(F32)
            outs.append(t)
        by_member(outs, yd, c)
        return carry

    lax.fori_loop(0, 2, total, 0)
    give_half(8, 2, yd, td, 0)
    for b in range(2):
        pair[b].wait()
        mine[b] = (db[:, pl.ds(aligned(b * 2 + p.core, 512), 512)] + other[b]).astype(BF16)

    def assemble(src, part):
        rows = slice(part * 32, part * 32 + 32)
        return jnp.concatenate([src[:, pp, rows, :].reshape(256, 128) for pp in range(2)], axis=1)

    taken(6, 0, ya, ta)
    attended = assemble(ta, 0)
    dq = assemble(ta, 1).astype(BF16)
    gate = sc["gate"][...]
    gated = (gate * attended).astype(BF16)
    grad_gate = (sc["gg"][...] * attended * gate * (1.0 - gate)).astype(BF16)
    sc["dq"][...] = dq
    sc["dg"][...] = grad_gate
    normed = sc["normed"][...]
    wa, wb = sc["wa"], sc["wb"]

    def put(dst, n, value):
        for i in range(2):
            dst[i, n * 256 : n * 256 + 256, :] = value[:, i * 128 : i * 128 + 128]

    put(wa, 0, mm(normed, dq, NT))
    put(wa, 1, mm(normed, grad_gate, NT))
    put(wa, 2, mm(gated, slope[...]))
    first = Reduce(p, wa, oa, [sc[n] for n in ("a_b0", "a_a0", "a_b1", "a_a1")], (sm["as"], sm["ar"]))
    last = Reduce(p, wb, ob, [sc[n] for n in ("b_b0", "b_a0", "b_b1", "b_a1")], (sm["bs"], sm["br"]))
    first.pair()
    lax.fori_loop(2, 4, total, 0)
    give_half(8, 2, yd, td, 1)

    def bias_of(h):
        z, r = p.spot(h)
        return mine.at[z, pl.ds(aligned(r, 64), 64)]

    bias_back = fan.members(7, bias_of, lambda k: bo.at[p.h])
    own_m = pltpu.make_async_copy(bias_of(p.h), bo.at[p.h], local.at[1])
    own_m.start()
    first.block()
    grad_normed = mm(wq[...], sc["dq"][...]) + mm(wg[...], sc["dg"][...])
    first.member()

    taken(8, 2, yd, td)
    dk_hi, dk_lo = halves(assemble(td, 0))
    dv_hi, dv_lo = halves(assemble(td, 1))
    normed = sc["normed"][...]
    put(wb, 0, mm(normed, dk_hi, NT) + mm(normed, dk_lo, NT))
    put(wb, 1, mm(normed, dv_hi, NT) + mm(normed, dv_lo, NT))
    last.pair()
    grad_normed = grad_normed + mm(wk[...], dk_hi) + mm(wk[...], dk_lo) + mm(wv[...], dv_hi) + mm(wv[...], dv_lo)
    hat = sc["hat"][...]
    by_gain = jnp.sum(jnp.transpose(grad_normed * hat), axis=0, keepdims=True)
    last.block()

    own_m.wait()
    finish(bias_back)
    grad_bias = jnp.zeros((128, 128), F32)
    for n in range(4):
        stream(n).wait()
        part = bo[:, n * 16 : (n + 1) * 16, :].reshape(128, 512)
        for i in range(16):
            grad_bias = grad_bias + mm(only(part, 16, i), rows_buf[n % 2, i])
        if n + 2 < 4:
            stream(n + 2).start()
    ex, ex_own, exm, exb = sc["ex"], sc["ex_own"], sc["exm"], sc["exb"]
    ex[0:8, :] = jnp.sum(grad_bias.reshape(8, 16, 128), axis=1)
    ex[8:16, :] = jnp.concatenate([by_gain[:, :128], by_gain[:, 128:], jnp.zeros((6, 128), F32)], axis=0)
    extra = fan.partner(9, ex, ex_own)
    last.member()
    first.back_block()
    finish(extra)
    exm[p.h] = ex[...] + ex_own[...]
    extra = fan.members(10, lambda h: exm.at[p.h], lambda k: exm.at[p.h])

    scaled = grad_normed * sc["scale"][...]
    m1 = jnp.mean(scaled, axis=0, keepdims=True)
    m2 = jnp.mean(scaled * hat, axis=0, keepdims=True)
    align[...] = jnp.transpose(sc["inv"][0:1, :] * (scaled - m1 - hat * m2)).astype(BF16)

    last.back_block()
    finish(extra)
    exb[p.g] = sum_of(exm)
    extra = fan.blocks(11, lambda g: exb.at[p.g], lambda k: exb.at[p.g])
    first.back_pair()
    last.back_pair()
    finish(extra)
    ex_out[...] = sum_of(exb)
    first.done()
    last.done()

    def drain(c, carry):
        for k in ORDER:
            keys(c, k).wait_send()
            partial(c, k).wait_send()
        return carry

    lax.fori_loop(0, CHUNKS, drain, 0)


def sum_of(ref):
    total = ref[0]
    for n in range(1, 8):
        total = total + ref[n]
    return total


def main(hom, slope, gain, wq, wk, wv, wg, wo, pbt, pair_rows):
    dma = pltpu.SemaphoreType.DMA
    vmem = pltpu.VMEM

    def reduce_bufs(name, rows):
        return {
            name + "_b0": vmem((rows, 128), F32),
            name + "_a0": vmem((rows, 128), F32),
            name + "_b1": vmem((7, rows // 8, 128), F32),
            name + "_a1": vmem((8, rows // 8, 128), F32),
        }

    square = vmem((256, 256), F32)
    square_half = vmem((256, 256), BF16)
    scratch = {
        "rows": vmem((2, 16, 512, 128), BF16),
        "mask": vmem((16, 128, 128), BF16),
        "hom": square_half, "slope": square_half, "gain": vmem((1, 256), F32), "pbt": vmem((8, 128), BF16),
        "wq": square_half, "wk": square_half, "wv": square_half, "wg": square_half, "wo": square_half,
        "hat": square, "scale": square, "inv": vmem((8, 256), F32), "gate": square, "gg": square,
        "normed": square_half, "dq": square_half, "dg": square_half,
        "t": vmem((8, 128, 256), BF16),
        "b": vmem((8, 64, 512), BF16),
        "xr": vmem((2, 4, 128, 256), BF16),
        "xt": vmem((8, 128, 256), BF16),
        "kv": vmem((8, 64, 2048), BF16),
        "bias": vmem((256, 2048), BF16),
        "db": vmem((256, 2048), F32),
        "dkv": vmem((8, 64, 2048), BF16),
        "parts": vmem((7, 8, 64, 256), BF16),
        "ya": vmem((4, 4, 64, 128), F32),
        "yd": vmem((4, 4, 64, 128), F32),
        "ta": vmem((8, 2, 64, 128), F32),
        "td": vmem((8, 2, 64, 128), F32),
        "mine": vmem((2, 256, 512), BF16),
        "other": vmem((2, 256, 512), F32),
        "wa": vmem((2, 768, 128), F32),
        "wb": vmem((2, 512, 128), F32),
        "ex": vmem((16, 128), F32), "ex_own": vmem((16, 128), F32),
        "exm": vmem((8, 16, 128), F32), "exb": vmem((8, 16, 128), F32),
        **reduce_bufs("a", 768),
        **reduce_bufs("b", 512),
    }
    sems = {
        "hbm": dma((2,)), "local": dma((4,)), "in": dma((9,)),
        "send": dma((13, 7)), "recv": dma((13, 7)),
        "ks": dma((CHUNKS, 7)), "kr": dma((CHUNKS, 7)),
        "es": dma((CHUNKS, 7)), "er": dma((CHUNKS, 7)),
        "as": dma((5, 7)), "ar": dma((5, 7)),
        "bs": dma((5, 7)), "br": dma((5, 7)),
    }
    return pl.pallas_call(
        main_kernel,
        out_shape=(
            jax.ShapeDtypeStruct((256, 256), BF16),
            jax.ShapeDtypeStruct((8, 64, 512), BF16),
            jax.ShapeDtypeStruct((768, 256), F32),
            jax.ShapeDtypeStruct((512, 256), F32),
            jax.ShapeDtypeStruct((16, 128), F32),
        ),
        in_specs=[HB] * 10,
        out_specs=(VM,) * 5,
        scratch_shapes=[scratch, sems],
        compiler_params=params(0),
        name="main",
    )(hom, slope, gain, wq, wk, wv, wg, wo, pbt, pair_rows)


def tail_kernel(bo, pbt, align, oa, ob, ex, pair, align_out, q, k, v, g, o, gain, bias, base, sem):
    n = pl.program_id(0)
    moves = [(align, align_out), (ex.at[8:10], gain), (ex.at[0:8], bias)]
    moves += [(oa.at[0:256], q), (oa.at[256:512], g), (oa.at[512:768], o), (ob.at[0:256], k), (ob.at[256:512], v)]
    copies = [pltpu.make_async_copy(a, b, sem.at[i]) for i, (a, b) in enumerate(moves)]

    @pl.when(n == 0)
    def _():
        for c in copies:
            c.start()
        spreaded = spread(pbt[...])
        for i in range(16):
            base[:, i * 128 : i * 128 + 128] = only(spreaded, 16, i).astype(BF16)

    part = jnp.transpose(bo[:, pl.ds(pl.multiple_of(n * 16, 16), 16), :].reshape(128, 512))
    for i in range(8):
        out = mm(part, base[:, i * 256 : i * 256 + 256]).astype(BF16)
        pair[2 * i] = out[:, :128]
        pair[2 * i + 1] = out[:, 128:]

    @pl.when(n == 3)
    def _():
        for c in copies:
            c.wait()


def tail(bo, pbt, align, oa, ob, ex):
    square = jax.ShapeDtypeStruct((256, 256), F32)
    return pl.pallas_call(
        tail_kernel,
        grid=(4,),
        out_shape=(
            jax.ShapeDtypeStruct((64, 512, 128), BF16),
            jax.ShapeDtypeStruct((256, 256), BF16),
            square, square, square, square, square,
            jax.ShapeDtypeStruct((2, 128), F32),
            jax.ShapeDtypeStruct((8, 128), F32),
        ),
        in_specs=[VM] * 6,
        out_specs=(pl.BlockSpec((16, 512, 128), lambda n: (n, 0, 0)),) + (HB,) * 8,
        scratch_shapes=[pltpu.VMEM((128, 2048), BF16), pltpu.SemaphoreType.DMA((8,))],
        compiler_params=pltpu.CompilerParams(vmem_limit_bytes=32 * 1024 * 1024),
        name="tail",
    )(bo, pbt, align, oa, ob, ex)


def body(
    homolog_embedding,
    pair_input_rows,
    incoming_slope,
    rescale_factor,
    probe_weights,
    lookup_weights,
    content_weights,
    sigmoid_weights,
    final_projection,
    pair_bias_matrix,
):
    rows, toks, width = homolog_embedding.shape
    align, db_own, oa, ob, extra = main(
        homolog_embedding.reshape(-1, width),
        incoming_slope.reshape(-1, width),
        rescale_factor.reshape(1, width),
        probe_weights,
        lookup_weights,
        content_weights,
        sigmoid_weights,
        final_projection,
        pair_bias_matrix.T,
        pair_input_rows,
    )
    pair_grad, align, grad_q, grad_k, grad_v, grad_g, grad_o, gain, bias = tail(
        db_own, pair_bias_matrix.T, align, oa, ob, extra
    )
    return (
        align.reshape(rows, toks, width),
        pair_grad,
        gain.reshape(width),
        grad_q,
        grad_k,
        grad_v,
        grad_g,
        grad_o,
        bias.T,
    )


def solution(mesh):
    in_specs = (
        P("seq", "res", None),
        P("res", "seq", None),
        P("seq", "res", None),
        P(),
        P(),
        P(),
        P(),
        P(),
        P(),
        P(),
    )
    out_specs = (P("seq", "res", None), P("res", "seq", None), P(), P(), P(), P(), P(), P(), P())
    return jax.shard_map(body, mesh=mesh, in_specs=in_specs, out_specs=out_specs, check_vma=False)
```

time: 127 us -> 113 us (0.89)
  Pallas kernels: 109 us -> 103 us
  matrix products: 5.51 us -> 0 us
  local copies, waits for them, and re-layouts: 10.6 us -> 7.68 us
    pallas_call x1, Pallas kernels: 109 us -> 97.7 us  [main(): pl.pallas_call(main_kernel, out_shape=(jax.ShapeDtypeStruct((256, 256), B...]
    dot_general x1 -> x0, matrix products: 5.51 us -> none  [body(): jnp.einsum('hij,ch->ijc', db_own, pair_bias_matrix, preferred_element_typ...]
    pallas_call x0 -> x1, Pallas kernels: none -> 5.07 us  [tail(): pl.pallas_call(tail_kernel, grid=(4,), out_shape=(jax.ShapeDtypeStruct((6...]
    unnamed x19 -> x18, local copies, waits for them, and re-layouts: 8.33 us -> 7.68 us
where the time goes in v4:
time: 113 us; the launch traced here: 111 us
  Pallas kernels  103 us (91%)
  local copies, waits for them, and re-layouts  7.68 us (7%)
    pallas_call x1, Pallas kernels, main(): pl.pallas_call(main_kernel, out_shape=(jax.ShapeDtypeStruct((256, 256), B...  97.7 us
    unnamed x18, local copies, waits for them, and re-layouts  7.68 us
    pallas_call x1, Pallas kernels, tail(): pl.pallas_call(tail_kernel, grid=(4,), out_shape=(jax.ShapeDtypeStruct((6...  5.07 us

profile of v4, /device:TPU:0, one launch (start us, length us, event | category | flops | bytes accessed | tf_op | source)
XLA Modules:
  0.0 111.3 jit_solution(16481951542014285554)
XLA Ops:
  0.6 0.0 copy-start
  0.7 0.9 copy-done
  1.6 0.0 copy-start.1
  1.6 0.9 copy-done.1
  2.5 0.0 copy-start.2
  2.5 0.9 copy-done.2
  3.4 0.0 copy-start.3
  3.4 0.9 copy-done.3
  4.3 0.0 copy-start.4
  4.3 0.9 copy-done.4
  5.2 0.0 copy-start.5
  5.2 0.9 copy-done.5
  6.1 0.0 copy-start.6
  6.1 0.9 copy-done.6
  7.0 0.0 copy-start.7
  7.0 0.7 copy-done.7
  7.7 0.0 copy-start.8
  7.7 0.7 copy-done.8
  8.3 97.7 %main.1 = (bf16[256,256]{1,0:T(8,128)(2,1)S(1)}, bf16[8,64,512]{2,1,0:T(8,128)(2,1)S(1)}, f32[768,256]{1,0:T(8,128)S(1)}, f32[512,256]{1,0:T(8,128)S(1)}, f32[16,128]{1,0:T(8,128)S(1)}) custom-call(bf16[256,256]{1,0:T(8,128)(2,1)S(1)} %bitcast.7, bf16[256,256]{1,0:T(8,128)(2,1)S(1)} %bitcast.8, f32[1,256]{1,0:T(1,128)S(1)} %bitcast.11, ...), custom_call_target="tpu_custom_call" | custom-call | tf_op jit(solution)/shard_map/main/pallas_call | solution.py:570
  106.1 5.1 %tail.1 = (bf16[64,512,128]{2,1,0:T(8,128)(2,1)}, bf16[256,256]{1,0:T(8,128)(2,1)}, f32[256,256]{1,0:T(8,128)}, f32[256,256]{1,0:T(8,128)}, f32[256,256]{1,0:T(8...) custom-call(bf16[8,64,512]{2,1,0:T(8,128)(2,1)S(1)} %get-tuple-element.23.bo, ...), custom_call_target="tpu_custom_call" | custom-call | tf_op jit(solution)/shard_map/tail/pallas_call | solution.py:615
Async XLA Ops:
  0.6 0.9 copy-start
  1.6 0.9 copy-start.1
  2.5 0.9 copy-start.2
  3.4 0.9 copy-start.3
  4.3 0.9 copy-start.4
  5.2 0.9 copy-start.5
  6.1 0.9 copy-start.6
  7.0 0.7 copy-start.7
  7.7 0.7 copy-start.8

commit v5 on v4

--- a/solution.py
+++ b/solution.py
@@ -154,31 +154,31 @@
         self.lanes = pl.ds(aligned(p.core, 128), 128)
         self.copies = []
 
-    def rows(self, g):
-        return pl.ds(aligned(g, self.n), self.n)
+    def rows(self, h):
+        return pl.ds(aligned(h, self.n), self.n)
 
     def pair(self):
         self.copies = self.fan.partner(0, self.w.at[1 - self.p.core], self.b0)
 
+    def member(self):
+        finish(self.copies)
+        self.a0[...] = self.w[self.p.core] + self.b0[...]
+        self.copies = self.fan.members(1, lambda h: self.a0.at[self.rows(h)], lambda k: self.b1.at[k - 1])
+
     def block(self):
         finish(self.copies)
-        self.a0[...] = self.w[self.p.core] + self.b0[...]
-        self.copies = self.fan.blocks(1, lambda g: self.a0.at[self.rows(g)], lambda k: self.b1.at[k - 1])
-
-    def member(self):
-        finish(self.copies)
-        total = self.a0[self.rows(self.p.g)]
+        total = self.a0[self.rows(self.p.h)]
         for k in range(7):
             total = total + self.b1[k]
-        self.a1[self.p.h] = total
-        piece = self.a1.at[self.p.h]
-        self.copies = self.fan.members(2, lambda h: piece, lambda k: piece)
-
-    def back_block(self):
+        self.a1[self.p.g] = total
+        piece = self.a1.at[self.p.g]
+        self.copies = self.fan.blocks(2, lambda g: piece, lambda k: piece)
+
+    def back_member(self):
         finish(self.copies)
-        self.o[self.rows(self.p.g), self.lanes] = sum_of(self.a1)
-        piece = self.o.at[self.rows(self.p.g), self.lanes]
-        self.copies = self.fan.blocks(3, lambda g: piece, lambda k: piece)
+        self.o[self.rows(self.p.h), self.lanes] = sum_of(self.a1)
+        piece = self.o.at[self.rows(self.p.h), self.lanes]
+        self.copies = self.fan.members(3, lambda h: piece, lambda k: piece)
 
     def back_pair(self):
         finish(self.copies)
@@ -283,6 +283,9 @@
     biases = fan.members(1, lambda h: b_ref.at[h], lambda k: bias.at[toks, cols])
     own_b = pltpu.make_async_copy(b_ref.at[p.h], bias.at[toks, cols], local.at[1])
     own_b.start()
+    normed_all = sc["xn"]
+    moved_n = fan.members(13, lambda h: sc["normed"], lambda k: normed_all.at[z_lo, r4])
+    own_n = pltpu.make_async_copy(sc["normed"], normed_all.at[z_lo, r4], local.at[3])
 
     def by_row(lo):
         for z in range(2):
@@ -322,6 +325,7 @@
     own_k.start()
     db[...] = jnp.zeros_like(db)
     own_q.wait()
+    own_n.start()
     finish(moved_q)
     by_row(64)
     own_k.wait()
@@ -336,9 +340,12 @@
     ya, yd = sc["ya"], sc["yd"]
 
     def by_member(outs, dst, c):
+        pieces = []
         for r in range(4):
             lane = slice(r * 64, r * 64 + 64)
-            dst[c, r] = jnp.concatenate([outs[0][:, lane], outs[1][:, lane]], axis=1)
+            pieces.append(jnp.concatenate([outs[0][:, lane], outs[1][:, lane]], axis=1))
+            dst[c, r] = pieces[r]
+        return pieces
 
     ta, td, other, mine = sc["ta"], sc["td"], sc["other"], sc["mine"]
 
@@ -393,6 +400,10 @@
     pair = []
     for b in range(2):
         pair += fan.partner(4 + b, db.at[:, pl.ds(aligned(b * 2 + 1 - p.core, 512), 512)], other.at[b])
+    own_n.wait()
+    finish(moved_n)
+    dw = sc["dw"]
+    dw[...] = jnp.zeros_like(dw)
 
     def total(c, carry):
         for k in ORDER:
@@ -404,7 +415,13 @@
             for k in range(7):
                 t = t + parts[k, row].astype(F32)
             outs.append(t)
-        by_member(outs, yd, c)
+        grad = dw[...]
+        lanes = pl.ds(aligned(c % 2, 128), 128)
+        for r, piece in enumerate(by_member(outs, yd, c)):
+            hi, lo = halves(piece)
+            n = normed_all[c // 2, r, :, lanes]
+            grad = grad + mm(hi, n, NT) + mm(lo, n, NT)
+        dw[...] = grad
         return carry
 
     lax.fori_loop(0, 2, total, 0)
@@ -412,6 +429,14 @@
     for b in range(2):
         pair[b].wait()
         mine[b] = (db[:, pl.ds(aligned(b * 2 + p.core, 512), 512)] + other[b]).astype(BF16)
+
+    def bias_of(h):
+        z, r = p.spot(h)
+        return mine.at[z, pl.ds(aligned(r, 64), 64)]
+
+    bias_back = fan.members(7, bias_of, lambda k: bo.at[p.h])
+    own_m = pltpu.make_async_copy(bias_of(p.h), bo.at[p.h], local.at[1])
+    own_m.start()
 
     def assemble(src, part):
         rows = slice(part * 32, part * 32 + 32)
@@ -426,7 +451,7 @@
     sc["dq"][...] = dq
     sc["dg"][...] = grad_gate
     normed = sc["normed"][...]
-    wa, wb = sc["wa"], sc["wb"]
+    wa = sc["wa"]
 
     def put(dst, n, value):
         for i in range(2):
@@ -436,33 +461,9 @@
     put(wa, 1, mm(normed, grad_gate, NT))
     put(wa, 2, mm(gated, slope[...]))
     first = Reduce(p, wa, oa, [sc[n] for n in ("a_b0", "a_a0", "a_b1", "a_a1")], (sm["as"], sm["ar"]))
-    last = Reduce(p, wb, ob, [sc[n] for n in ("b_b0", "b_a0", "b_b1", "b_a1")], (sm["bs"], sm["br"]))
     first.pair()
-    lax.fori_loop(2, 4, total, 0)
-    give_half(8, 2, yd, td, 1)
-
-    def bias_of(h):
-        z, r = p.spot(h)
-        return mine.at[z, pl.ds(aligned(r, 64), 64)]
-
-    bias_back = fan.members(7, bias_of, lambda k: bo.at[p.h])
-    own_m = pltpu.make_async_copy(bias_of(p.h), bo.at[p.h], local.at[1])
-    own_m.start()
-    first.block()
-    grad_normed = mm(wq[...], sc["dq"][...]) + mm(wg[...], sc["dg"][...])
+    lax.fori_loop(2, 3, total, 0)
     first.member()
-
-    taken(8, 2, yd, td)
-    dk_hi, dk_lo = halves(assemble(td, 0))
-    dv_hi, dv_lo = halves(assemble(td, 1))
-    normed = sc["normed"][...]
-    put(wb, 0, mm(normed, dk_hi, NT) + mm(normed, dk_lo, NT))
-    put(wb, 1, mm(normed, dv_hi, NT) + mm(normed, dv_lo, NT))
-    last.pair()
-    grad_normed = grad_normed + mm(wk[...], dk_hi) + mm(wk[...], dk_lo) + mm(wv[...], dv_hi) + mm(wv[...], dv_lo)
-    hat = sc["hat"][...]
-    by_gain = jnp.sum(jnp.transpose(grad_normed * hat), axis=0, keepdims=True)
-    last.block()
 
     own_m.wait()
     finish(bias_back)
@@ -476,29 +477,54 @@
             stream(n + 2).start()
     ex, ex_own, exm, exb = sc["ex"], sc["ex_own"], sc["exm"], sc["exb"]
     ex[0:8, :] = jnp.sum(grad_bias.reshape(8, 16, 128), axis=1)
+    grad_normed = mm(wq[...], sc["dq"][...]) + mm(wg[...], sc["dg"][...])
+
+    lax.fori_loop(3, 4, total, 0)
+    dw_r, dw_s, dw_o = sc["dw_r"], sc["dw_s"], sc["dw_o"]
+    eight = pl.ds(aligned(p.g, 8), 8)
+    weights = fan.blocks(14, lambda g: dw.at[pl.ds(aligned(g, 8), 8)], lambda k: dw_r.at[k - 1])
+    give_half(8, 2, yd, td, 1)
+    first.block()
+    finish(weights)
+    grad = dw[eight]
+    for k in range(7):
+        grad = grad + dw_r[k]
+    dw_s[...] = grad
+    weights = fan.partner(15, dw_s, dw_o)
+
+    taken(8, 2, yd, td)
+    dk_hi, dk_lo = halves(assemble(td, 0))
+    dv_hi, dv_lo = halves(assemble(td, 1))
+    grad_normed = grad_normed + mm(wk[...], dk_hi) + mm(wk[...], dk_lo) + mm(wv[...], dv_hi) + mm(wv[...], dv_lo)
+    hat = sc["hat"][...]
+    by_gain = jnp.sum(jnp.transpose(grad_normed * hat), axis=0, keepdims=True)
     ex[8:16, :] = jnp.concatenate([by_gain[:, :128], by_gain[:, 128:], jnp.zeros((6, 128), F32)], axis=0)
     extra = fan.partner(9, ex, ex_own)
-    last.member()
-    first.back_block()
+    finish(weights)
+    ob[p.h, eight] = dw_s[...] + dw_o[...]
+    piece = ob.at[p.h, eight]
+    weights = fan.blocks(16, lambda g: piece, lambda k: piece)
     finish(extra)
     exm[p.h] = ex[...] + ex_own[...]
     extra = fan.members(10, lambda h: exm.at[p.h], lambda k: exm.at[p.h])
+    first.back_member()
 
     scaled = grad_normed * sc["scale"][...]
     m1 = jnp.mean(scaled, axis=0, keepdims=True)
     m2 = jnp.mean(scaled * hat, axis=0, keepdims=True)
     align[...] = jnp.transpose(sc["inv"][0:1, :] * (scaled - m1 - hat * m2)).astype(BF16)
 
-    last.back_block()
+    finish(weights)
+    weights = fan.members(17, lambda h: ob.at[p.h], lambda k: ob.at[p.h])
     finish(extra)
     exb[p.g] = sum_of(exm)
     extra = fan.blocks(11, lambda g: exb.at[p.g], lambda k: exb.at[p.g])
     first.back_pair()
-    last.back_pair()
     finish(extra)
-    ex_out[...] = sum_of(exb)
+    ex_out[0:16, :] = sum_of(exb)
+    ex_out[16:24, :] = pbt[...].astype(F32)
+    finish(weights)
     first.done()
-    last.done()
 
     def drain(c, carry):
         for k in ORDER:
@@ -553,19 +579,19 @@
         "mine": vmem((2, 256, 512), BF16),
         "other": vmem((2, 256, 512), F32),
         "wa": vmem((2, 768, 128), F32),
-        "wb": vmem((2, 512, 128), F32),
+        "xn": vmem((2, 4, 256, 256), BF16),
+        "dw": vmem((64, 256), F32), "dw_r": vmem((7, 8, 256), F32),
+        "dw_s": vmem((8, 256), F32), "dw_o": vmem((8, 256), F32),
         "ex": vmem((16, 128), F32), "ex_own": vmem((16, 128), F32),
         "exm": vmem((8, 16, 128), F32), "exb": vmem((8, 16, 128), F32),
         **reduce_bufs("a", 768),
-        **reduce_bufs("b", 512),
     }
     sems = {
         "hbm": dma((2,)), "local": dma((4,)), "in": dma((9,)),
-        "send": dma((13, 7)), "recv": dma((13, 7)),
+        "send": dma((18, 7)), "recv": dma((18, 7)),
         "ks": dma((CHUNKS, 7)), "kr": dma((CHUNKS, 7)),
         "es": dma((CHUNKS, 7)), "er": dma((CHUNKS, 7)),
         "as": dma((5, 7)), "ar": dma((5, 7)),
-        "bs": dma((5, 7)), "br": dma((5, 7)),
     }
     return pl.pallas_call(
         main_kernel,
@@ -573,28 +599,30 @@
             jax.ShapeDtypeStruct((256, 256), BF16),
             jax.ShapeDtypeStruct((8, 64, 512), BF16),
             jax.ShapeDtypeStruct((768, 256), F32),
-            jax.ShapeDtypeStruct((512, 256), F32),
-            jax.ShapeDtypeStruct((16, 128), F32),
+            jax.ShapeDtypeStruct((8, 64, 256), F32),
+            jax.ShapeDtypeStruct((24, 128), F32),
         ),
         in_specs=[HB] * 10,
         out_specs=(VM,) * 5,
         scratch_shapes=[scratch, sems],
         compiler_params=params(0),
         name="main",
-    )(hom, slope, gain, wq, wk, wv, wg, wo, pbt, pair_rows)
-
-
-def tail_kernel(bo, pbt, align, oa, ob, ex, pair, align_out, q, k, v, g, o, gain, bias, base, sem):
+    )(*[pltpu.with_memory_space_constraint(a, pltpu.HBM) for a in (hom, slope, gain, wq, wk, wv, wg, wo, pbt, pair_rows)])
+
+
+def tail_kernel(bo, align, oa, ob, ex, pair, align_out, q, k, v, g, o, gain, bias, base, kv, sem):
     n = pl.program_id(0)
     moves = [(align, align_out), (ex.at[8:10], gain), (ex.at[0:8], bias)]
-    moves += [(oa.at[0:256], q), (oa.at[256:512], g), (oa.at[512:768], o), (ob.at[0:256], k), (ob.at[256:512], v)]
+    moves += [(oa.at[0:256], q), (oa.at[256:512], g), (oa.at[512:768], o), (kv.at[0], k), (kv.at[1], v)]
     copies = [pltpu.make_async_copy(a, b, sem.at[i]) for i, (a, b) in enumerate(moves)]
 
     @pl.when(n == 0)
     def _():
+        for i in range(2):
+            kv[i] = jnp.transpose(ob[:, i * 32 : i * 32 + 32, :].reshape(256, 256))
         for c in copies:
             c.start()
-        spreaded = spread(pbt[...])
+        spreaded = spread(ex[16:24, :])
         for i in range(16):
             base[:, i * 128 : i * 128 + 128] = only(spreaded, 16, i).astype(BF16)
 
@@ -610,7 +638,7 @@
             c.wait()
 
 
-def tail(bo, pbt, align, oa, ob, ex):
+def tail(bo, align, oa, ob, ex):
     square = jax.ShapeDtypeStruct((256, 256), F32)
     return pl.pallas_call(
         tail_kernel,
@@ -622,12 +650,12 @@
             jax.ShapeDtypeStruct((2, 128), F32),
             jax.ShapeDtypeStruct((8, 128), F32),
         ),
-        in_specs=[VM] * 6,
+        in_specs=[VM] * 5,
         out_specs=(pl.BlockSpec((16, 512, 128), lambda n: (n, 0, 0)),) + (HB,) * 8,
-        scratch_shapes=[pltpu.VMEM((128, 2048), BF16), pltpu.SemaphoreType.DMA((8,))],
+        scratch_shapes=[pltpu.VMEM((128, 2048), BF16), pltpu.VMEM((2, 256, 256), F32), pltpu.SemaphoreType.DMA((8,))],
         compiler_params=pltpu.CompilerParams(vmem_limit_bytes=32 * 1024 * 1024),
         name="tail",
-    )(bo, pbt, align, oa, ob, ex)
+    )(bo, align, oa, ob, ex)
 
 
 def body(
@@ -656,7 +684,7 @@
         pair_input_rows,
     )
     pair_grad, align, grad_q, grad_k, grad_v, grad_g, grad_o, gain, bias = tail(
-        db_own, pair_bias_matrix.T, align, oa, ob, extra
+        db_own, align, oa, ob, extra
     )
     return (
         align.reshape(rows, toks, width),

time: 113 us -> 104 us (0.920)
  local copies, waits for them, and re-layouts: 7.68 us -> 0 us
    unnamed x18 -> x0, local copies, waits for them, and re-layouts: 7.68 us -> none
where the time goes in v5:
time: 104 us; the launch traced here: 103 us
  Pallas kernels  102 us (98%)
    pallas_call x1, Pallas kernels, main(): pl.pallas_call(main_kernel, out_shape=(jax.ShapeDtypeStruct((256, 256), B...  96.8 us
    pallas_call x1, Pallas kernels, tail(): pl.pallas_call(tail_kernel, grid=(4,), out_shape=(jax.ShapeDtypeStruct((6...  5.21 us

profile of v5, /device:TPU:0, one launch (start us, length us, event | category | flops | bytes accessed | tf_op | source)
XLA Modules:
  0.0 102.9 jit_solution(3989292792373742794)
XLA Ops:
  0.6 96.8 %main.1 = (bf16[256,256]{1,0:T(8,128)(2,1)S(1)}, bf16[8,64,512]{2,1,0:T(8,128)(2,1)S(1)}, f32[768,256]{1,0:T(8,128)S(1)}, f32[8,64,256]{2,1,0:T(8,128)S(1)}, f32[24,128]{1,0:T(8,128)S(1)}) custom-call(bf16[256,256]{1,0:T(8,128)(2,1)} %bitcast.7, bf16[256,256]{1,0:T(8,128)(2,1)} %bitcast.8, f32[1,256]{1,0:T(1,128)} %bitcast.10, bf16[256,256]{1,0:T(8,128)(2,1)} %wq_in.1, ...), custom_call_target="tpu_custom_call" | custom-call | tf_op jit(solution)/shard_map/main/pallas_call | solution.py:596
  97.5 5.2 %tail.1 = (bf16[64,512,128]{2,1,0:T(8,128)(2,1)}, bf16[256,256]{1,0:T(8,128)(2,1)}, f32[256,256]{1,0:T(8,128)}, f32[256,256]{1,0:T(8,128)}, f32[256,256]{1,0:T(8...) custom-call(bf16[8,64,512]{2,1,0:T(8,128)(2,1)S(1)} %get-tuple-element.23.bo, ...), custom_call_target="tpu_custom_call" | custom-call | tf_op jit(solution)/shard_map/tail/pallas_call | solution.py:643

commit v6 on v5

--- a/solution.py
+++ b/solution.py
@@ -430,14 +430,6 @@
         pair[b].wait()
         mine[b] = (db[:, pl.ds(aligned(b * 2 + p.core, 512), 512)] + other[b]).astype(BF16)
 
-    def bias_of(h):
-        z, r = p.spot(h)
-        return mine.at[z, pl.ds(aligned(r, 64), 64)]
-
-    bias_back = fan.members(7, bias_of, lambda k: bo.at[p.h])
-    own_m = pltpu.make_async_copy(bias_of(p.h), bo.at[p.h], local.at[1])
-    own_m.start()
-
     def assemble(src, part):
         rows = slice(part * 32, part * 32 + 32)
         return jnp.concatenate([src[:, pp, rows, :].reshape(256, 128) for pp in range(2)], axis=1)
@@ -464,6 +456,28 @@
     first.pair()
     lax.fori_loop(2, 3, total, 0)
     first.member()
+
+    def bias_of(h):
+        z, r = p.spot(h)
+        return mine.at[z, pl.ds(aligned(r, 64), 64)]
+
+    bias_back = fan.members(7, bias_of, lambda k: bo.at[p.h])
+    own_m = pltpu.make_async_copy(bias_of(p.h), bo.at[p.h], local.at[1])
+    own_m.start()
+
+    lax.fori_loop(3, 4, total, 0)
+    dw_r, dw_s, dw_o = sc["dw_r"], sc["dw_s"], sc["dw_o"]
+    eight = pl.ds(aligned(p.g, 8), 8)
+    weights = fan.blocks(14, lambda g: dw.at[pl.ds(aligned(g, 8), 8)], lambda k: dw_r.at[k - 1])
+    give_half(8, 2, yd, td, 1)
+    grad_normed = mm(wq[...], sc["dq"][...]) + mm(wg[...], sc["dg"][...])
+    first.block()
+    finish(weights)
+    grad = dw[eight]
+    for k in range(7):
+        grad = grad + dw_r[k]
+    dw_s[...] = grad
+    weights = fan.partner(15, dw_s, dw_o)
 
     own_m.wait()
     finish(bias_back)
@@ -477,20 +491,11 @@
             stream(n + 2).start()
     ex, ex_own, exm, exb = sc["ex"], sc["ex_own"], sc["exm"], sc["exb"]
     ex[0:8, :] = jnp.sum(grad_bias.reshape(8, 16, 128), axis=1)
-    grad_normed = mm(wq[...], sc["dq"][...]) + mm(wg[...], sc["dg"][...])
-
-    lax.fori_loop(3, 4, total, 0)
-    dw_r, dw_s, dw_o = sc["dw_r"], sc["dw_s"], sc["dw_o"]
-    eight = pl.ds(aligned(p.g, 8), 8)
-    weights = fan.blocks(14, lambda g: dw.at[pl.ds(aligned(g, 8), 8)], lambda k: dw_r.at[k - 1])
-    give_half(8, 2, yd, td, 1)
-    first.block()
     finish(weights)
-    grad = dw[eight]
-    for k in range(7):
-        grad = grad + dw_r[k]
-    dw_s[...] = grad
-    weights = fan.partner(15, dw_s, dw_o)
+    ob[p.h, eight] = dw_s[...] + dw_o[...]
+    piece = ob.at[p.h, eight]
+    weights = fan.blocks(16, lambda g: piece, lambda k: piece)
+    first.back_member()
 
     taken(8, 2, yd, td)
     dk_hi, dk_lo = halves(assemble(td, 0))
@@ -501,21 +506,16 @@
     ex[8:16, :] = jnp.concatenate([by_gain[:, :128], by_gain[:, 128:], jnp.zeros((6, 128), F32)], axis=0)
     extra = fan.partner(9, ex, ex_own)
     finish(weights)
-    ob[p.h, eight] = dw_s[...] + dw_o[...]
-    piece = ob.at[p.h, eight]
-    weights = fan.blocks(16, lambda g: piece, lambda k: piece)
+    weights = fan.members(17, lambda h: ob.at[p.h], lambda k: ob.at[p.h])
     finish(extra)
     exm[p.h] = ex[...] + ex_own[...]
     extra = fan.members(10, lambda h: exm.at[p.h], lambda k: exm.at[p.h])
-    first.back_member()
 
     scaled = grad_normed * sc["scale"][...]
     m1 = jnp.mean(scaled, axis=0, keepdims=True)
     m2 = jnp.mean(scaled * hat, axis=0, keepdims=True)
     align[...] = jnp.transpose(sc["inv"][0:1, :] * (scaled - m1 - hat * m2)).astype(BF16)
 
-    finish(weights)
-    weights = fan.members(17, lambda h: ob.at[p.h], lambda k: ob.at[p.h])
     finish(extra)
     exb[p.g] = sum_of(exm)
     extra = fan.blocks(11, lambda g: exb.at[p.g], lambda k: exb.at[p.g])

time: 104 us -> 102 us (0.981); the launches traced: 103 us -> 102 us
  no operation moved by 1% of the time
where the time goes in v6:
time: 102 us
  Pallas kernels  101 us (99%)
    pallas_call x1, Pallas kernels, main(): pl.pallas_call(main_kernel, out_shape=(jax.ShapeDtypeStruct((256, 256), B...  96.2 us
    pallas_call x1, Pallas kernels, tail(): pl.pallas_call(tail_kernel, grid=(4,), out_shape=(jax.ShapeDtypeStruct((6...  5.21 us

profile of v6, /device:TPU:0, one launch (start us, length us, event | category | flops | bytes accessed | tf_op | source)
XLA Modules:
  0.0 102.2 jit_solution(17739003412000946802)
XLA Ops:
  0.6 96.2 %main.1 = (bf16[256,256]{1,0:T(8,128)(2,1)S(1)}, bf16[8,64,512]{2,1,0:T(8,128)(2,1)S(1)}, f32[768,256]{1,0:T(8,128)S(1)}, f32[8,64,256]{2,1,0:T(8,128)S(1)}, f32[24,128]{1,0:T(8,128)S(1)}) custom-call(bf16[256,256]{1,0:T(8,128)(2,1)} %bitcast.7, bf16[256,256]{1,0:T(8,128)(2,1)} %bitcast.8, f32[1,256]{1,0:T(1,128)} %bitcast.10, bf16[256,256]{1,0:T(8,128)(2,1)} %wq_in.1, ...), custom_call_target="tpu_custom_call" | custom-call | tf_op jit(solution)/shard_map/main/pallas_call | solution.py:596
  96.9 5.2 %tail.1 = (bf16[64,512,128]{2,1,0:T(8,128)(2,1)}, bf16[256,256]{1,0:T(8,128)(2,1)}, f32[256,256]{1,0:T(8,128)}, f32[256,256]{1,0:T(8,128)}, f32[256,256]{1,0:T(8...) custom-call(bf16[8,64,512]{2,1,0:T(8,128)(2,1)S(1)} %get-tuple-element.23.bo, ...), custom_call_target="tpu_custom_call" | custom-call | tf_op jit(solution)/shard_map/tail/pallas_call | solution.py:643

commit v7 on v6

--- a/solution.py
+++ b/solution.py
@@ -415,13 +415,14 @@
             for k in range(7):
                 t = t + parts[k, row].astype(F32)
             outs.append(t)
-        grad = dw[...]
+        grad = jnp.concatenate([dw[0], dw[1]], axis=1)
         lanes = pl.ds(aligned(c % 2, 128), 128)
         for r, piece in enumerate(by_member(outs, yd, c)):
             hi, lo = halves(piece)
             n = normed_all[c // 2, r, :, lanes]
             grad = grad + mm(hi, n, NT) + mm(lo, n, NT)
-        dw[...] = grad
+        dw[0] = grad[:, :128]
+        dw[1] = grad[:, 128:]
         return carry
 
     lax.fori_loop(0, 2, total, 0)
@@ -466,18 +467,14 @@
     own_m.start()
 
     lax.fori_loop(3, 4, total, 0)
-    dw_r, dw_s, dw_o = sc["dw_r"], sc["dw_s"], sc["dw_o"]
-    eight = pl.ds(aligned(p.g, 8), 8)
-    weights = fan.blocks(14, lambda g: dw.at[pl.ds(aligned(g, 8), 8)], lambda k: dw_r.at[k - 1])
+    dw_o, dws = sc["dw_o"], sc["dws"]
+    weights = fan.partner(14, dw.at[1 - p.core], dw_o)
     give_half(8, 2, yd, td, 1)
     grad_normed = mm(wq[...], sc["dq"][...]) + mm(wg[...], sc["dg"][...])
+    finish(weights)
+    dws[p.g] = dw[p.core] + dw_o[...]
+    weights = fan.blocks(15, lambda g: dws.at[p.g], lambda k: dws.at[p.g])
     first.block()
-    finish(weights)
-    grad = dw[eight]
-    for k in range(7):
-        grad = grad + dw_r[k]
-    dw_s[...] = grad
-    weights = fan.partner(15, dw_s, dw_o)
 
     own_m.wait()
     finish(bias_back)
@@ -492,10 +489,9 @@
     ex, ex_own, exm, exb = sc["ex"], sc["ex_own"], sc["exm"], sc["exb"]
     ex[0:8, :] = jnp.sum(grad_bias.reshape(8, 16, 128), axis=1)
     finish(weights)
-    ob[p.h, eight] = dw_s[...] + dw_o[...]
-    piece = ob.at[p.h, eight]
-    weights = fan.blocks(16, lambda g: piece, lambda k: piece)
-    first.back_member()
+    ob[p.core, p.h] = sum_of(dws)
+    piece = ob.at[p.core, p.h]
+    weights = fan.members(16, lambda h: piece, lambda k: piece)
 
     taken(8, 2, yd, td)
     dk_hi, dk_lo = halves(assemble(td, 0))
@@ -505,8 +501,7 @@
     by_gain = jnp.sum(jnp.transpose(grad_normed * hat), axis=0, keepdims=True)
     ex[8:16, :] = jnp.concatenate([by_gain[:, :128], by_gain[:, 128:], jnp.zeros((6, 128), F32)], axis=0)
     extra = fan.partner(9, ex, ex_own)
-    finish(weights)
-    weights = fan.members(17, lambda h: ob.at[p.h], lambda k: ob.at[p.h])
+    first.back_member()
     finish(extra)
     exm[p.h] = ex[...] + ex_own[...]
     extra = fan.members(10, lambda h: exm.at[p.h], lambda k: exm.at[p.h])
@@ -519,6 +514,8 @@
     finish(extra)
     exb[p.g] = sum_of(exm)
     extra = fan.blocks(11, lambda g: exb.at[p.g], lambda k: exb.at[p.g])
+    finish(weights)
+    weights = fan.partner(17, ob.at[p.core], ob.at[p.core])
     first.back_pair()
     finish(extra)
     ex_out[0:16, :] = sum_of(exb)
@@ -580,8 +577,7 @@
         "other": vmem((2, 256, 512), F32),
         "wa": vmem((2, 768, 128), F32),
         "xn": vmem((2, 4, 256, 256), BF16),
-        "dw": vmem((64, 256), F32), "dw_r": vmem((7, 8, 256), F32),
-        "dw_s": vmem((8, 256), F32), "dw_o": vmem((8, 256), F32),
+        "dw": vmem((2, 64, 128), F32), "dw_o": vmem((64, 128), F32), "dws": vmem((8, 64, 128), F32),
         "ex": vmem((16, 128), F32), "ex_own": vmem((16, 128), F32),
         "exm": vmem((8, 16, 128), F32), "exb": vmem((8, 16, 128), F32),
         **reduce_bufs("a", 768),
@@ -599,7 +595,7 @@
             jax.ShapeDtypeStruct((256, 256), BF16),
             jax.ShapeDtypeStruct((8, 64, 512), BF16),
             jax.ShapeDtypeStruct((768, 256), F32),
-            jax.ShapeDtypeStruct((8, 64, 256), F32),
+            jax.ShapeDtypeStruct((2, 8, 64, 128), F32),
             jax.ShapeDtypeStruct((24, 128), F32),
         ),
         in_specs=[HB] * 10,
@@ -619,7 +615,9 @@
     @pl.when(n == 0)
     def _():
         for i in range(2):
-            kv[i] = jnp.transpose(ob[:, i * 32 : i * 32 + 32, :].reshape(256, 256))
+            for half in range(2):
+                part = ob[half, :, i * 32 : i * 32 + 32, :].reshape(256, 128)
+                kv[i, half * 128 : half * 128 + 128, :] = jnp.transpose(part)
         for c in copies:
             c.start()
         spreaded = spread(ex[16:24, :])

time: 102 us -> 101 us (level)
  Pallas kernels: 101 us -> 99.8 us
    pallas_call x1, Pallas kernels: 96.2 us -> 94.6 us  [main(): pl.pallas_call(main_kernel, out_shape=(jax.ShapeDtypeStruct((256, 256), B...]
where the time goes in v7:
time: 101 us
  Pallas kernels  99.8 us (99%)
    pallas_call x1, Pallas kernels, main(): pl.pallas_call(main_kernel, out_shape=(jax.ShapeDtypeStruct((256, 256), B...  94.6 us
    pallas_call x1, Pallas kernels, tail(): pl.pallas_call(tail_kernel, grid=(4,), out_shape=(jax.ShapeDtypeStruct((6...  5.21 us

profile of v7, /device:TPU:0, one launch (start us, length us, event | category | flops | bytes accessed | tf_op | source)
XLA Modules:
  0.0 100.6 jit_solution(6458563666933337625)
XLA Ops:
  0.6 94.6 %main.1 = (bf16[256,256]{1,0:T(8,128)(2,1)S(1)}, bf16[8,64,512]{2,1,0:T(8,128)(2,1)S(1)}, f32[768,256]{1,0:T(8,128)S(1)}, f32[2,8,64,128]{3,2,1,0:T(8,128)S(1)}, f32[24,128]{1,0:T(8,128)S(1)}) custom-call(bf16[256,256]{1,0:T(8,128)(2,1)} %bitcast.7, bf16[256,256]{1,0:T(8,128)(2,1)} %bitcast.8, f32[1,256]{1,0:T(1,128)} %bitcast.10, bf16[256,256]{1,0:T(8,128)(2,1)} %wq_in.1, ...), custom_call_target="tpu_custom_call" | custom-call | tf_op jit(solution)/shard_map/main/pallas_call | solution.py:592
  95.3 5.2 %tail.1 = (bf16[64,512,128]{2,1,0:T(8,128)(2,1)}, bf16[256,256]{1,0:T(8,128)(2,1)}, f32[256,256]{1,0:T(8,128)}, f32[256,256]{1,0:T(8,128)}, f32[256,256]{1,0:T(8...) custom-call(bf16[8,64,512]{2,1,0:T(8,128)(2,1)S(1)} %get-tuple-element.23.bo, ...), custom_call_target="tpu_custom_call" | custom-call | tf_op jit(solution)/shard_map/tail/pallas_call | solution.py:641

commit v8 on v7

--- a/solution.py
+++ b/solution.py
@@ -145,49 +145,34 @@
         c.wait()
 
 
-class Reduce:
-    def __init__(self, p, w, o, bufs, sems):
-        self.p, self.w, self.o = p, w, o
-        self.b0, self.a0, self.b1, self.a1 = bufs
-        self.fan = Fan(p, *sems)
-        self.n = w.shape[1] // 8
-        self.lanes = pl.ds(aligned(p.core, 128), 128)
+class Gather:
+    def __init__(self, p, fan, stage, w, other, slots, o):
+        self.p, self.fan, self.stage = p, fan, stage
+        self.w, self.other, self.slots, self.o = w, other, slots, o
         self.copies = []
 
-    def rows(self, h):
-        return pl.ds(aligned(h, self.n), self.n)
-
     def pair(self):
-        self.copies = self.fan.partner(0, self.w.at[1 - self.p.core], self.b0)
+        self.copies = self.fan.partner(self.stage, self.w.at[1 - self.p.core], self.other)
+
+    def block(self):
+        finish(self.copies)
+        self.slots[self.p.g] = self.w[self.p.core] + self.other[...]
+        piece = self.slots.at[self.p.g]
+        self.copies = self.fan.blocks(self.stage + 1, lambda g: piece, lambda k: piece)
 
     def member(self):
         finish(self.copies)
-        self.a0[...] = self.w[self.p.core] + self.b0[...]
-        self.copies = self.fan.members(1, lambda h: self.a0.at[self.rows(h)], lambda k: self.b1.at[k - 1])
-
-    def block(self):
-        finish(self.copies)
-        total = self.a0[self.rows(self.p.h)]
-        for k in range(7):
-            total = total + self.b1[k]
-        self.a1[self.p.g] = total
-        piece = self.a1.at[self.p.g]
-        self.copies = self.fan.blocks(2, lambda g: piece, lambda k: piece)
-
-    def back_member(self):
-        finish(self.copies)
-        self.o[self.rows(self.p.h), self.lanes] = sum_of(self.a1)
-        piece = self.o.at[self.rows(self.p.h), self.lanes]
-        self.copies = self.fan.members(3, lambda h: piece, lambda k: piece)
+        self.o[self.p.core, self.p.h] = sum_of(self.slots)
+        piece = self.o.at[self.p.core, self.p.h]
+        self.copies = self.fan.members(self.stage + 2, lambda h: piece, lambda k: piece)
 
     def back_pair(self):
         finish(self.copies)
-        piece = self.o.at[:, self.lanes]
-        self.copies = self.fan.partner(4, piece, piece)
+        piece = self.o.at[self.p.core]
+        self.copies = self.fan.partner(self.stage + 3, piece, piece)
 
     def done(self):
         finish(self.copies)
-        self.copies = []
 
 
 def only(value, n, i):
@@ -261,8 +246,9 @@
     t_ref[:, 64:96, :] = mm(wq[...], normed, TN).astype(BF16).reshape(8, 32, 256)
     gate = jax.nn.sigmoid(mm(wg[...], normed, TN))
     grad_gated = mm(wo[...], slope[...], NT)
-    sc["gate"][...] = gate
-    sc["gg"][...] = grad_gated
+    gates = sc["gates"]
+    gates[:, 0:32, :] = gate.reshape(8, 32, 256)
+    gates[:, 32:64, :] = grad_gated.reshape(8, 32, 256)
     t_ref[:, 96:128, :] = (grad_gated * gate).astype(BF16).reshape(8, 32, 256)
     moved_q = fan.members(12, lambda h: t_ref.at[h, 64:128], lambda k: xr.at[z_lo, r4, 64:128])
     own_q = pltpu.make_async_copy(t_ref.at[p.h, 64:128], xr.at[z_lo, r4, 64:128], local.at[3])
@@ -283,9 +269,15 @@
     biases = fan.members(1, lambda h: b_ref.at[h], lambda k: bias.at[toks, cols])
     own_b = pltpu.make_async_copy(b_ref.at[p.h], bias.at[toks, cols], local.at[1])
     own_b.start()
-    normed_all = sc["xn"]
+    gates_all, normed_all, slope_all = sc["xg"], sc["xn"], sc["xs"]
+    moved_g = fan.members(10, lambda h: gates.at[h], lambda k: gates_all.at[z_lo, r4])
+    own_g = pltpu.make_async_copy(gates.at[p.h], gates_all.at[z_lo, r4], local.at[4])
+    own_g.start()
     moved_n = fan.members(13, lambda h: sc["normed"], lambda k: normed_all.at[z_lo, r4])
+    moved_n += fan.members(11, lambda h: slope, lambda k: slope_all.at[z_lo, r4])
     own_n = pltpu.make_async_copy(sc["normed"], normed_all.at[z_lo, r4], local.at[3])
+    own_s = pltpu.make_async_copy(slope, slope_all.at[z_lo, r4], local.at[5])
+    own_s.start()
 
     def by_row(lo):
         for z in range(2):
@@ -344,10 +336,11 @@
         for r in range(4):
             lane = slice(r * 64, r * 64 + 64)
             pieces.append(jnp.concatenate([outs[0][:, lane], outs[1][:, lane]], axis=1))
-            dst[c, r] = pieces[r]
+            if dst is not None:
+                dst[c, r] = pieces[r]
         return pieces
 
-    ta, td, other, mine = sc["ta"], sc["td"], sc["other"], sc["mine"]
+    ta, td, other, mine, gated = sc["ta"], sc["td"], sc["other"], sc["mine"], sc["gated"]
 
     def give(stage, src, dst, k, z):
         h = (p.h + k) % 8
@@ -384,7 +377,19 @@
             outs.append(row_backward(xt, kv, bias, db, dkv, c * per + i))
         for k in ORDER:
             partial(c, k).start()
-        by_member(outs, ya, c)
+        @pl.when(c == 0)
+        def _():
+            own_g.wait()
+            finish(moved_g)
+
+        lanes = pl.ds(aligned(c % 2, 128), 128)
+        for r, piece in enumerate(by_member(outs, None, c)):
+            attended = piece[0:32]
+            gate = gates_all[c // 2, r, 0:32, lanes]
+            grad_gated = gates_all[c // 2, r, 32:64, lanes]
+            ya[c, r, 0:32] = piece[32:64].astype(BF16)
+            ya[c, r, 32:64] = (grad_gated * attended * gate * (1.0 - gate)).astype(BF16)
+            gated[c, r] = (gate * attended).astype(BF16)
         for z in range(2):
 
             @pl.when(c == 2 * z + 1)
@@ -401,9 +406,25 @@
     for b in range(2):
         pair += fan.partner(4 + b, db.at[:, pl.ds(aligned(b * 2 + 1 - p.core, 512), 512)], other.at[b])
     own_n.wait()
+    own_s.wait()
     finish(moved_n)
-    dw = sc["dw"]
+    dw, de = sc["dw"], sc["de"]
     dw[...] = jnp.zeros_like(dw)
+
+    grad_qg = jnp.zeros((64, 256), F32)
+    grad_o = jnp.zeros((32, 256), F32)
+    for c in range(CHUNKS):
+        lane = slice(c % 2 * 128, c % 2 * 128 + 128)
+        for r in range(4):
+            grad_qg = grad_qg + mm(ya[c, r], normed_all[c // 2, r, :, lane], NT)
+            grad_o = grad_o + mm(gated[c, r], slope_all[c // 2, r, lane, :])
+    for half in range(2):
+        lane = slice(half * 128, half * 128 + 128)
+        de[half, 0:64] = grad_qg[:, lane]
+        de[half, 64:96] = grad_o[:, lane]
+    first = Gather(p, fan, 18, de, sc["de_o"], sc["des"], oa)
+    last = Gather(p, fan, 14, dw, sc["dw_o"], sc["dws"], ob)
+    first.pair()
 
     def total(c, carry):
         for k in ORDER:
@@ -435,28 +456,8 @@
         rows = slice(part * 32, part * 32 + 32)
         return jnp.concatenate([src[:, pp, rows, :].reshape(256, 128) for pp in range(2)], axis=1)
 
-    taken(6, 0, ya, ta)
-    attended = assemble(ta, 0)
-    dq = assemble(ta, 1).astype(BF16)
-    gate = sc["gate"][...]
-    gated = (gate * attended).astype(BF16)
-    grad_gate = (sc["gg"][...] * attended * gate * (1.0 - gate)).astype(BF16)
-    sc["dq"][...] = dq
-    sc["dg"][...] = grad_gate
-    normed = sc["normed"][...]
-    wa = sc["wa"]
-
-    def put(dst, n, value):
-        for i in range(2):
-            dst[i, n * 256 : n * 256 + 256, :] = value[:, i * 128 : i * 128 + 128]
-
-    put(wa, 0, mm(normed, dq, NT))
-    put(wa, 1, mm(normed, grad_gate, NT))
-    put(wa, 2, mm(gated, slope[...]))
-    first = Reduce(p, wa, oa, [sc[n] for n in ("a_b0", "a_a0", "a_b1", "a_a1")], (sm["as"], sm["ar"]))
-    first.pair()
+    first.block()
     lax.fori_loop(2, 3, total, 0)
-    first.member()
 
     def bias_of(h):
         z, r = p.spot(h)
@@ -467,14 +468,11 @@
     own_m.start()
 
     lax.fori_loop(3, 4, total, 0)
-    dw_o, dws = sc["dw_o"], sc["dws"]
-    weights = fan.partner(14, dw.at[1 - p.core], dw_o)
+    last.pair()
     give_half(8, 2, yd, td, 1)
-    grad_normed = mm(wq[...], sc["dq"][...]) + mm(wg[...], sc["dg"][...])
-    finish(weights)
-    dws[p.g] = dw[p.core] + dw_o[...]
-    weights = fan.blocks(15, lambda g: dws.at[p.g], lambda k: dws.at[p.g])
-    first.block()
+    taken(6, 0, ya, ta)
+    grad_normed = mm(wq[...], assemble(ta, 0)) + mm(wg[...], assemble(ta, 1))
+    last.block()
 
     own_m.wait()
     finish(bias_back)
@@ -488,10 +486,8 @@
             stream(n + 2).start()
     ex, ex_own, exm, exb = sc["ex"], sc["ex_own"], sc["exm"], sc["exb"]
     ex[0:8, :] = jnp.sum(grad_bias.reshape(8, 16, 128), axis=1)
-    finish(weights)
-    ob[p.core, p.h] = sum_of(dws)
-    piece = ob.at[p.core, p.h]
-    weights = fan.members(16, lambda h: piece, lambda k: piece)
+    first.member()
+    last.member()
 
     taken(8, 2, yd, td)
     dk_hi, dk_lo = halves(assemble(td, 0))
@@ -501,10 +497,9 @@
     by_gain = jnp.sum(jnp.transpose(grad_normed * hat), axis=0, keepdims=True)
     ex[8:16, :] = jnp.concatenate([by_gain[:, :128], by_gain[:, 128:], jnp.zeros((6, 128), F32)], axis=0)
     extra = fan.partner(9, ex, ex_own)
-    first.back_member()
     finish(extra)
     exm[p.h] = ex[...] + ex_own[...]
-    extra = fan.members(10, lambda h: exm.at[p.h], lambda k: exm.at[p.h])
+    extra = fan.members(22, lambda h: exm.at[p.h], lambda k: exm.at[p.h])
 
     scaled = grad_normed * sc["scale"][...]
     m1 = jnp.mean(scaled, axis=0, keepdims=True)
@@ -513,15 +508,14 @@
 
     finish(extra)
     exb[p.g] = sum_of(exm)
-    extra = fan.blocks(11, lambda g: exb.at[p.g], lambda k: exb.at[p.g])
-    finish(weights)
-    weights = fan.partner(17, ob.at[p.core], ob.at[p.core])
+    extra = fan.blocks(23, lambda g: exb.at[p.g], lambda k: exb.at[p.g])
     first.back_pair()
+    last.back_pair()
     finish(extra)
     ex_out[0:16, :] = sum_of(exb)
     ex_out[16:24, :] = pbt[...].astype(F32)
-    finish(weights)
     first.done()
+    last.done()
 
     def drain(c, carry):
         for k in ORDER:
@@ -542,14 +536,6 @@
 def main(hom, slope, gain, wq, wk, wv, wg, wo, pbt, pair_rows):
     dma = pltpu.SemaphoreType.DMA
     vmem = pltpu.VMEM
-
-    def reduce_bufs(name, rows):
-        return {
-            name + "_b0": vmem((rows, 128), F32),
-            name + "_a0": vmem((rows, 128), F32),
-            name + "_b1": vmem((7, rows // 8, 128), F32),
-            name + "_a1": vmem((8, rows // 8, 128), F32),
-        }
 
     square = vmem((256, 256), F32)
     square_half = vmem((256, 256), BF16)
@@ -558,8 +544,8 @@
         "mask": vmem((16, 128, 128), BF16),
         "hom": square_half, "slope": square_half, "gain": vmem((1, 256), F32), "pbt": vmem((8, 128), BF16),
         "wq": square_half, "wk": square_half, "wv": square_half, "wg": square_half, "wo": square_half,
-        "hat": square, "scale": square, "inv": vmem((8, 256), F32), "gate": square, "gg": square,
-        "normed": square_half, "dq": square_half, "dg": square_half,
+        "hat": square, "scale": square, "inv": vmem((8, 256), F32), "gates": vmem((8, 64, 256), F32),
+        "normed": square_half,
         "t": vmem((8, 128, 256), BF16),
         "b": vmem((8, 64, 512), BF16),
         "xr": vmem((2, 4, 128, 256), BF16),
@@ -569,32 +555,31 @@
         "db": vmem((256, 2048), F32),
         "dkv": vmem((8, 64, 2048), BF16),
         "parts": vmem((7, 8, 64, 256), BF16),
-        "ya": vmem((4, 4, 64, 128), F32),
+        "ya": vmem((4, 4, 64, 128), BF16),
+        "gated": vmem((4, 4, 32, 128), BF16),
         "yd": vmem((4, 4, 64, 128), F32),
-        "ta": vmem((8, 2, 64, 128), F32),
+        "ta": vmem((8, 2, 64, 128), BF16),
         "td": vmem((8, 2, 64, 128), F32),
         "mine": vmem((2, 256, 512), BF16),
         "other": vmem((2, 256, 512), F32),
-        "wa": vmem((2, 768, 128), F32),
-        "xn": vmem((2, 4, 256, 256), BF16),
+        "xn": vmem((2, 4, 256, 256), BF16), "xs": vmem((2, 4, 256, 256), BF16), "xg": vmem((2, 4, 64, 256), F32),
+        "de": vmem((2, 96, 128), F32), "de_o": vmem((96, 128), F32), "des": vmem((8, 96, 128), F32),
         "dw": vmem((2, 64, 128), F32), "dw_o": vmem((64, 128), F32), "dws": vmem((8, 64, 128), F32),
         "ex": vmem((16, 128), F32), "ex_own": vmem((16, 128), F32),
         "exm": vmem((8, 16, 128), F32), "exb": vmem((8, 16, 128), F32),
-        **reduce_bufs("a", 768),
     }
     sems = {
-        "hbm": dma((2,)), "local": dma((4,)), "in": dma((9,)),
-        "send": dma((18, 7)), "recv": dma((18, 7)),
+        "hbm": dma((2,)), "local": dma((6,)), "in": dma((9,)),
+        "send": dma((24, 7)), "recv": dma((24, 7)),
         "ks": dma((CHUNKS, 7)), "kr": dma((CHUNKS, 7)),
         "es": dma((CHUNKS, 7)), "er": dma((CHUNKS, 7)),
-        "as": dma((5, 7)), "ar": dma((5, 7)),
     }
     return pl.pallas_call(
         main_kernel,
         out_shape=(
             jax.ShapeDtypeStruct((256, 256), BF16),
             jax.ShapeDtypeStruct((8, 64, 512), BF16),
-            jax.ShapeDtypeStruct((768, 256), F32),
+            jax.ShapeDtypeStruct((2, 8, 96, 128), F32),
             jax.ShapeDtypeStruct((2, 8, 64, 128), F32),
             jax.ShapeDtypeStruct((24, 128), F32),
         ),
@@ -609,15 +594,16 @@
 def tail_kernel(bo, align, oa, ob, ex, pair, align_out, q, k, v, g, o, gain, bias, base, kv, sem):
     n = pl.program_id(0)
     moves = [(align, align_out), (ex.at[8:10], gain), (ex.at[0:8], bias)]
-    moves += [(oa.at[0:256], q), (oa.at[256:512], g), (oa.at[512:768], o), (kv.at[0], k), (kv.at[1], v)]
+    moves += [(kv.at[i], w) for i, w in enumerate((k, v, q, g, o))]
     copies = [pltpu.make_async_copy(a, b, sem.at[i]) for i, (a, b) in enumerate(moves)]
 
     @pl.when(n == 0)
     def _():
-        for i in range(2):
-            for half in range(2):
-                part = ob[half, :, i * 32 : i * 32 + 32, :].reshape(256, 128)
-                kv[i, half * 128 : half * 128 + 128, :] = jnp.transpose(part)
+        for half in range(2):
+            lane = slice(half * 128, half * 128 + 128)
+            for i, (ref, row) in enumerate(((ob, 0), (ob, 32), (oa, 0), (oa, 32))):
+                kv[i, lane, :] = jnp.transpose(ref[half, :, row : row + 32, :].reshape(256, 128))
+            kv[4, :, lane] = oa[half, :, 64:96, :].reshape(256, 128)
         for c in copies:
             c.start()
         spreaded = spread(ex[16:24, :])
@@ -650,7 +636,7 @@
         ),
         in_specs=[VM] * 5,
         out_specs=(pl.BlockSpec((16, 512, 128), lambda n: (n, 0, 0)),) + (HB,) * 8,
-        scratch_shapes=[pltpu.VMEM((128, 2048), BF16), pltpu.VMEM((2, 256, 256), F32), pltpu.SemaphoreType.DMA((8,))],
+        scratch_shapes=[pltpu.VMEM((128, 2048), BF16), pltpu.VMEM((5, 256, 256), F32), pltpu.SemaphoreType.DMA((8,))],
         compiler_params=pltpu.CompilerParams(vmem_limit_bytes=32 * 1024 * 1024),
         name="tail",
     )(bo, align, oa, ob, ex)

time: 101 us -> 96.2 us (0.952)
  Pallas kernels: 99.8 us -> 95.2 us
    pallas_call x1, Pallas kernels: 94.6 us -> 89.9 us  [main(): pl.pallas_call(main_kernel, out_shape=(jax.ShapeDtypeStruct((256, 256), B...]
where the time goes in v8:
time: 96.2 us; the launch traced here: 96 us
  Pallas kernels  95.2 us (99%)
    pallas_call x1, Pallas kernels, main(): pl.pallas_call(main_kernel, out_shape=(jax.ShapeDtypeStruct((256, 256), B...  89.9 us
    pallas_call x1, Pallas kernels, tail(): pl.pallas_call(tail_kernel, grid=(4,), out_shape=(jax.ShapeDtypeStruct((6...  5.38 us

profile of v8, /device:TPU:0, one launch (start us, length us, event | category | flops | bytes accessed | tf_op | source)
XLA Modules:
  0.0 96.0 jit_solution(3769747490819444359)
XLA Ops:
  0.6 89.9 %main.1 = (bf16[256,256]{1,0:T(8,128)(2,1)S(1)}, bf16[8,64,512]{2,1,0:T(8,128)(2,1)S(1)}, f32[2,8,96,128]{3,2,1,0:T(8,128)S(1)}, f32[2,8,64,128]{3,2,1,0:T(8,128)S(1)}, f32[24,128]{1,0:T(8,128)S(1)}) custom-call(bf16[256,256]{1,0:T(8,128)(2,1)} %bitcast.7, bf16[256,256]{1,0:T(8,128)(2,1)} %bitcast.8, f32[1,256]{1,0:T(1,128)} %bitcast.10, ...), custom_call_target="tpu_custom_call" | custom-call | tf_op jit(solution)/shard_map/main/pallas_call | solution.py:577
  90.5 5.4 %tail.1 = (bf16[64,512,128]{2,1,0:T(8,128)(2,1)}, bf16[256,256]{1,0:T(8,128)(2,1)}, f32[256,256]{1,0:T(8,128)}, f32[256,256]{1,0:T(8,128)}, f32[256,256]{1,0:T(8...) custom-call(bf16[8,64,512]{2,1,0:T(8,128)(2,1)S(1)} %get-tuple-element.23.bo, ...), custom_call_target="tpu_custom_call" | custom-call | tf_op jit(solution)/shard_map/tail/pallas_call | solution.py:627

commit v9 on v8

--- a/solution.py
+++ b/solution.py
@@ -274,7 +274,7 @@
     own_g = pltpu.make_async_copy(gates.at[p.h], gates_all.at[z_lo, r4], local.at[4])
     own_g.start()
     moved_n = fan.members(13, lambda h: sc["normed"], lambda k: normed_all.at[z_lo, r4])
-    moved_n += fan.members(11, lambda h: slope, lambda k: slope_all.at[z_lo, r4])
+    moved_s = fan.members(11, lambda h: slope, lambda k: slope_all.at[z_lo, r4])
     own_n = pltpu.make_async_copy(sc["normed"], normed_all.at[z_lo, r4], local.at[3])
     own_s = pltpu.make_async_copy(slope, slope_all.at[z_lo, r4], local.at[5])
     own_s.start()
@@ -406,25 +406,9 @@
     for b in range(2):
         pair += fan.partner(4 + b, db.at[:, pl.ds(aligned(b * 2 + 1 - p.core, 512), 512)], other.at[b])
     own_n.wait()
-    own_s.wait()
     finish(moved_n)
     dw, de = sc["dw"], sc["de"]
     dw[...] = jnp.zeros_like(dw)
-
-    grad_qg = jnp.zeros((64, 256), F32)
-    grad_o = jnp.zeros((32, 256), F32)
-    for c in range(CHUNKS):
-        lane = slice(c % 2 * 128, c % 2 * 128 + 128)
-        for r in range(4):
-            grad_qg = grad_qg + mm(ya[c, r], normed_all[c // 2, r, :, lane], NT)
-            grad_o = grad_o + mm(gated[c, r], slope_all[c // 2, r, lane, :])
-    for half in range(2):
-        lane = slice(half * 128, half * 128 + 128)
-        de[half, 0:64] = grad_qg[:, lane]
-        de[half, 64:96] = grad_o[:, lane]
-    first = Gather(p, fan, 18, de, sc["de_o"], sc["des"], oa)
-    last = Gather(p, fan, 14, dw, sc["dw_o"], sc["dws"], ob)
-    first.pair()
 
     def total(c, carry):
         for k in ORDER:
@@ -452,20 +436,36 @@
         pair[b].wait()
         mine[b] = (db[:, pl.ds(aligned(b * 2 + p.core, 512), 512)] + other[b]).astype(BF16)
 
+    def bias_of(h):
+        z, r = p.spot(h)
+        return mine.at[z, pl.ds(aligned(r, 64), 64)]
+
+    bias_back = fan.members(7, bias_of, lambda k: bo.at[p.h])
+    own_m = pltpu.make_async_copy(bias_of(p.h), bo.at[p.h], local.at[1])
+    own_m.start()
+
     def assemble(src, part):
         rows = slice(part * 32, part * 32 + 32)
         return jnp.concatenate([src[:, pp, rows, :].reshape(256, 128) for pp in range(2)], axis=1)
 
+    own_s.wait()
+    finish(moved_s)
+    grad_qg = jnp.zeros((64, 256), F32)
+    grad_o = jnp.zeros((32, 256), F32)
+    for c in range(CHUNKS):
+        lane = slice(c % 2 * 128, c % 2 * 128 + 128)
+        for r in range(4):
+            grad_qg = grad_qg + mm(ya[c, r], normed_all[c // 2, r, :, lane], NT)
+            grad_o = grad_o + mm(gated[c, r], slope_all[c // 2, r, lane, :])
+    for half in range(2):
+        lane = slice(half * 128, half * 128 + 128)
+        de[half, 0:64] = grad_qg[:, lane]
+        de[half, 64:96] = grad_o[:, lane]
+    first = Gather(p, fan, 18, de, sc["de_o"], sc["des"], oa)
+    last = Gather(p, fan, 14, dw, sc["dw_o"], sc["dws"], ob)
+    first.pair()
     first.block()
     lax.fori_loop(2, 3, total, 0)
-
-    def bias_of(h):
-        z, r = p.spot(h)
-        return mine.at[z, pl.ds(aligned(r, 64), 64)]
-
-    bias_back = fan.members(7, bias_of, lambda k: bo.at[p.h])
-    own_m = pltpu.make_async_copy(bias_of(p.h), bo.at[p.h], local.at[1])
-    own_m.start()
 
     lax.fori_loop(3, 4, total, 0)
     last.pair()
@@ -608,15 +608,15 @@
             c.start()
         spreaded = spread(ex[16:24, :])
         for i in range(16):
-            base[:, i * 128 : i * 128 + 128] = only(spreaded, 16, i).astype(BF16)
-
-    part = jnp.transpose(bo[:, pl.ds(pl.multiple_of(n * 16, 16), 16), :].reshape(128, 512))
-    for i in range(8):
-        out = mm(part, base[:, i * 256 : i * 256 + 256]).astype(BF16)
+            base[i // 8, :, i % 8 * 128 : i % 8 * 128 + 128] = only(spreaded, 16, i).astype(BF16)
+
+    part = jnp.transpose(bo[:, pl.ds(pl.multiple_of(n // 2 * 16, 16), 16), :].reshape(128, 512))
+    for i in range(4):
+        out = mm(part, base[n % 2, :, i * 256 : i * 256 + 256]).astype(BF16)
         pair[2 * i] = out[:, :128]
         pair[2 * i + 1] = out[:, 128:]
 
-    @pl.when(n == 3)
+    @pl.when(n == 7)
     def _():
         for c in copies:
             c.wait()
@@ -626,7 +626,7 @@
     square = jax.ShapeDtypeStruct((256, 256), F32)
     return pl.pallas_call(
         tail_kernel,
-        grid=(4,),
+        grid=(8,),
         out_shape=(
             jax.ShapeDtypeStruct((64, 512, 128), BF16),
             jax.ShapeDtypeStruct((256, 256), BF16),
@@ -635,8 +635,8 @@
             jax.ShapeDtypeStruct((8, 128), F32),
         ),
         in_specs=[VM] * 5,
-        out_specs=(pl.BlockSpec((16, 512, 128), lambda n: (n, 0, 0)),) + (HB,) * 8,
-        scratch_shapes=[pltpu.VMEM((128, 2048), BF16), pltpu.VMEM((5, 256, 256), F32), pltpu.SemaphoreType.DMA((8,))],
+        out_specs=(pl.BlockSpec((8, 512, 128), lambda n: (n, 0, 0)),) + (HB,) * 8,
+        scratch_shapes=[pltpu.VMEM((2, 128, 1024), BF16), pltpu.VMEM((5, 256, 256), F32), pltpu.SemaphoreType.DMA((8,))],
         compiler_params=pltpu.CompilerParams(vmem_limit_bytes=32 * 1024 * 1024),
         name="tail",
     )(bo, align, oa, ob, ex)

time: 96.2 us -> 96.1 us (level)
    pallas_call x1, Pallas kernels: 89.9 us -> 88 us  [main(): pl.pallas_call(main_kernel, out_shape=(jax.ShapeDtypeStruct((256, 256), B...]
    pallas_call x1, Pallas kernels: 5.38 us -> 6.72 us  [tail(): pl.pallas_call(tail_kernel, grid=(8,), out_shape=(jax.ShapeDtypeStruct((6...]
where the time goes in v9:
time: 96.1 us; the launch traced here: 95.6 us
  Pallas kernels  94.7 us (99%)
    pallas_call x1, Pallas kernels, main(): pl.pallas_call(main_kernel, out_shape=(jax.ShapeDtypeStruct((256, 256), B...  88 us
    pallas_call x1, Pallas kernels, tail(): pl.pallas_call(tail_kernel, grid=(8,), out_shape=(jax.ShapeDtypeStruct((6...  6.72 us

profile of v9, /device:TPU:0, one launch (start us, length us, event | category | flops | bytes accessed | tf_op | source)
XLA Modules:
  0.0 95.6 jit_solution(10655355754235202099)
XLA Ops:
  0.6 88.0 %main.1 = (bf16[256,256]{1,0:T(8,128)(2,1)S(1)}, bf16[8,64,512]{2,1,0:T(8,128)(2,1)S(1)}, f32[2,8,96,128]{3,2,1,0:T(8,128)S(1)}, f32[2,8,64,128]{3,2,1,0:T(8,128)S(1)}, f32[24,128]{1,0:T(8,128)S(1)}) custom-call(bf16[256,256]{1,0:T(8,128)(2,1)} %bitcast.7, bf16[256,256]{1,0:T(8,128)(2,1)} %bitcast.8, f32[1,256]{1,0:T(1,128)} %bitcast.10, ...), custom_call_target="tpu_custom_call" | custom-call | tf_op jit(solution)/shard_map/main/pallas_call | solution.py:577
  88.7 6.7 %tail.1 = (bf16[64,512,128]{2,1,0:T(8,128)(2,1)}, bf16[256,256]{1,0:T(8,128)(2,1)}, f32[256,256]{1,0:T(8,128)}, f32[256,256]{1,0:T(8,128)}, f32[256,256]{1,0:T(8...) custom-call(bf16[8,64,512]{2,1,0:T(8,128)(2,1)S(1)} %get-tuple-element.23.bo, ...), custom_call_target="tpu_custom_call" | custom-call | tf_op jit(solution)/shard_map/tail/pallas_call | solution.py:627

commit v10 on v9

--- a/solution.py
+++ b/solution.py
@@ -35,6 +35,9 @@
 
     def block(self, g):
         return (self.seq, g * 4 + ((self.h // 4 + g % 2) % 2) * 2 + self.z_hi)
+
+    def across(self, g):
+        return (self.z_lo * 2 + 1 - self.core, self.block(g)[1])
 
     def partner(self):
         return (self.z_lo * 2 + 1 - self.core, self.res)
@@ -201,6 +204,7 @@
     greet(
         [p.member((p.h + k) % 8) for k in range(1, 8)]
         + [p.block((p.g + k) % 8) for k in range(1, 8)]
+        + [p.across((p.g + k) % 8) for k in range(1, 8)]
         + [p.partner()]
     )
     loads = {}
@@ -231,7 +235,7 @@
     loads["wv"].wait()
     for n, w in enumerate((wk, wv)):
         t_ref[:, n * 32 : n * 32 + 32, :] = mm(w[...], normed, TN).astype(BF16).reshape(8, 32, 256)
-    pl.semaphore_wait(pltpu.get_barrier_semaphore(), 15)
+    pl.semaphore_wait(pltpu.get_barrier_semaphore(), 22)
     fan = Fan(p, sm["send"], sm["recv"])
 
     moved = fan.members(0, lambda h: t_ref.at[h, 0:64], lambda k: xr.at[z_lo, r4, 0:64])
@@ -292,27 +296,25 @@
     finish(moved)
     by_row(0)
 
-    def keys(c, k):
-        rows = pl.ds(c * per, per)
+    def keys(row, k):
         return remote(
-            xt.at[rows, 0:64], kv.at[rows, :, here], sm["ks"].at[c, k - 1], sm["kr"].at[c, k - 1],
+            xt.at[row, 0:64], kv.at[row, :, here], sm["ks"].at[row, k - 1], sm["kr"].at[row, k - 1],
             p.block((p.g + k) % 8),
         )
 
-    def partial(c, k):
-        rows = pl.ds(c * per, per)
+    def partial(row, k):
         g = (p.g + k) % 8
         return remote(
-            dkv.at[rows, :, pl.ds(aligned(g, 256), 256)],
-            parts.at[k - 1, rows],
-            sm["es"].at[c, k - 1],
-            sm["er"].at[c, k - 1],
+            dkv.at[row, :, pl.ds(aligned(g, 256), 256)],
+            parts.at[k - 1, row],
+            sm["es"].at[row, k - 1],
+            sm["er"].at[row, k - 1],
             p.block(g),
         )
 
-    for c in range(CHUNKS):
+    for row in range(8):
         for k in ORDER:
-            keys(c, k).start()
+            keys(row, k).start()
     own_k = pltpu.make_async_copy(xt.at[:, 0:64], kv.at[:, :, here], local.at[2])
     own_k.start()
     db[...] = jnp.zeros_like(db)
@@ -370,13 +372,14 @@
             give(stage, src, dst, k, 0).wait()
 
     def step(c, carry):
-        for k in ORDER:
-            keys(c, k).wait_recv()
         outs = []
         for i in range(per):
-            outs.append(row_backward(xt, kv, bias, db, dkv, c * per + i))
-        for k in ORDER:
-            partial(c, k).start()
+            row = c * per + i
+            for k in ORDER:
+                keys(row, k).wait_recv()
+            outs.append(row_backward(xt, kv, bias, db, dkv, row))
+            for k in ORDER:
+                partial(row, k).start()
         @pl.when(c == 0)
         def _():
             own_g.wait()
@@ -411,11 +414,11 @@
     dw[...] = jnp.zeros_like(dw)
 
     def total(c, carry):
-        for k in ORDER:
-            partial(c, k).wait_recv()
         outs = []
         for i in range(per):
             row = c * per + i
+            for k in ORDER:
+                partial(row, k).wait_recv()
             t = dkv[row, :, here].astype(F32)
             for k in range(7):
                 t = t + parts[k, row].astype(F32)
@@ -484,7 +487,7 @@
             grad_bias = grad_bias + mm(only(part, 16, i), rows_buf[n % 2, i])
         if n + 2 < 4:
             stream(n + 2).start()
-    ex, ex_own, exm, exb = sc["ex"], sc["ex_own"], sc["exm"], sc["exb"]
+    ex, exm, exb = sc["ex"], sc["exm"], sc["exb"]
     ex[0:8, :] = jnp.sum(grad_bias.reshape(8, 16, 128), axis=1)
     first.member()
     last.member()
@@ -496,9 +499,7 @@
     hat = sc["hat"][...]
     by_gain = jnp.sum(jnp.transpose(grad_normed * hat), axis=0, keepdims=True)
     ex[8:16, :] = jnp.concatenate([by_gain[:, :128], by_gain[:, 128:], jnp.zeros((6, 128), F32)], axis=0)
-    extra = fan.partner(9, ex, ex_own)
-    finish(extra)
-    exm[p.h] = ex[...] + ex_own[...]
+    exm[p.h] = ex[...]
     extra = fan.members(22, lambda h: exm.at[p.h], lambda k: exm.at[p.h])
 
     scaled = grad_normed * sc["scale"][...]
@@ -507,8 +508,11 @@
     align[...] = jnp.transpose(sc["inv"][0:1, :] * (scaled - m1 - hat * m2)).astype(BF16)
 
     finish(extra)
-    exb[p.g] = sum_of(exm)
-    extra = fan.blocks(23, lambda g: exb.at[p.g], lambda k: exb.at[p.g])
+    exb[p.core * 8 + p.g] = sum_of(exm)
+    piece = exb.at[p.core * 8 + p.g]
+    extra = fan.partner(9, piece, piece)
+    extra += fan.blocks(23, lambda g: piece, lambda k: piece)
+    extra += fan.all(24, lambda g: piece, lambda k: piece, p.g, p.across)
     first.back_pair()
     last.back_pair()
     finish(extra)
@@ -523,12 +527,12 @@
             partial(c, k).wait_send()
         return carry
 
-    lax.fori_loop(0, CHUNKS, drain, 0)
+    lax.fori_loop(0, 8, drain, 0)
 
 
 def sum_of(ref):
     total = ref[0]
-    for n in range(1, 8):
+    for n in range(1, ref.shape[0]):
         total = total + ref[n]
     return total
 
@@ -565,14 +569,14 @@
         "xn": vmem((2, 4, 256, 256), BF16), "xs": vmem((2, 4, 256, 256), BF16), "xg": vmem((2, 4, 64, 256), F32),
         "de": vmem((2, 96, 128), F32), "de_o": vmem((96, 128), F32), "des": vmem((8, 96, 128), F32),
         "dw": vmem((2, 64, 128), F32), "dw_o": vmem((64, 128), F32), "dws": vmem((8, 64, 128), F32),
-        "ex": vmem((16, 128), F32), "ex_own": vmem((16, 128), F32),
-        "exm": vmem((8, 16, 128), F32), "exb": vmem((8, 16, 128), F32),
+        "ex": vmem((16, 128), F32),
+        "exm": vmem((8, 16, 128), F32), "exb": vmem((16, 16, 128), F32),
     }
     sems = {
         "hbm": dma((2,)), "local": dma((6,)), "in": dma((9,)),
-        "send": dma((24, 7)), "recv": dma((24, 7)),
-        "ks": dma((CHUNKS, 7)), "kr": dma((CHUNKS, 7)),
-        "es": dma((CHUNKS, 7)), "er": dma((CHUNKS, 7)),
+        "send": dma((25, 7)), "recv": dma((25, 7)),
+        "ks": dma((8, 7)), "kr": dma((8, 7)),
+        "es": dma((8, 7)), "er": dma((8, 7)),
     }
     return pl.pallas_call(
         main_kernel,

time: 96.1 us -> 98.5 us (1.025)
  Pallas kernels: 94.7 us -> 96.6 us
    pallas_call x1, Pallas kernels: 88 us -> 89.8 us  [main(): pl.pallas_call(main_kernel, out_shape=(jax.ShapeDtypeStruct((256, 256), B...]
where the time goes in v10:
time: 98.5 us; the launch traced here: 97.4 us
  Pallas kernels  96.6 us (98%)
    pallas_call x1, Pallas kernels, main(): pl.pallas_call(main_kernel, out_shape=(jax.ShapeDtypeStruct((256, 256), B...  89.8 us
    pallas_call x1, Pallas kernels, tail(): pl.pallas_call(tail_kernel, grid=(8,), out_shape=(jax.ShapeDtypeStruct((6...  6.73 us

profile of v10, /device:TPU:0, one launch (start us, length us, event | category | flops | bytes accessed | tf_op | source)
XLA Modules:
  0.0 97.4 jit_solution(570073335401514612)
XLA Ops:
  0.6 89.8 %main.1 = (bf16[256,256]{1,0:T(8,128)(2,1)S(1)}, bf16[8,64,512]{2,1,0:T(8,128)(2,1)S(1)}, f32[2,8,96,128]{3,2,1,0:T(8,128)S(1)}, f32[2,8,64,128]{3,2,1,0:T(8,128)S(1)}, f32[24,128]{1,0:T(8,128)S(1)}) custom-call(bf16[256,256]{1,0:T(8,128)(2,1)} %bitcast.7, bf16[256,256]{1,0:T(8,128)(2,1)} %bitcast.8, f32[1,256]{1,0:T(1,128)} %bitcast.10, ...), custom_call_target="tpu_custom_call" | custom-call | tf_op jit(solution)/shard_map/main/pallas_call | solution.py:581
  90.5 6.7 %tail.1 = (bf16[64,512,128]{2,1,0:T(8,128)(2,1)}, bf16[256,256]{1,0:T(8,128)(2,1)}, f32[256,256]{1,0:T(8,128)}, f32[256,256]{1,0:T(8,128)}, f32[256,256]{1,0:T(8...) custom-call(bf16[8,64,512]{2,1,0:T(8,128)(2,1)S(1)} %get-tuple-element.23.bo, ...), custom_call_target="tpu_custom_call" | custom-call | tf_op jit(solution)/shard_map/tail/pallas_call | solution.py:631
